TPU v7x, 256 devices: a whole 4x4x8 slice. The times are simulated.
256 devices in a mesh: gx: 4 (over y), gy: 8 (over x, core), gz: 8 (over z).
Axes of the slice: x: 4, y: 4, z: 8, core: 2. Of those that a mesh axis runs over, the one named last changes fastest.
Arguments:
- earlier_edge_voltage: float32 [6, 32, 128, 2048], P(None, 'gx', 'gy', 'gz'), may hold values from -6 to 6
- coil_drive_current: float32 [6, 32, 128, 2048], P(None, 'gx', 'gy', 'gz'), may hold values from -18 to 18
- sigma_omega_cellwise: float32 [32, 128, 2048], P('gx', 'gy', 'gz'), may hold values from 0.2 to 3
- subdomain_inverse_full: bfloat16 [4, 8, 8, 16, 512, 512], P('gx', 'gy', 'gz'), may hold values from -0.25 to 0.25
- subdomain_inverse_main: float32 [4, 8, 8, 16, 512], P('gx', 'gy', 'gz'), may hold values from 0.25 to 1.75
- subdomain_layer_counts: int32 [4, 8, 8, 16], P('gx', 'gy', 'gz'), may hold values from 1 to 19, 256 in all within a row
- heat_layer_lookup: int32 [8, 32], P('gz'), may hold values from 1 to 24, 256 in all within a row
- warming_amount: float32 [4, 8, 8, 24, 32, 128], P('gx', 'gy', 'gz'), may hold values from 0 to 2
- heat_spreading_coef: float32 [4, 8, 8, 24, 32, 128], P('gx', 'gy', 'gz'), may hold values from 0.25 to 1
Outputs:
- field_new: float32 [6, 32, 128, 2048], P(None, 'gx', 'gy', 'gz')
- renewed_heat_rise: float32 [4, 8, 8, 24, 32, 128], P('gx', 'gy', 'gz')
- renewed_sigma_omega: float32 [32, 128, 2048], P('gx', 'gy', 'gz')
Inputs may be any that keep to these rules, and one draw needn't show every extreme that they name: `subdomain_layer_counts`: each device's 16 segment lengths sum to 256, and every device has a segment of exactly 19 planes. `heat_layer_lookup`: each row sums to 256, and every row has a slab of exactly 24 planes.
All inputs are finite; a program needn't handle non-finite values.
Results may differ from a plain program's by a relative error of at most 0.013.
Values sent between devices are 32-bit elements; how exact they have to be, the bound alone decides.
No kernel may reach another device: no remote copies, remote signals or barrier semaphores. Data moves between devices by JAX's collectives and lax.ppermute only.
A program may use at most 128 MiB of HBM per device.

v0:
```python
import functools

import jax
import jax.numpy as jnp
from jax import lax
from jax.experimental import pallas as pl
from jax.experimental.pallas import tpu as pltpu
from jax.sharding import PartitionSpec as P

SWEEPS = 2
SECTIONS = 4

mass_shift = 1.0
solver_scale = 0.2
coupling_scale = 0.05
time_step = 2.5
heat_drop = 0.15

CX, CY, CZ = 8, 16, 256
LANES = CX * CY
PLANE = 24
WINDOW = 21
MAXSEG = 19
COLS = LANES // 4
F32 = jnp.float32
HALO = 8
CHUNK = 32
XP_PLUS, XP_MINUS = 6, 7
RING = SECTIONS
VMEM = pl.BlockSpec(memory_space=pltpu.VMEM)
SMEM = pl.BlockSpec(memory_space=pltpu.SMEM)
ANY = pl.BlockSpec(memory_space=pl.ANY)


def params(mib=40):
    return pltpu.CompilerParams(vmem_limit_bytes=mib << 20)


def cost(flops, moved):
    return pl.CostEstimate(flops=flops, bytes_accessed=moved, transcendentals=0)


def lane_of(value):
    return lax.broadcasted_iota(jnp.int32, value.shape, value.ndim - 1)


def ahead(value, by):
    shift = (-by) % LANES
    return value if shift == 0 else pltpu.roll(value, shift, value.ndim - 1)


def x_slot(slot):
    return (slot // 4) * 64 + (slot % 4) * 8


def y_slot(slot):
    return (slot // 8) * 32 + slot % 8


def x_next(value, halo, slot):
    lane = lane_of(value)
    inner = jnp.where(lane < 64, ahead(value, 64), ahead(value, -56))
    return jnp.where((lane // 8) % 4 + 4 * (lane // 64) == 7, ahead(halo, x_slot(slot) - 88), inner)


def x_before(value, halo, slot):
    lane = lane_of(value)
    inner = jnp.where(lane < 64, ahead(value, 56), ahead(value, -64))
    return jnp.where((lane // 8) % 4 + 4 * (lane // 64) == 0, ahead(halo, x_slot(slot)), inner)


def y_next(value, halo, slot):
    lane = lane_of(value)
    low = (lane // 32) % 2 == 0
    inner = jnp.where(low, ahead(value, 32), ahead(value, -31))
    return jnp.where(lane % 8 + 8 * ((lane // 32) % 2) == 15, ahead(halo, y_slot(slot) - 39), inner)


def y_before(value, halo, slot):
    lane = lane_of(value)
    low = (lane // 32) % 2 == 0
    inner = jnp.where(low, ahead(value, 31), ahead(value, -32))
    return jnp.where(lane % 8 + 8 * ((lane // 32) % 2) == 0, ahead(halo, y_slot(slot)), inner)


def x_faces(parts):
    lane = lane_of(parts[0])
    own = (lane // 8) % 4 + 4 * (lane // 64)
    first = jnp.zeros_like(parts[0])
    last = first
    for slot, part in enumerate(parts):
        first = jnp.where(own == slot, ahead(part, -x_slot(slot)), first)
        last = jnp.where(own == slot, ahead(part, 88 - x_slot(slot)), last)
    return first, last


def y_faces(parts):
    lane = lane_of(parts[0])
    own = lane % 8 + 8 * ((lane // 32) % 2)
    first = jnp.zeros_like(parts[0])
    last = first
    for slot, part in enumerate(parts):
        first = jnp.where(own == slot, ahead(part, -y_slot(slot)), first)
        last = jnp.where(own == slot, ahead(part, 39 - y_slot(slot)), last)
    return first, last


def cell_rows(part):
    for dx in range(2):
        for dy in range(2):
            for a in range(CX // 2):
                yield (2 * dx + dy) * 32 + a * 8, 32 * a + 16 * dx + dy


def to_planes(source, index, target, out_index, turned):
    for to_row, from_row in cell_rows(None):
        for half in range(CZ // LANES):
            turned[half, to_row : to_row + 8, :] = source[index, half, pl.ds(from_row, 8, stride=2), :]
    for half in range(CZ // LANES):
        target[out_index, half * LANES : (half + 1) * LANES, :] = turned[half].T


def load_halves(source, loaded, index):
    for half in range(CZ // LANES):
        loaded[index, half] = source[index, :, half * LANES : (half + 1) * LANES]


def prepare_field(field, planes, first, last, loaded, turned):
    for comp in range(6):
        load_halves(field, loaded, comp)
        to_planes(loaded, comp, planes, comp, turned.at[comp % 2])

    def chunk(i, carry):
        rows = pl.ds(pl.multiple_of(i * CHUNK, CHUNK), CHUNK)
        low, high = x_faces([planes[comp, rows, :] for comp in range(6)])
        first[rows, :] = low
        last[rows, :] = high
        return carry

    lax.fori_loop(0, CZ // CHUNK, chunk, 0)


def prepare_drive(drive, conduct, diagonal, drive_planes, conduct_planes, diagonal_turned, loaded, turned):
    for comp in range(6):
        load_halves(drive, loaded, comp)
        to_planes(loaded, comp, drive_planes, comp, turned.at[comp % 2])
    load_halves(conduct, loaded, 0)
    to_planes(loaded, 0, conduct_planes, 0, turned.at[0])
    diagonal_turned[...] = diagonal[...].T


def kept(flag, value):
    return jnp.where(flag > 0, value, jnp.zeros_like(value))


def pack_y(flags, field, x_plus, x_minus, first, last):
    def chunk(i, carry):
        rows = pl.ds(pl.multiple_of(i * CHUNK, CHUNK), CHUNK)
        parts = [field[comp, rows, :] for comp in range(6)]
        parts += [kept(flags[1], x_plus[rows, :]), kept(flags[0], x_minus[rows, :])]
        low, high = y_faces(parts)
        first[rows, :] = low
        last[rows, :] = high
        return carry

    lax.fori_loop(0, CZ // CHUNK, chunk, 0)


def pack_z(flags, *refs):
    lows, highs, (first, last) = refs[:5], refs[5:10], refs[10:]
    for (field, xp, xm, yp, ym), row, out in ((lows, 0, first), (highs, 7, last)):
        for comp in range(6):
            out[comp : comp + 1, :] = field[comp, row : row + 1, :]
        out[6:7, :] = kept(flags[1], xp[row : row + 1, :])
        out[7:8, :] = kept(flags[0], xm[row : row + 1, :])
        out[8:9, :] = kept(flags[3], yp[row : row + 1, :])
        out[9:10, :] = kept(flags[2], ym[row : row + 1, :])
        out[10:16, :] = jnp.zeros((6, LANES), F32)


def curl_chunk(wide, part):
    ex, ey, ez = wide[3 * part], wide[3 * part + 1], wide[3 * part + 2]
    xp, xm, yp, ym = wide[6], wide[7], wide[8], wide[9]
    sx, sy, sz = 3 * part, 3 * part + 1, 3 * part + 2

    def here(v):
        return v[8 : 8 + CHUNK]

    def up(v):
        return v[9 : 9 + CHUNK]

    def down(v):
        return v[7 : 7 + CHUNK]

    upper = [v[8:] for v in (ex, ey, xm, ym)]
    ex_xm = x_before(upper[0], upper[2], sx)
    ey_ym = y_before(upper[1], upper[3], sy)
    ex_xm_up, ex_xm = ex_xm[1 : 1 + CHUNK], ex_xm[:CHUNK]
    ey_ym_up, ey_ym = ey_ym[1 : 1 + CHUNK], ey_ym[:CHUNK]
    lower = [v[: 8 + CHUNK] for v in (ez, xp, yp)]
    ez_xp = x_next(lower[0], lower[1], sz)
    ez_yp = y_next(lower[0], lower[2], sz)
    ez_xp_down, ez_xp = down(ez_xp), ez_xp[8:]
    ez_yp_down, ez_yp = down(ez_yp), ez_yp[8:]
    xp0, xm0, yp0, ym0 = here(xp), here(xm), here(yp), here(ym)
    ex0, ey0, ez0 = here(ex), here(ey), here(ez)
    ex_yp = y_next(ex0, yp0, sx)
    ex_ym = y_before(ex0, ym0, sx)
    ex_xm_yp = x_before(ex_yp, y_next(xm0, yp0, XP_MINUS), sx)
    ey_xp = x_next(ey0, xp0, sy)
    ey_xm = x_before(ey0, xm0, sy)
    ey_xp_ym = x_next(ey_ym, y_before(xp0, ym0, XP_PLUS), sy)
    ez_xm = x_before(ez0, xm0, sz)
    ez_ym = y_before(ez0, ym0, sz)
    kx = 4.0 * ex0 - ex_yp - ex_ym - up(ex) - down(ex)
    kx = kx + (ey_xp - ey0 - ey_xp_ym + ey_ym) + (ez_xp - ez0 - ez_xp_down + down(ez))
    ky = 4.0 * ey0 - ey_xp - ey_xm - up(ey) - down(ey)
    ky = ky + (ex_yp - ex0 - ex_xm_yp + ex_xm) + (ez_yp - ez0 - ez_yp_down + down(ez))
    kz = 4.0 * ez0 - ez_xp - ez_xm - ez_yp - ez_ym
    kz = kz + (up(ex) - ex0 - ex_xm_up + ex_xm) + (up(ey) - ey0 - ey_ym_up + ey_ym)
    return (kx, ky, kz), (ex0, ey0, ez0)


def sweep(last_sweep, flags, seg_len, field, drive, conduct, xp, xm, yp, ym, zp, zm, diagonal, solver, *rest):
    if last_sweep:
        permute, field_out, heat_out, ext, columns, solved, matrices, sems, turned = rest
    else:
        field_out, first, last, ext, columns, solved, matrices, sems = rest
    segs = matrices.shape[0]
    copies = [pltpu.make_async_copy(solver.at[s], matrices.at[s], sems.at[s]) for s in range(segs)]
    for copy in copies:
        copy.start()

    def fill(i, carry):
        rows = pl.ds(pl.multiple_of(i * CHUNK, CHUNK), CHUNK)
        to = pl.ds(pl.multiple_of(i * CHUNK + HALO, 8), CHUNK)
        for comp in range(6):
            ext[comp, to, :] = field[comp, rows, :]
        ext[6, to, :] = kept(flags[1], xp[rows, :])
        ext[7, to, :] = kept(flags[0], xm[rows, :])
        ext[8, to, :] = kept(flags[3], yp[rows, :])
        ext[9, to, :] = kept(flags[2], ym[rows, :])
        return carry

    lax.fori_loop(0, CZ // CHUNK, fill, 0)
    for comp in range(10):
        ext[comp, HALO - 1 : HALO, :] = kept(flags[4], zm[comp : comp + 1, :])
        ext[comp, HALO + CZ : HALO + CZ + 1, :] = kept(flags[5], zp[comp : comp + 1, :])

    columns[0:PLANE, :] = jnp.zeros((PLANE, LANES), F32)
    tail = columns.shape[0] - (CZ + 1) * PLANE
    columns[(CZ + 1) * PLANE :, :] = jnp.zeros((tail, LANES), F32)

    def residual(i, carry):
        base = pl.multiple_of(i * CHUNK, CHUNK)
        rows = pl.ds(base, CHUNK)
        wide = [ext[comp, pl.ds(base, CHUNK + 2 * HALO), :] for comp in range(10)]
        curl_real, real = curl_chunk(wide, 0)
        curl_imag, imag = curl_chunk(wide, 1)
        sigma = conduct[0, rows, :]
        for axis in range(3):
            both = (
                curl_real[axis] + mass_shift * real[axis] - sigma * imag[axis],
                curl_imag[axis] + mass_shift * imag[axis] + sigma * real[axis],
            )
            for part in range(2):
                comp = 3 * part + axis
                rest_of = drive[comp, rows, :] - both[part]
                for q in range(4):
                    at = (base + 1) * PLANE + comp * 4 + q
                    columns[pl.ds(at, CHUNK, stride=PLANE), :] = ahead(rest_of, 32 * q)
        return carry

    lax.fori_loop(0, CZ // CHUNK, residual, 0)

    row_of = lax.broadcasted_iota(jnp.int32, (512, LANES), 0)
    start = jnp.int32(0)
    for s in range(segs):
        length = seg_len[s]
        window = columns[pl.ds(pl.multiple_of(start * PLANE, 8), 512), :]
        window = jnp.where(row_of < (length + 2) * PLANE, window, 0.0).astype(jnp.bfloat16)
        copies[s].wait()
        product = jnp.dot(matrices[s], window, preferred_element_type=F32)
        scaled = solver_scale * diagonal[:, s : s + 1] * window.astype(F32)
        result = coupling_scale * product + scaled
        to = pl.ds(pl.multiple_of(start * PLANE, 8), MAXSEG * PLANE)
        solved[to, :] = result[PLANE : (MAXSEG + 1) * PLANE, :]
        start = start + length

    def update(i, carry):
        base = pl.multiple_of(i * CHUNK, CHUNK)
        rows = pl.ds(base, CHUNK)
        lane = lax.broadcasted_iota(jnp.int32, (CHUNK, LANES), 1)
        parts = []
        for comp in range(6):
            add = jnp.zeros((CHUNK, LANES), F32)
            for q in range(4):
                piece = solved[pl.ds(base * PLANE + comp * 4 + q, CHUNK, stride=PLANE), :]
                add = jnp.where(lane // COLS == q, ahead(piece, -32 * q), add)
            parts.append(field[comp, rows, :] + add)
        if last_sweep:
            total = parts[0] * parts[0]
            for part in parts[1:]:
                total = total + part * part
            heat = 0.5 * conduct[0, rows, :] * total
            heat_out[rows, :] = jnp.dot(
                heat, permute[...], precision=lax.Precision.HIGHEST, preferred_element_type=F32
            )
            for comp in range(6):
                ext[comp, rows, :] = parts[comp]
        else:
            for comp in range(6):
                field_out[comp, rows, :] = parts[comp]
            low, high = x_faces(parts)
            first[rows, :] = low
            last[rows, :] = high
        return carry

    lax.fori_loop(0, CZ // CHUNK, update, 0)
    if last_sweep:
        for comp in range(6):
            for half in range(CZ // LANES):
                flat = ext[comp, half * LANES : (half + 1) * LANES, :].T
                for from_row, to_row in cell_rows(None):
                    turned[comp % 2, half, pl.ds(to_row, 8, stride=2), :] = flat[from_row : from_row + 8]
                field_out[comp, :, half * LANES : (half + 1) * LANES] = turned[comp % 2, half]


def pack_heat(flags, starts, heat, below, above, out, ext):
    ext[0:8, :] = kept(flags[4], below[...])
    ext[8 : 8 + CZ, :] = heat[...]
    ext[8 + CZ : 16 + CZ, :] = kept(flags[5], above[...])
    ext[16 + CZ :, :] = jnp.zeros((ext.shape[0] - 16 - CZ, LANES), F32)
    for owner in range(out.shape[0]):
        out[owner] = ext[pl.ds(starts[owner] + 8 - (RING - 1), out.shape[1]), :]


def swap_tiles(value):
    row = lax.broadcasted_iota(jnp.int32, value.shape, value.ndim - 2)
    lane = lane_of(value)
    axis = value.ndim - 2
    for k in range(3):
        step = 1 << k
        row_bit = (row // step) % 2
        lane_bit = (lane // (16 * step)) % 2
        up = ahead(pltpu.roll(value, 8 - step, axis), -16 * step)
        down = up if step == 4 else ahead(pltpu.roll(value, step, axis), 16 * step)
        value = jnp.where(row_bit == lane_bit, value, jnp.where(row_bit == 0, up, down))
    return value


def prepare_slab(warm, rates, out):
    for plane in range(out.shape[0]):
        for which, source in enumerate((warm, rates)):
            out[plane, which] = swap_tiles(source[plane].reshape(4, 8, LANES))


def choose_planes(length, round_id, slab, *refs):
    received = refs[: 2 * (round_id - 1)]
    up_out, down_out = refs[2 * (round_id - 1) :]
    below, above = received[0::2], received[1::2]
    count = length[0]
    up_out[...] = slab[jnp.maximum(count - round_id, 0)]
    down_out[...] = slab[round_id - 1]
    for short in range(1, round_id):

        @pl.when(count == short)
        def _():
            up_out[...] = below[round_id - short - 1][...]
            down_out[...] = above[round_id - short - 1][...]


def heat_step(slab_info, slab, b1, a1, b2, a2, b3, a3, b4, a4, arrived, factor_out, warm_out, temp, rates, joule):
    count, low_open, high_open = slab_info[0], slab_info[1], slab_info[2]
    planes = temp.shape[1]
    owners = arrived.shape[0]
    for plane in range(planes - 2 * RING):
        temp[0, plane + RING] = slab[plane, 0]
        rates[plane + RING] = slab[plane, 1]
    for r, (below, above) in enumerate(((b1, a1), (b2, a2), (b3, a3), (b4, a4))):
        temp[0, RING - 1 - r] = below[0]
        rates[RING - 1 - r] = below[1]
        temp[0, RING + count + r] = above[0]
        rates[RING + count + r] = above[1]
    for owner in range(owners):
        joule[pl.ds(owners + owner, arrived.shape[1], stride=owners), :] = arrived[owner]

    group = 6
    section = time_step / (SECTIONS * SECTIONS)

    def one(step, now, before, base):
        value = temp[now, pl.ds(base - 1, group + 2)]
        mid = value[1:-1]
        lane = lane_of(mid)
        row = lax.broadcasted_iota(jnp.int32, mid.shape, 2)
        none = jnp.zeros_like(mid[:, :1])
        gx_up = jnp.concatenate([mid[:, 1:], none], axis=1)
        gx_down = jnp.concatenate([none, mid[:, :-1]], axis=1)
        gy_up = jnp.where(row == 7, 0.0, pltpu.roll(mid, 7, 2))
        gy_down = jnp.where(row == 0, 0.0, pltpu.roll(mid, 1, 2))
        total = ahead(jnp.where(lane < 16, gx_up, mid), 16)
        total = total + ahead(jnp.where(lane >= 112, gx_down, mid), -16)
        total = total + jnp.where(lane % 16 == 15, ahead(gy_up, -15), ahead(mid, 1))
        total = total + jnp.where(lane % 16 == 0, ahead(gy_down, 15), ahead(mid, -1))
        total = total + value[:-2] + value[2:]
        heat = joule[pl.ds(base * owners, group * owners), :].reshape(group, 4, 8, LANES)
        rate = rates[pl.ds(base, group)] * (total - 6.0 * mid) + heat
        if step == 1:
            temp[before, pl.ds(base, group)] = mid + section * rate
        else:
            old = temp[before, pl.ds(base, group)]
            temp[before, pl.ds(base, group)] = 2.0 * mid - old + 2.0 * section * rate

    for step in range(1, SECTIONS + 1):
        now, before = (step - 1) % 2, step % 2

        def loop(g, carry):
            one(step, now, before, 1 + g * group)
            return carry

        lax.fori_loop(0, (planes - 2) // group, loop, 0)
    final = SECTIONS % 2
    for plane in range(warm_out.shape[0]):
        result = temp[final, plane + RING]
        warm_out[plane] = result
        joule[plane * owners : (plane + 1) * owners, :] = jnp.exp(-heat_drop * result).reshape(owners, LANES)
    for owner in range(owners):
        factor_out[owner] = joule[pl.ds(owner, factor_out.shape[1], stride=owners), :]


def finish_slab(slab_info, warm, out):
    count = slab_info[0]
    for plane in range(out.shape[0]):
        out[plane] = kept(count - plane, swap_tiles(warm[plane])).reshape(32, LANES)


def finish_conduct(starts, returned, conduct, out, rows):
    for owner in range(returned.shape[0]):
        rows[pl.ds(starts[owner], returned.shape[1]), :] = returned[owner]
    for half in range(CZ // LANES):
        lanes = slice(half * LANES, (half + 1) * LANES)
        out[:, lanes] = conduct[:, lanes] * rows[half * LANES : (half + 1) * LANES, :].T


def shape(*dims):
    return jax.ShapeDtypeStruct(dims, F32)


def body(
    earlier_edge_voltage,
    coil_drive_current,
    sigma_omega_cellwise,
    subdomain_inverse_full,
    subdomain_inverse_main,
    subdomain_layer_counts,
    heat_layer_lookup,
    warming_amount,
    heat_spreading_coef,
):
    count_x, count_y, count_z = (lax.axis_size(axis) for axis in ("gx", "gy", "gz"))
    at_x, at_y, at_z = (lax.axis_index(axis) for axis in ("gx", "gy", "gz"))
    owners = count_x * count_y
    segs = subdomain_layer_counts.shape[3]
    slab_cap = warming_amount.shape[3]

    def turn(value, axis, step):
        count = lax.axis_size(axis)
        return lax.ppermute(value, axis, [(i, (i + step) % count) for i in range(count)])

    def device(slab):
        return (slab % owners) * count_z + slab // owners

    def ring(value, step):
        total = owners * count_z
        pairs = [(device(i), device((i + step) % total)) for i in range(total)]
        return lax.ppermute(value, ("gx", "gy", "gz"), pairs)

    flags = jnp.stack(
        [at_x > 0, at_x < count_x - 1, at_y > 0, at_y < count_y - 1, at_z > 0, at_z < count_z - 1]
    ).astype(jnp.int32)
    seg_len = subdomain_layer_counts[0, 0, 0]
    slab_lengths = heat_layer_lookup[0]
    slab_ids = jnp.arange(owners, dtype=jnp.int32)
    starts = jnp.sum(
        jnp.where(slab_ids[None, :] < slab_ids[:, None], slab_lengths[None, :], 0), axis=1
    ).astype(jnp.int32)
    my_owner = at_x * count_y + at_y
    my_length = jnp.sum(jnp.where(slab_ids == my_owner, slab_lengths, 0)).astype(jnp.int32)
    low_open = (my_owner > 0) | (at_z > 0)
    high_open = (my_owner < owners - 1) | (at_z < count_z - 1)
    slab_info = jnp.stack([my_length, low_open.astype(jnp.int32), high_open.astype(jnp.int32)])

    field_bytes = 6 * CZ * LANES * 4
    plane_array = shape(CZ, LANES)
    halves = pltpu.VMEM((6, 2, LANES, LANES), F32)
    turned = pltpu.VMEM((2, 2, LANES, LANES), F32)
    field, face_low, face_high = pl.pallas_call(
        prepare_field,
        out_shape=(shape(6, CZ, LANES), plane_array, plane_array),
        in_specs=[VMEM],
        out_specs=[VMEM] * 3,
        scratch_shapes=[halves, turned],
        compiler_params=params(),
        cost_estimate=cost(1 << 20, 2 * field_bytes),
        name="prepare_field",
    )(earlier_edge_voltage.reshape(6, LANES, CZ))
    drive, conduct, diagonal = pl.pallas_call(
        prepare_drive,
        out_shape=(shape(6, CZ, LANES), shape(1, CZ, LANES), shape(512, segs)),
        in_specs=[VMEM] * 3,
        out_specs=[VMEM] * 3,
        scratch_shapes=[halves, turned],
        compiler_params=params(),
        cost_estimate=cost(1 << 20, 2 * field_bytes),
        name="prepare_drive",
    )(
        coil_drive_current.reshape(6, LANES, CZ),
        sigma_omega_cellwise.reshape(1, LANES, CZ),
        subdomain_inverse_main[0, 0, 0],
    )
    slab = pl.pallas_call(
        prepare_slab,
        out_shape=shape(slab_cap, 2, 4, 8, LANES),
        in_specs=[VMEM] * 2,
        out_specs=VMEM,
        compiler_params=params(),
        cost_estimate=cost(1 << 20, 2 * field_bytes),
        name="prepare_slab",
    )(warming_amount[0, 0, 0], heat_spreading_coef[0, 0, 0])

    def halo(field, face_low, face_high):
        x_plus, x_minus = turn(face_low, "gx", -1), turn(face_high, "gx", 1)
        y_low, y_high = pl.pallas_call(
            pack_y,
            out_shape=(plane_array, plane_array),
            in_specs=[SMEM] + [VMEM] * 3,
            out_specs=[VMEM] * 2,
            compiler_params=params(),
            cost_estimate=cost(1 << 20, 2 * field_bytes),
            name="pack_y",
        )(flags, field, x_plus, x_minus)
        y_plus, y_minus = turn(y_low, "gy", -1), turn(y_high, "gy", 1)
        sides = (x_plus, x_minus, y_plus, y_minus)
        end = CZ // 8 - 1
        specs = []
        for block in (0, end):
            specs.append(pl.BlockSpec((6, 8, LANES), lambda i, block=block: (0, block, 0)))
            specs += [pl.BlockSpec((8, LANES), lambda i, block=block: (block, 0))] * 4
        z_low, z_high = pl.pallas_call(
            pack_z,
            grid=(1,),
            out_shape=(shape(16, LANES), shape(16, LANES)),
            in_specs=[SMEM] + specs,
            out_specs=[pl.BlockSpec((16, LANES), lambda i: (0, 0))] * 2,
            compiler_params=params(),
            name="pack_z",
        )(flags, field, *sides, field, *sides)
        z_plus, z_minus = turn(z_low, "gz", -1), turn(z_high, "gz", 1)
        return sides + (z_plus, z_minus)

    received = []
    for round_id in range(1, RING + 1):
        up, down = pl.pallas_call(
            lambda length, *refs, round_id=round_id: choose_planes(length, round_id, *refs),
            out_shape=(shape(2, 4, 8, LANES),) * 2,
            in_specs=[SMEM] + [VMEM] * (1 + len(received)),
            out_specs=[VMEM] * 2,
            compiler_params=params(),
            name="choose_planes",
        )(slab_info, slab, *received)
        below, above = ring(up, 1), ring(down, -1)
        received += [jnp.where(low_open, below, 0.0), jnp.where(high_open, above, 0.0)]

    solver = subdomain_inverse_full[0, 0, 0]
    for sweep_index in range(SWEEPS):
        final = sweep_index == SWEEPS - 1
        ghosts = halo(field, face_low, face_high)
        scratch = [
            pltpu.VMEM((10, CZ + 2 * HALO, LANES), F32),
            pltpu.VMEM(((CZ + 1 + WINDOW) * PLANE + 8, LANES), F32),
            pltpu.VMEM(((CZ + MAXSEG) * PLANE, LANES), F32),
            pltpu.VMEM((segs, 512, 512), jnp.bfloat16),
            pltpu.SemaphoreType.DMA((segs,)),
        ]
        inputs = [flags, seg_len, field, drive, conduct, *ghosts, diagonal, solver]
        specs = [SMEM] * 2 + [VMEM] * 10 + [ANY]
        if final:
            lane = jnp.arange(LANES, dtype=jnp.int32)
            natural = (
                (2 * ((lane // 8) % 4) + lane // 64) * 16 + 2 * (lane % 8) + (lane // 32) % 2
            )
            inputs.append((natural[:, None] == lane[None, :]).astype(F32))
            specs.append(VMEM)
            scratch.append(turned)
            outs = (shape(6, LANES, CZ), plane_array)
        else:
            outs = (shape(6, CZ, LANES), plane_array, plane_array)
        result = pl.pallas_call(
            functools.partial(sweep, final),
            out_shape=outs,
            in_specs=specs,
            out_specs=[VMEM] * len(outs),
            scratch_shapes=scratch,
            compiler_params=params(),
            cost_estimate=cost(1 << 28, 4 * field_bytes),
            name="sweep",
        )(*inputs)
        if final:
            field_new, heat = result
        else:
            field, face_low, face_high = result

    heat_above, heat_below = turn(heat[:8], "gz", -1), turn(heat[CZ - 8 :], "gz", 1)
    rows = slab_cap + 8
    outgoing = pl.pallas_call(
        pack_heat,
        out_shape=shape(owners, rows, LANES),
        in_specs=[SMEM] * 2 + [VMEM] * 3,
        out_specs=VMEM,
        scratch_shapes=[pltpu.VMEM((CZ + 16 + rows, LANES), F32)],
        compiler_params=params(),
        name="pack_heat",
    )(flags, starts, heat, heat_below, heat_above)
    arrived = lax.all_to_all(outgoing, ("gx", "gy"), split_axis=0, concat_axis=0, tiled=True)
    planes = slab_cap + 2 * RING
    factor, warm = pl.pallas_call(
        heat_step,
        out_shape=(shape(owners, slab_cap, LANES), shape(slab_cap, 4, 8, LANES)),
        in_specs=[SMEM] + [VMEM] * 10,
        out_specs=[VMEM] * 2,
        scratch_shapes=[
            pltpu.VMEM((2, planes, 4, 8, LANES), F32),
            pltpu.VMEM((planes, 4, 8, LANES), F32),
            pltpu.VMEM(((1 + rows) * owners, LANES), F32),
        ],
        compiler_params=params(),
        name="heat_step",
    )(slab_info, slab, *received, arrived)
    returned = lax.all_to_all(factor, ("gx", "gy"), split_axis=0, concat_axis=0, tiled=True)
    renewed_heat_rise = pl.pallas_call(
        finish_slab,
        out_shape=shape(slab_cap, 32, LANES),
        in_specs=[SMEM, VMEM],
        out_specs=VMEM,
        compiler_params=params(),
        name="finish_slab",
    )(slab_info, warm)
    renewed_sigma_omega = pl.pallas_call(
        finish_conduct,
        out_shape=shape(LANES, CZ),
        in_specs=[SMEM] + [VMEM] * 2,
        out_specs=VMEM,
        scratch_shapes=[pltpu.VMEM((CZ + slab_cap, LANES), F32)],
        compiler_params=params(),
        name="finish_conduct",
    )(starts, returned, sigma_omega_cellwise.reshape(LANES, CZ))
    return (
        field_new.reshape(6, CX, CY, CZ),
        renewed_heat_rise[None, None, None],
        renewed_sigma_omega.reshape(CX, CY, CZ),
    )


def solution(mesh):
    return jax.shard_map(
        body,
        mesh=mesh,
        in_specs=(
            P(None, "gx", "gy", "gz"),
            P(None, "gx", "gy", "gz"),
            P("gx", "gy", "gz"),
            P("gx", "gy", "gz", None, None, None),
            P("gx", "gy", "gz", None, None),
            P("gx", "gy", "gz", None),
            P("gz", None),
            P("gx", "gy", "gz", None, None, None),
            P("gx", "gy", "gz", None, None, None),
        ),
        out_specs=(
            P(None, "gx", "gy", "gz"),
            P("gx", "gy", "gz", None, None, None),
            P("gx", "gy", "gz"),
        ),
        check_vma=False,
    )
```

profile of v0, /device:TPU:1, one launch (start us, length us, event | category | flops | bytes accessed | tf_op | source)
XLA Modules:
  0.0 157.2 jit_solution(1320355152397206206)
XLA Ops:
  3.0 3.6 %collective-permute-start = (f32[256,128]{1,0:T(8,128)S(1)}, f32[256,128]{1,0:T(8,128)S(1)}, u32[]{:S(2)}, u32[]{:S(2)}) collective-permute-start(f32[256,128]{1,0:T(8,128)S(1)} %get-tuple-element.35), channel_id=1, source_target_pairs={{0,192},{64,0},{128,64},{192,128},{1,193},{65,1},{129,65},{193,129... | collective-permute-start | bytes 393224 | tf_op jit(solution)/shard_map/ppermute | solution.py:468
  10.6 6.1 %prepare_slab.1.refs_0_.slab = f32[24,2,4,8,128]{4,3,2,1,0:T(8,128)S(1)} custom-call(f32[24,32,128]{2,1,0:T(8,128)S(1)} %bitcast.29, f32[24,32,128]{2,1,0:T(8,128)S(1)} %bitcast.30), custom_call_target="tpu_custom_call" | custom-call | flops 1048576 | bytes 1572864 | tf_op jit(solution)/shard_map/prepare_slab/pallas_call | solution.py:521
  17.3 1.8 %collective-permute-start.13 = (f32[2,4,8,128]{3,2,1,0:T(8,128)S(1)}, f32[2,4,8,128]{3,2,1,0:T(8,128)S(1)}, u32[]{:S(2)}, u32[]{:S(2)}) collective-permute-start(f32[2,4,8,128]{3,2,1,0:T(8,128)S(1)} %get-tuple-element.51), channel_id=1, source_target_pairs={{0,255},{8,0},{16,8},{24,16},{32,24},{40,32},{48,40},{56,48},{64,5... | collective-permute-start | bytes 98312 | tf_op jit(solution)/shard_map/ppermute | solution.py:476
  19.7 1.6 %pack_y.2 = (f32[256,128]{1,0:T(8,128)S(1)}, f32[256,128]{1,0:T(8,128)S(1)}) custom-call(s32[6]{0:T(128)S(1)} %convert_element_type.8.flags, f32[6,256,128]{2,1,0:T(8,128)S(1)} %get-tuple-element.32.field.refs_0_.refs_5_, f32[256,128]{1,0:T(8,128)S(1)} %collective-permute-done.x_plus.refs_1_.refs_6_.xp, ...), custom_call_target="tpu_custom_call" | custom-call | flops 1048576 | bytes 1572864 | tf_op jit(solution)/shard_map/pack_y/pallas_call | solution.py:533
  21.3 8.4 %collective-permute-start.2 = (f32[256,128]{1,0:T(8,128)S(1)}, f32[256,128]{1,0:T(8,128)S(1)}, u32[]{:S(2)}, u32[]{:S(2)}) collective-permute-start(f32[256,128]{1,0:T(8,128)S(1)} %get-tuple-element.37), channel_id=1, source_target_pairs={{0,56},{8,0},{16,8},{24,16},{32,24},{40,32},{48,40},{56,48},{1,57}... | collective-permute-start | bytes 393224 | tf_op jit(solution)/shard_map/ppermute | solution.py:468
  36.3 1.7 %collective-permute-done.5.zm = f32[16,128]{1,0:T(8,128)S(1)} collective-permute-done((f32[16,128]{1,0:T(8,128)S(1)}, f32[16,128]{1,0:T(8,128)S(1)}, u32[]{:S(2)}, u32[]{:S(2)}) %collective-permute-start.5) | collective-permute-done | bytes 8224 | tf_op jit(solution)/shard_map/ppermute | solution.py:468
  38.1 3.4 %copy-done = bf16[1,1,1,16,512,512]{5,4,3,2,1,0:T(8,128)(2,1)S(1)} copy-done((bf16[1,1,1,16,512,512]{5,4,3,2,1,0:T(8,128)(2,1)S(1)}, bf16[1,1,1,16,512,512]{5,4,3,2,1,0:T(8,128)(2,1)}, u32[]{:S(2)}) %copy-start) | copy-done | bytes 8388632
  42.1 15.7 %sweep.2 = (f32[6,256,128]{2,1,0:T(8,128)S(1)}, f32[256,128]{1,0:T(8,128)S(1)}, f32[256,128]{1,0:T(8,128)S(1)}) custom-call(s32[6]{0:T(128)S(1)} %convert_element_type.8.flags, s32[16]{0:T(128)S(1)} %bitcast.32, f32[6,256,128]{2,1,0:T(8,128)S(1)} %get-tuple-element.32.field.refs_0_.refs_5_, f32[6,256,128]{2,1,0:T(8,128)S(1)} %get-tuple-element.33.drive, ...), custom_call_target="tpu_custom_call" | custom-call | flops 268435456 | bytes 3145728 | tf_op jit(solution)/shard_map/sweep/pallas_call | solution.py:598
  57.8 4.6 %collective-permute-start.6 = (f32[256,128]{1,0:T(8,128)S(1)}, f32[256,128]{1,0:T(8,128)S(1)}, u32[]{:S(2)}, u32[]{:S(2)}) collective-permute-start(f32[256,128]{1,0:T(8,128)S(1)} %get-tuple-element.43), channel_id=1, source_target_pairs={{0,192},{64,0},{128,64},{192,128},{1,193},{65,1},{129,65},{193,129... | collective-permute-start | bytes 393224 | tf_op jit(solution)/shard_map/ppermute | solution.py:468
  63.0 6.5 %collective-permute-start.15 = (f32[2,4,8,128]{3,2,1,0:T(8,128)S(1)}, f32[2,4,8,128]{3,2,1,0:T(8,128)S(1)}, u32[]{:S(2)}, u32[]{:S(2)}) collective-permute-start(f32[2,4,8,128]{3,2,1,0:T(8,128)S(1)} %get-tuple-element.53), channel_id=1, source_target_pairs={{0,255},{8,0},{16,8},{24,16},{32,24},{40,32},{48,40},{56,48},{64,5... | collective-permute-start | bytes 98312 | tf_op jit(solution)/shard_map/ppermute | solution.py:476
  69.8 1.6 %pack_y.3 = (f32[256,128]{1,0:T(8,128)S(1)}, f32[256,128]{1,0:T(8,128)S(1)}) custom-call(s32[6]{0:T(128)S(1)} %convert_element_type.8.flags, f32[6,256,128]{2,1,0:T(8,128)S(1)} %get-tuple-element.42.field.refs_0_.refs_5_, f32[256,128]{1,0:T(8,128)S(1)} %collective-permute-done.6.x_plus.refs_1_.refs_6_.xp, ...), custom_call_target="tpu_custom_call" | custom-call | flops 1048576 | bytes 1572864 | tf_op jit(solution)/shard_map/pack_y/pallas_call | solution.py:533
  71.4 5.3 %collective-permute-start.8 = (f32[256,128]{1,0:T(8,128)S(1)}, f32[256,128]{1,0:T(8,128)S(1)}, u32[]{:S(2)}, u32[]{:S(2)}) collective-permute-start(f32[256,128]{1,0:T(8,128)S(1)} %get-tuple-element.45), channel_id=1, source_target_pairs={{0,56},{8,0},{16,8},{24,16},{32,24},{40,32},{48,40},{56,48},{1,57}... | collective-permute-start | bytes 393224 | tf_op jit(solution)/shard_map/ppermute | solution.py:468
  79.3 1.5 collective-permute-start.11
  81.3 4.3 %collective-permute-start.17 = (f32[2,4,8,128]{3,2,1,0:T(8,128)S(1)}, f32[2,4,8,128]{3,2,1,0:T(8,128)S(1)}, u32[]{:S(2)}, u32[]{:S(2)}) collective-permute-start(f32[2,4,8,128]{3,2,1,0:T(8,128)S(1)} %get-tuple-element.55), channel_id=1, source_target_pairs={{0,255},{8,0},{16,8},{24,16},{32,24},{40,32},{48,40},{56,48},{64,5... | collective-permute-start | bytes 98312 | tf_op jit(solution)/shard_map/ppermute | solution.py:476
  85.7 17.5 %sweep.3 = (f32[6,128,256]{2,1,0:T(8,128)}, f32[256,128]{1,0:T(8,128)S(1)}) custom-call(s32[6]{0:T(128)S(1)} %convert_element_type.8.flags, s32[16]{0:T(128)S(1)} %bitcast.33, f32[6,256,128]{2,1,0:T(8,128)S(1)} %get-tuple-element.42.field.refs_0_.refs_5_, f32[6,256,128]{2,1,0:T(8,128)S(1)} %get-tuple-element.33.drive, ...), custom_call_target="tpu_custom_call" | custom-call | flops 268435456 | bytes 3145728 | tf_op jit(solution)/shard_map/sweep/pallas_call | solution.py:598
  103.2 2.7 %collective-permute-start.21 = (f32[8,128]{1,0:T(8,128)S(1)}, f32[8,128]{1,0:T(8,128)S(1)}, u32[]{:S(2)}, u32[]{:S(2)}) collective-permute-start(f32[8,128]{1,0:T(8,128)S(1)} %get-tuple-element.61), channel_id=1, source_target_pairs={{0,7},{1,0},{2,1},{3,2},{4,3},{5,4},{6,5},{7,6},{8,15},{9,8},{10,9... | collective-permute-start | bytes 12296 | tf_op jit(solution)/shard_map/ppermute | solution.py:468
  108.3 9.7 %all-to-all-start = ((f32[32,32,128]{2,1,0:T(8,128)}), f32[32,32,128]{2,1,0:T(8,128)S(1)}, u32[]{:S(2)}, u32[]{:S(2)}) async-start(f32[32,32,128]{2,1,0:T(8,128)} %pack_heat.1), calls=%async_computation | async-start | bytes 1048576 | tf_op jit(solution)/shard_map/all_to_all | solution.py:624
  118.9 1.5 collective-permute-start.18
  120.4 6.3 %collective-permute-done.19 = f32[2,4,8,128]{3,2,1,0:T(8,128)S(1)} collective-permute-done((f32[2,4,8,128]{3,2,1,0:T(8,128)S(1)}, f32[2,4,8,128]{3,2,1,0:T(8,128)S(1)}, u32[]{:S(2)}, u32[]{:S(2)}) %collective-permute-start.19) | collective-permute-done | bytes 32800 | tf_op jit(solution)/shard_map/ppermute | solution.py:476
  127.1 2.5 %all-to-all-done.arrived = f32[32,32,128]{2,1,0:T(8,128)S(1)} async-done(((f32[32,32,128]{2,1,0:T(8,128)}), f32[32,32,128]{2,1,0:T(8,128)S(1)}, u32[]{:S(2)}, u32[]{:S(2)}) %all-to-all-start) | async-done | bytes 524320 | tf_op jit(solution)/shard_map/all_to_all | solution.py:624
  129.6 6.9 %heat_step.1 = (f32[32,24,128]{2,1,0:T(8,128)}, f32[24,4,8,128]{3,2,1,0:T(8,128)S(1)}) custom-call(s32[3]{0:T(128)S(1)} %pad_add_fusion.length.slab_info, f32[24,2,4,8,128]{4,3,2,1,0:T(8,128)S(1)} %prepare_slab.1.refs_0_.slab, f32[2,4,8,128]{3,2,1,0:T(8,128)S(1)} %broadcast_select_fusion.7.refs_1_.b1, ...), custom_call_target="tpu_custom_call" | custom-call | tf_op jit(solution)/shard_map/heat_step/pallas_call | solution.py:626
  136.5 9.1 %all-to-all-start.1 = ((f32[32,24,128]{2,1,0:T(8,128)}), f32[32,24,128]{2,1,0:T(8,128)S(1)}, u32[]{:S(2)}, u32[]{:S(2)}) async-start(f32[32,24,128]{2,1,0:T(8,128)} %get-tuple-element.60), calls=%async_computation.1 | async-start | bytes 786432 | tf_op jit(solution)/shard_map/all_to_all | solution.py:639
  145.6 3.8 %finish_slab.1 = f32[24,32,128]{2,1,0:T(8,128)} custom-call(s32[3]{0:T(128)S(1)} %pad_add_fusion.length.slab_info, f32[24,4,8,128]{3,2,1,0:T(8,128)S(1)} %get-tuple-element.59.warm), custom_call_target="tpu_custom_call" | custom-call | tf_op jit(solution)/shard_map/finish_slab/pallas_call | solution.py:640
  149.4 6.5 %all-to-all-done.1.returned = f32[32,24,128]{2,1,0:T(8,128)S(1)} async-done(((f32[32,24,128]{2,1,0:T(8,128)}), f32[32,24,128]{2,1,0:T(8,128)S(1)}, u32[]{:S(2)}, u32[]{:S(2)}) %all-to-all-start.1) | async-done | bytes 393248 | tf_op jit(solution)/shard_map/all_to_all | solution.py:639
  (79 shorter events, 23.6 us)
Async XLA Ops:
  3.0 16.7 %collective-permute-start = (f32[256,128]{1,0:T(8,128)S(1)}, f32[256,128]{1,0:T(8,128)S(1)}, u32[]{:S(2)}, u32[]{:S(2)}) collective-permute-start(f32[256,128]{1,0:T(8,128)S(1)} %get-tuple-element.35), channel_id=1, source_target_pairs={{0,192},{64,0},{128,64},{192,128},{1,193},{65,1},{129,65},{193,129... | collective-permute-start | bytes 393224 | tf_op jit(solution)/shard_map/ppermute | solution.py:468
  6.6 13.1 %collective-permute-start.1 = (f32[256,128]{1,0:T(8,128)S(1)}, f32[256,128]{1,0:T(8,128)S(1)}, u32[]{:S(2)}, u32[]{:S(2)}) collective-permute-start(f32[256,128]{1,0:T(8,128)S(1)} %get-tuple-element.36), channel_id=1, source_target_pairs={{0,64},{64,128},{128,192},{192,0},{1,65},{65,129},{129,193},{193,1... | collective-permute-start | bytes 393224 | tf_op jit(solution)/shard_map/ppermute | solution.py:468
  17.3 17.8 %collective-permute-start.13 = (f32[2,4,8,128]{3,2,1,0:T(8,128)S(1)}, f32[2,4,8,128]{3,2,1,0:T(8,128)S(1)}, u32[]{:S(2)}, u32[]{:S(2)}) collective-permute-start(f32[2,4,8,128]{3,2,1,0:T(8,128)S(1)} %get-tuple-element.51), channel_id=1, source_target_pairs={{0,255},{8,0},{16,8},{24,16},{32,24},{40,32},{48,40},{56,48},{64,5... | collective-permute-start | bytes 98312 | tf_op jit(solution)/shard_map/ppermute | solution.py:476
  19.1 43.4 %collective-permute-start.12 = (f32[2,4,8,128]{3,2,1,0:T(8,128)S(1)}, f32[2,4,8,128]{3,2,1,0:T(8,128)S(1)}, u32[]{:S(2)}, u32[]{:S(2)}) collective-permute-start(f32[2,4,8,128]{3,2,1,0:T(8,128)S(1)} %get-tuple-element.50), channel_id=1, source_target_pairs={{0,8},{8,16},{16,24},{24,32},{32,40},{40,48},{48,56},{56,64},{64,7... | collective-permute-start | bytes 98312 | tf_op jit(solution)/shard_map/ppermute | solution.py:476
  21.3 11.7 %collective-permute-start.2 = (f32[256,128]{1,0:T(8,128)S(1)}, f32[256,128]{1,0:T(8,128)S(1)}, u32[]{:S(2)}, u32[]{:S(2)}) collective-permute-start(f32[256,128]{1,0:T(8,128)S(1)} %get-tuple-element.37), channel_id=1, source_target_pairs={{0,56},{8,0},{16,8},{24,16},{32,24},{40,32},{48,40},{56,48},{1,57}... | collective-permute-start | bytes 393224 | tf_op jit(solution)/shard_map/ppermute | solution.py:468
  29.7 3.3 %collective-permute-start.3 = (f32[256,128]{1,0:T(8,128)S(1)}, f32[256,128]{1,0:T(8,128)S(1)}, u32[]{:S(2)}, u32[]{:S(2)}) collective-permute-start(f32[256,128]{1,0:T(8,128)S(1)} %get-tuple-element.38), channel_id=1, source_target_pairs={{0,8},{8,16},{16,24},{24,32},{32,40},{40,48},{48,56},{56,0},{1,9},... | collective-permute-start | bytes 393224 | tf_op jit(solution)/shard_map/ppermute | solution.py:468
  33.5 2.8 %collective-permute-start.4 = (f32[16,128]{1,0:T(8,128)S(1)}, f32[16,128]{1,0:T(8,128)S(1)}, u32[]{:S(2)}, u32[]{:S(2)}) collective-permute-start(f32[16,128]{1,0:T(8,128)S(1)} %get-tuple-element.39), channel_id=1, source_target_pairs={{0,7},{1,0},{2,1},{3,2},{4,3},{5,4},{6,5},{7,6},{8,15},{9,8},{10,9... | collective-permute-start | bytes 24584 | tf_op jit(solution)/shard_map/ppermute | solution.py:468
  34.4 3.7 %collective-permute-start.5 = (f32[16,128]{1,0:T(8,128)S(1)}, f32[16,128]{1,0:T(8,128)S(1)}, u32[]{:S(2)}, u32[]{:S(2)}) collective-permute-start(f32[16,128]{1,0:T(8,128)S(1)} %get-tuple-element.40), channel_id=1, source_target_pairs={{0,1},{1,2},{2,3},{3,4},{4,5},{5,6},{6,7},{7,0},{8,9},{9,10},{10,1... | collective-permute-start | bytes 24584 | tf_op jit(solution)/shard_map/ppermute | solution.py:468
  57.8 12.0 %collective-permute-start.6 = (f32[256,128]{1,0:T(8,128)S(1)}, f32[256,128]{1,0:T(8,128)S(1)}, u32[]{:S(2)}, u32[]{:S(2)}) collective-permute-start(f32[256,128]{1,0:T(8,128)S(1)} %get-tuple-element.43), channel_id=1, source_target_pairs={{0,192},{64,0},{128,64},{192,128},{1,193},{65,1},{129,65},{193,129... | collective-permute-start | bytes 393224 | tf_op jit(solution)/shard_map/ppermute | solution.py:468
  62.5 7.3 %collective-permute-start.7 = (f32[256,128]{1,0:T(8,128)S(1)}, f32[256,128]{1,0:T(8,128)S(1)}, u32[]{:S(2)}, u32[]{:S(2)}) collective-permute-start(f32[256,128]{1,0:T(8,128)S(1)} %get-tuple-element.44), channel_id=1, source_target_pairs={{0,64},{64,128},{128,192},{192,0},{1,65},{65,129},{129,193},{193,1... | collective-permute-start | bytes 393224 | tf_op jit(solution)/shard_map/ppermute | solution.py:468
  63.0 13.7 %collective-permute-start.15 = (f32[2,4,8,128]{3,2,1,0:T(8,128)S(1)}, f32[2,4,8,128]{3,2,1,0:T(8,128)S(1)}, u32[]{:S(2)}, u32[]{:S(2)}) collective-permute-start(f32[2,4,8,128]{3,2,1,0:T(8,128)S(1)} %get-tuple-element.53), channel_id=1, source_target_pairs={{0,255},{8,0},{16,8},{24,16},{32,24},{40,32},{48,40},{56,48},{64,5... | collective-permute-start | bytes 98312 | tf_op jit(solution)/shard_map/ppermute | solution.py:476
  69.7 11.1 %collective-permute-start.14 = (f32[2,4,8,128]{3,2,1,0:T(8,128)S(1)}, f32[2,4,8,128]{3,2,1,0:T(8,128)S(1)}, u32[]{:S(2)}, u32[]{:S(2)}) collective-permute-start(f32[2,4,8,128]{3,2,1,0:T(8,128)S(1)} %get-tuple-element.52), channel_id=1, source_target_pairs={{0,8},{8,16},{16,24},{24,32},{32,40},{40,48},{48,56},{56,64},{64,7... | collective-permute-start | bytes 98312 | tf_op jit(solution)/shard_map/ppermute | solution.py:476
  71.4 6.3 %collective-permute-start.8 = (f32[256,128]{1,0:T(8,128)S(1)}, f32[256,128]{1,0:T(8,128)S(1)}, u32[]{:S(2)}, u32[]{:S(2)}) collective-permute-start(f32[256,128]{1,0:T(8,128)S(1)} %get-tuple-element.45), channel_id=1, source_target_pairs={{0,56},{8,0},{16,8},{24,16},{32,24},{40,32},{48,40},{56,48},{1,57}... | collective-permute-start | bytes 393224 | tf_op jit(solution)/shard_map/ppermute | solution.py:468
  76.7 2.0 %collective-permute-start.9 = (f32[256,128]{1,0:T(8,128)S(1)}, f32[256,128]{1,0:T(8,128)S(1)}, u32[]{:S(2)}, u32[]{:S(2)}) collective-permute-start(f32[256,128]{1,0:T(8,128)S(1)} %get-tuple-element.46), channel_id=1, source_target_pairs={{0,8},{8,16},{16,24},{24,32},{32,40},{40,48},{48,56},{56,0},{1,9},... | collective-permute-start | bytes 393224 | tf_op jit(solution)/shard_map/ppermute | solution.py:468
  79.2 6.4 %collective-permute-start.10 = (f32[16,128]{1,0:T(8,128)S(1)}, f32[16,128]{1,0:T(8,128)S(1)}, u32[]{:S(2)}, u32[]{:S(2)}) collective-permute-start(f32[16,128]{1,0:T(8,128)S(1)} %get-tuple-element.47), channel_id=1, source_target_pairs={{0,7},{1,0},{2,1},{3,2},{4,3},{5,4},{6,5},{7,6},{8,15},{9,8},{10,9... | collective-permute-start | bytes 24584 | tf_op jit(solution)/shard_map/ppermute | solution.py:468
  79.3 6.4 %collective-permute-start.11 = (f32[16,128]{1,0:T(8,128)S(1)}, f32[16,128]{1,0:T(8,128)S(1)}, u32[]{:S(2)}, u32[]{:S(2)}) collective-permute-start(f32[16,128]{1,0:T(8,128)S(1)} %get-tuple-element.48), channel_id=1, source_target_pairs={{0,1},{1,2},{2,3},{3,4},{4,5},{5,6},{6,7},{7,0},{8,9},{9,10},{10,1... | collective-permute-start | bytes 24584 | tf_op jit(solution)/shard_map/ppermute | solution.py:468
  81.3 24.6 %collective-permute-start.17 = (f32[2,4,8,128]{3,2,1,0:T(8,128)S(1)}, f32[2,4,8,128]{3,2,1,0:T(8,128)S(1)}, u32[]{:S(2)}, u32[]{:S(2)}) collective-permute-start(f32[2,4,8,128]{3,2,1,0:T(8,128)S(1)} %get-tuple-element.55), channel_id=1, source_target_pairs={{0,255},{8,0},{16,8},{24,16},{32,24},{40,32},{48,40},{56,48},{64,5... | collective-permute-start | bytes 98312 | tf_op jit(solution)/shard_map/ppermute | solution.py:476
  85.6 32.4 %collective-permute-start.16 = (f32[2,4,8,128]{3,2,1,0:T(8,128)S(1)}, f32[2,4,8,128]{3,2,1,0:T(8,128)S(1)}, u32[]{:S(2)}, u32[]{:S(2)}) collective-permute-start(f32[2,4,8,128]{3,2,1,0:T(8,128)S(1)} %get-tuple-element.54), channel_id=1, source_target_pairs={{0,8},{8,16},{16,24},{24,32},{32,40},{40,48},{48,56},{56,64},{64,7... | collective-permute-start | bytes 98312 | tf_op jit(solution)/shard_map/ppermute | solution.py:476
  103.2 3.7 %collective-permute-start.20 = (f32[8,128]{1,0:T(8,128)S(1)}, f32[8,128]{1,0:T(8,128)S(1)}, u32[]{:S(2)}, u32[]{:S(2)}) collective-permute-start(f32[8,128]{1,0:T(8,128)S(1)} %get-tuple-element.62), channel_id=1, source_target_pairs={{0,1},{1,2},{2,3},{3,4},{4,5},{5,6},{6,7},{7,0},{8,9},{9,10},{10,1... | collective-permute-start | bytes 12296 | tf_op jit(solution)/shard_map/ppermute | solution.py:468
  103.2 3.7 %collective-permute-start.21 = (f32[8,128]{1,0:T(8,128)S(1)}, f32[8,128]{1,0:T(8,128)S(1)}, u32[]{:S(2)}, u32[]{:S(2)}) collective-permute-start(f32[8,128]{1,0:T(8,128)S(1)} %get-tuple-element.61), channel_id=1, source_target_pairs={{0,7},{1,0},{2,1},{3,2},{4,3},{5,4},{6,5},{7,6},{8,15},{9,8},{10,9... | collective-permute-start | bytes 12296 | tf_op jit(solution)/shard_map/ppermute | solution.py:468
  108.3 21.3 %all-to-all-start = ((f32[32,32,128]{2,1,0:T(8,128)}), f32[32,32,128]{2,1,0:T(8,128)S(1)}, u32[]{:S(2)}, u32[]{:S(2)}) async-start(f32[32,32,128]{2,1,0:T(8,128)} %pack_heat.1), calls=%async_computation | async-start | bytes 1048576 | tf_op jit(solution)/shard_map/all_to_all | solution.py:624
  118.6 8.1 %collective-permute-start.19 = (f32[2,4,8,128]{3,2,1,0:T(8,128)S(1)}, f32[2,4,8,128]{3,2,1,0:T(8,128)S(1)}, u32[]{:S(2)}, u32[]{:S(2)}) collective-permute-start(f32[2,4,8,128]{3,2,1,0:T(8,128)S(1)} %get-tuple-element.57), channel_id=1, source_target_pairs={{0,255},{8,0},{16,8},{24,16},{32,24},{40,32},{48,40},{56,48},{64,5... | collective-permute-start | bytes 98312 | tf_op jit(solution)/shard_map/ppermute | solution.py:476
  118.9 8.1 %collective-permute-start.18 = (f32[2,4,8,128]{3,2,1,0:T(8,128)S(1)}, f32[2,4,8,128]{3,2,1,0:T(8,128)S(1)}, u32[]{:S(2)}, u32[]{:S(2)}) collective-permute-start(f32[2,4,8,128]{3,2,1,0:T(8,128)S(1)} %get-tuple-element.56), channel_id=1, source_target_pairs={{0,8},{8,16},{16,24},{24,32},{32,40},{40,48},{48,56},{56,64},{64,7... | collective-permute-start | bytes 98312 | tf_op jit(solution)/shard_map/ppermute | solution.py:476
  136.5 19.4 %all-to-all-start.1 = ((f32[32,24,128]{2,1,0:T(8,128)}), f32[32,24,128]{2,1,0:T(8,128)S(1)}, u32[]{:S(2)}, u32[]{:S(2)}) async-start(f32[32,24,128]{2,1,0:T(8,128)} %get-tuple-element.60), calls=%async_computation.1 | async-start | bytes 786432 | tf_op jit(solution)/shard_map/all_to_all | solution.py:639
  (11 other events, 176.0 us)
where the time goes:
time: 158 us; the launch traced here: 157 us
  starting transfers between devices  61.7 us (39%)
  Pallas kernels  60.8 us (38%)
  waiting for transfers between devices  21.5 us (14%)
  local copies, waits for them, and re-layouts  10.1 us (6%)
  other arithmetic  2.26 us (1%)
    pallas_call x2, Pallas kernels, body(): pl.pallas_call(functools.partial(sweep, final), out_shape=outs, in_specs=...  33.2 us
    ppermute x14, starting transfers between devices, turn(): lax.ppermute(value, axis, [(i, (i + step) % count) for i in range(count)])  27.8 us
    ppermute x8, starting transfers between devices, ring(): return lax.ppermute(value, ('gx', 'gy', 'gz'), pairs)  15 us
    unnamed x22, local copies, waits for them, and re-layouts  9.96 us
    all_to_all x1, starting transfers between devices, body(): lax.all_to_all(outgoing, ('gx', 'gy'), split_axis=0, concat_axis=0, tiled...  9.72 us
    all_to_all x1, starting transfers between devices, body(): lax.all_to_all(factor, ('gx', 'gy'), split_axis=0, concat_axis=0, tiled=T...  9.09 us
    pallas_call x1, Pallas kernels, body(): pl.pallas_call(heat_step, out_shape=(shape(owners, slab_cap, LANES), shap...  6.91 us
    ppermute x8, waiting for transfers between devices, ring(): return lax.ppermute(value, ('gx', 'gy', 'gz'), pairs)  6.62 us
  transfers between devices with their start and end apart: 24, of which 9 were waited for; matrix products, arithmetic and copies ran while one was open for 2% of the time, Pallas kernels for 33%

commit v1 on v0

--- a/solution.py
+++ b/solution.py
@@ -21,18 +21,19 @@
 PLANE = 24
 WINDOW = 21
 MAXSEG = 19
-COLS = LANES // 4
 F32 = jnp.float32
 HALO = 8
 CHUNK = 32
 XP_PLUS, XP_MINUS = 6, 7
+X_BITS, Y_BITS = 112, 15
 RING = SECTIONS
+HALF = CZ // 2
+CORNER = (0, 1, 16, 17)
 VMEM = pl.BlockSpec(memory_space=pltpu.VMEM)
 SMEM = pl.BlockSpec(memory_space=pltpu.SMEM)
-ANY = pl.BlockSpec(memory_space=pl.ANY)
-
-
-def params(mib=40):
+
+
+def params(mib=24):
     return pltpu.CompilerParams(vmem_limit_bytes=mib << 20)
 
 
@@ -50,85 +51,66 @@
 
 
 def x_slot(slot):
-    return (slot // 4) * 64 + (slot % 4) * 8
+    return 16 * slot
 
 
 def y_slot(slot):
-    return (slot // 8) * 32 + slot % 8
+    return slot
 
 
 def x_next(value, halo, slot):
     lane = lane_of(value)
-    inner = jnp.where(lane < 64, ahead(value, 64), ahead(value, -56))
-    return jnp.where((lane // 8) % 4 + 4 * (lane // 64) == 7, ahead(halo, x_slot(slot) - 88), inner)
+    return jnp.where(lane & X_BITS == X_BITS, ahead(halo, x_slot(slot) - X_BITS), ahead(value, 16))
 
 
 def x_before(value, halo, slot):
     lane = lane_of(value)
-    inner = jnp.where(lane < 64, ahead(value, 56), ahead(value, -64))
-    return jnp.where((lane // 8) % 4 + 4 * (lane // 64) == 0, ahead(halo, x_slot(slot)), inner)
+    return jnp.where(lane & X_BITS == 0, ahead(halo, x_slot(slot)), ahead(value, -16))
 
 
 def y_next(value, halo, slot):
     lane = lane_of(value)
-    low = (lane // 32) % 2 == 0
-    inner = jnp.where(low, ahead(value, 32), ahead(value, -31))
-    return jnp.where(lane % 8 + 8 * ((lane // 32) % 2) == 15, ahead(halo, y_slot(slot) - 39), inner)
+    return jnp.where(lane & Y_BITS == Y_BITS, ahead(halo, y_slot(slot) - Y_BITS), ahead(value, 1))
 
 
 def y_before(value, halo, slot):
     lane = lane_of(value)
-    low = (lane // 32) % 2 == 0
-    inner = jnp.where(low, ahead(value, 31), ahead(value, -32))
-    return jnp.where(lane % 8 + 8 * ((lane // 32) % 2) == 0, ahead(halo, y_slot(slot)), inner)
+    return jnp.where(lane & Y_BITS == 0, ahead(halo, y_slot(slot)), ahead(value, -1))
 
 
 def x_faces(parts):
     lane = lane_of(parts[0])
-    own = (lane // 8) % 4 + 4 * (lane // 64)
+    own = lane & X_BITS
     first = jnp.zeros_like(parts[0])
     last = first
     for slot, part in enumerate(parts):
-        first = jnp.where(own == slot, ahead(part, -x_slot(slot)), first)
-        last = jnp.where(own == slot, ahead(part, 88 - x_slot(slot)), last)
+        mine = own == x_slot(slot)
+        first = jnp.where(mine, ahead(part, -x_slot(slot)), first)
+        last = jnp.where(mine, ahead(part, X_BITS - x_slot(slot)), last)
     return first, last
 
 
 def y_faces(parts):
     lane = lane_of(parts[0])
-    own = lane % 8 + 8 * ((lane // 32) % 2)
+    own = lane & Y_BITS
     first = jnp.zeros_like(parts[0])
     last = first
     for slot, part in enumerate(parts):
-        first = jnp.where(own == slot, ahead(part, -y_slot(slot)), first)
-        last = jnp.where(own == slot, ahead(part, 39 - y_slot(slot)), last)
+        mine = own == y_slot(slot)
+        first = jnp.where(mine, ahead(part, -y_slot(slot)), first)
+        last = jnp.where(mine, ahead(part, Y_BITS - y_slot(slot)), last)
     return first, last
 
 
-def cell_rows(part):
-    for dx in range(2):
-        for dy in range(2):
-            for a in range(CX // 2):
-                yield (2 * dx + dy) * 32 + a * 8, 32 * a + 16 * dx + dy
-
-
-def to_planes(source, index, target, out_index, turned):
-    for to_row, from_row in cell_rows(None):
-        for half in range(CZ // LANES):
-            turned[half, to_row : to_row + 8, :] = source[index, half, pl.ds(from_row, 8, stride=2), :]
+def to_planes(source, index, target):
     for half in range(CZ // LANES):
-        target[out_index, half * LANES : (half + 1) * LANES, :] = turned[half].T
-
-
-def load_halves(source, loaded, index):
-    for half in range(CZ // LANES):
-        loaded[index, half] = source[index, :, half * LANES : (half + 1) * LANES]
-
-
-def prepare_field(field, planes, first, last, loaded, turned):
+        lanes = slice(half * LANES, (half + 1) * LANES)
+        target[index, lanes, :] = source[index, :, lanes].T
+
+
+def prepare_field(field, planes, first, last):
     for comp in range(6):
-        load_halves(field, loaded, comp)
-        to_planes(loaded, comp, planes, comp, turned.at[comp % 2])
+        to_planes(field, comp, planes)
 
     def chunk(i, carry):
         rows = pl.ds(pl.multiple_of(i * CHUNK, CHUNK), CHUNK)
@@ -140,12 +122,10 @@
     lax.fori_loop(0, CZ // CHUNK, chunk, 0)
 
 
-def prepare_drive(drive, conduct, diagonal, drive_planes, conduct_planes, diagonal_turned, loaded, turned):
+def prepare_drive(drive, conduct, diagonal, drive_planes, conduct_planes, diagonal_turned):
     for comp in range(6):
-        load_halves(drive, loaded, comp)
-        to_planes(loaded, comp, drive_planes, comp, turned.at[comp % 2])
-    load_halves(conduct, loaded, 0)
-    to_planes(loaded, 0, conduct_planes, 0, turned.at[0])
+        to_planes(drive, comp, drive_planes)
+    to_planes(conduct, 0, conduct_planes)
     diagonal_turned[...] = diagonal[...].T
 
 
@@ -153,17 +133,80 @@
     return jnp.where(flag > 0, value, jnp.zeros_like(value))
 
 
-def pack_y(flags, field, x_plus, x_minus, first, last):
+def tiled(plane):
+    return swap_tiles(plane.reshape(4, 8, LANES)).reshape(32, LANES)
+
+
+def pack_y(round_id, flags, info, field, x_plus, x_minus, *rest):
+    up, down = rest[-2:]
+
     def chunk(i, carry):
+        parts = []
+        for base in (0, HALF):
+            rows = pl.ds(pl.multiple_of(base + i * CHUNK, CHUNK), CHUNK)
+            parts += [field[comp, rows, :] for comp in range(6)]
+            parts += [kept(flags[1], x_plus[rows, :]), kept(flags[0], x_minus[rows, :])]
+        low, high = y_faces(parts)
         rows = pl.ds(pl.multiple_of(i * CHUNK, CHUNK), CHUNK)
-        parts = [field[comp, rows, :] for comp in range(6)]
-        parts += [kept(flags[1], x_plus[rows, :]), kept(flags[0], x_minus[rows, :])]
-        low, high = y_faces(parts)
-        first[rows, :] = low
-        last[rows, :] = high
+        down[rows, :] = low
+        up[rows, :] = high
         return carry
 
-    lax.fori_loop(0, CZ // CHUNK, chunk, 0)
+    lax.fori_loop(0, HALF // CHUNK, chunk, 0)
+    if round_id == 1:
+        for depth in range(RING):
+            top = jnp.maximum(info[0] - 1 - depth, 0)
+            for which in range(2):
+                at = HALF + 64 * depth + 32 * which
+                up[at : at + 32, :] = tiled(rest[which][top])
+                down[at : at + 32, :] = tiled(rest[which][depth])
+        count = jnp.full((8, LANES), info[0], jnp.int32).astype(F32)
+        up[-8:, :] = count
+        down[-8:, :] = count
+    else:
+        below, above = rest[:2]
+        size = 64 * (RING - 1)
+        up[HALF : HALF + size, :] = kept(info[1], below[HALF : HALF + size, :])
+        down[HALF : HALF + size, :] = kept(info[2], above[HALF : HALF + size, :])
+        up[-8:, :] = below[-8:, :]
+        down[-8:, :] = above[-8:, :]
+
+
+def planes_of(message, start, count, flag):
+    return [
+        kept(flag, message[start + 64 * d : start + 64 * (d + 1), :]).reshape(8, 8, LANES)
+        for d in range(count)
+    ]
+
+
+def choose_far(info, below1, above1, below2, above2, up, down):
+    for one, two, out, flag in ((below1, below2, up, info[1]), (above1, above2, down, info[2])):
+        first = planes_of(one, HALF, 2, flag)
+        second = planes_of(two, HALF, 1, flag)
+        out[0:64, :] = first[0].reshape(64, LANES)
+        out[64:128, :] = jnp.where(one[-8:, :] > 1.5, first[1], second[0]).reshape(64, LANES)
+
+
+def beyond(one, two, three, near, far):
+    a, b, c = planes_of(one, HALF, 4, near), planes_of(two, HALF, 3, near), planes_of(three, 0, 2, far)
+    first, second = one[-8:, :], two[-8:, :]
+    two_left = jnp.where(second > 1.5, b[1], c[0])
+    three_left = jnp.where(second > 2.5, b[2], jnp.where(second > 1.5, c[0], c[1]))
+    return (
+        a[0],
+        jnp.where(first > 1.5, a[1], b[0]),
+        jnp.where(first > 2.5, a[2], jnp.where(first > 1.5, b[0], two_left)),
+        jnp.where(
+            first > 3.5,
+            a[3],
+            jnp.where(first > 2.5, b[0], jnp.where(first > 1.5, two_left, three_left)),
+        ),
+    )
+
+
+def y_rows(message, row, count, upper):
+    value = message[row : row + count, :]
+    return ahead(value, 8) if upper else value
 
 
 def pack_z(flags, *refs):
@@ -173,8 +216,8 @@
             out[comp : comp + 1, :] = field[comp, row : row + 1, :]
         out[6:7, :] = kept(flags[1], xp[row : row + 1, :])
         out[7:8, :] = kept(flags[0], xm[row : row + 1, :])
-        out[8:9, :] = kept(flags[3], yp[row : row + 1, :])
-        out[9:10, :] = kept(flags[2], ym[row : row + 1, :])
+        out[8:9, :] = kept(flags[3], y_rows(yp, row, 1, row > 0))
+        out[9:10, :] = kept(flags[2], y_rows(ym, row, 1, row > 0))
         out[10:16, :] = jnp.zeros((6, LANES), F32)
 
 
@@ -223,26 +266,20 @@
 
 def sweep(last_sweep, flags, seg_len, field, drive, conduct, xp, xm, yp, ym, zp, zm, diagonal, solver, *rest):
     if last_sweep:
-        permute, field_out, heat_out, ext, columns, solved, matrices, sems, turned = rest
+        field_out, heat_out, ext, columns, solved = rest
     else:
-        field_out, first, last, ext, columns, solved, matrices, sems = rest
-    segs = matrices.shape[0]
-    copies = [pltpu.make_async_copy(solver.at[s], matrices.at[s], sems.at[s]) for s in range(segs)]
-    for copy in copies:
-        copy.start()
-
-    def fill(i, carry):
-        rows = pl.ds(pl.multiple_of(i * CHUNK, CHUNK), CHUNK)
-        to = pl.ds(pl.multiple_of(i * CHUNK + HALO, 8), CHUNK)
+        field_out, first, last, ext, columns, solved = rest
+    segs = solver.shape[0]
+
+    for base in range(0, CZ, CHUNK):
+        rows = slice(base, base + CHUNK)
+        to = slice(base + HALO, base + HALO + CHUNK)
         for comp in range(6):
             ext[comp, to, :] = field[comp, rows, :]
         ext[6, to, :] = kept(flags[1], xp[rows, :])
         ext[7, to, :] = kept(flags[0], xm[rows, :])
-        ext[8, to, :] = kept(flags[3], yp[rows, :])
-        ext[9, to, :] = kept(flags[2], ym[rows, :])
-        return carry
-
-    lax.fori_loop(0, CZ // CHUNK, fill, 0)
+        ext[8, to, :] = kept(flags[3], y_rows(yp, base % HALF, CHUNK, base >= HALF))
+        ext[9, to, :] = kept(flags[2], y_rows(ym, base % HALF, CHUNK, base >= HALF))
     for comp in range(10):
         ext[comp, HALO - 1 : HALO, :] = kept(flags[4], zm[comp : comp + 1, :])
         ext[comp, HALO + CZ : HALO + CZ + 1, :] = kept(flags[5], zp[comp : comp + 1, :])
@@ -268,7 +305,7 @@
                 rest_of = drive[comp, rows, :] - both[part]
                 for q in range(4):
                     at = (base + 1) * PLANE + comp * 4 + q
-                    columns[pl.ds(at, CHUNK, stride=PLANE), :] = ahead(rest_of, 32 * q)
+                    columns[pl.ds(at, CHUNK, stride=PLANE), :] = ahead(rest_of, CORNER[q])
         return carry
 
     lax.fori_loop(0, CZ // CHUNK, residual, 0)
@@ -279,8 +316,7 @@
         length = seg_len[s]
         window = columns[pl.ds(pl.multiple_of(start * PLANE, 8), 512), :]
         window = jnp.where(row_of < (length + 2) * PLANE, window, 0.0).astype(jnp.bfloat16)
-        copies[s].wait()
-        product = jnp.dot(matrices[s], window, preferred_element_type=F32)
+        product = jnp.dot(solver[s], window, preferred_element_type=F32)
         scaled = solver_scale * diagonal[:, s : s + 1] * window.astype(F32)
         result = coupling_scale * product + scaled
         to = pl.ds(pl.multiple_of(start * PLANE, 8), MAXSEG * PLANE)
@@ -296,34 +332,29 @@
             add = jnp.zeros((CHUNK, LANES), F32)
             for q in range(4):
                 piece = solved[pl.ds(base * PLANE + comp * 4 + q, CHUNK, stride=PLANE), :]
-                add = jnp.where(lane // COLS == q, ahead(piece, -32 * q), add)
-            parts.append(field[comp, rows, :] + add)
+                add = jnp.where(lane & 17 == CORNER[q], ahead(piece, -CORNER[q]), add)
+            part = field[comp, rows, :] + add
+            field_out[comp, rows, :] = part
+            parts.append(part)
         if last_sweep:
             total = parts[0] * parts[0]
             for part in parts[1:]:
                 total = total + part * part
-            heat = 0.5 * conduct[0, rows, :] * total
-            heat_out[rows, :] = jnp.dot(
-                heat, permute[...], precision=lax.Precision.HIGHEST, preferred_element_type=F32
-            )
-            for comp in range(6):
-                ext[comp, rows, :] = parts[comp]
+            heat_out[rows, :] = 0.5 * conduct[0, rows, :] * total
         else:
-            for comp in range(6):
-                field_out[comp, rows, :] = parts[comp]
             low, high = x_faces(parts)
             first[rows, :] = low
             last[rows, :] = high
         return carry
 
     lax.fori_loop(0, CZ // CHUNK, update, 0)
-    if last_sweep:
-        for comp in range(6):
-            for half in range(CZ // LANES):
-                flat = ext[comp, half * LANES : (half + 1) * LANES, :].T
-                for from_row, to_row in cell_rows(None):
-                    turned[comp % 2, half, pl.ds(to_row, 8, stride=2), :] = flat[from_row : from_row + 8]
-                field_out[comp, :, half * LANES : (half + 1) * LANES] = turned[comp % 2, half]
+
+
+def finish_field(planes, out):
+    for comp in range(6):
+        for half in range(CZ // LANES):
+            lanes = slice(half * LANES, (half + 1) * LANES)
+            out[comp, :, lanes] = planes[comp, lanes, :].T
 
 
 def pack_heat(flags, starts, heat, below, above, out, ext):
@@ -341,8 +372,8 @@
     axis = value.ndim - 2
     for k in range(3):
         step = 1 << k
-        row_bit = (row // step) % 2
-        lane_bit = (lane // (16 * step)) % 2
+        row_bit = (row >> k) & 1
+        lane_bit = (lane >> (4 + k)) & 1
         up = ahead(pltpu.roll(value, 8 - step, axis), -16 * step)
         down = up if step == 4 else ahead(pltpu.roll(value, step, axis), 16 * step)
         value = jnp.where(row_bit == lane_bit, value, jnp.where(row_bit == 0, up, down))
@@ -355,33 +386,19 @@
             out[plane, which] = swap_tiles(source[plane].reshape(4, 8, LANES))
 
 
-def choose_planes(length, round_id, slab, *refs):
-    received = refs[: 2 * (round_id - 1)]
-    up_out, down_out = refs[2 * (round_id - 1) :]
-    below, above = received[0::2], received[1::2]
-    count = length[0]
-    up_out[...] = slab[jnp.maximum(count - round_id, 0)]
-    down_out[...] = slab[round_id - 1]
-    for short in range(1, round_id):
-
-        @pl.when(count == short)
-        def _():
-            up_out[...] = below[round_id - short - 1][...]
-            down_out[...] = above[round_id - short - 1][...]
-
-
-def heat_step(slab_info, slab, b1, a1, b2, a2, b3, a3, b4, a4, arrived, factor_out, warm_out, temp, rates, joule):
-    count, low_open, high_open = slab_info[0], slab_info[1], slab_info[2]
+def heat_step(info, slab, below1, above1, below2, above2, below3, above3, arrived, factor_out, warm_out, temp, rates, joule):
+    count = info[0]
     planes = temp.shape[1]
     owners = arrived.shape[0]
     for plane in range(planes - 2 * RING):
         temp[0, plane + RING] = slab[plane, 0]
         rates[plane + RING] = slab[plane, 1]
-    for r, (below, above) in enumerate(((b1, a1), (b2, a2), (b3, a3), (b4, a4))):
-        temp[0, RING - 1 - r] = below[0]
-        rates[RING - 1 - r] = below[1]
-        temp[0, RING + count + r] = above[0]
-        rates[RING + count + r] = above[1]
+    lower = beyond(below1, below2, below3, info[1], info[3])
+    upper = beyond(above1, above2, above3, info[2], info[4])
+    for depth in range(RING):
+        for at, plane in ((RING - 1 - depth, lower[depth]), (RING + count + depth, upper[depth])):
+            temp[0, at] = plane[:4]
+            rates[at] = plane[4:]
     for owner in range(owners):
         joule[pl.ds(owners + owner, arrived.shape[1], stride=owners), :] = arrived[owner]
 
@@ -400,8 +417,8 @@
         gy_down = jnp.where(row == 0, 0.0, pltpu.roll(mid, 1, 2))
         total = ahead(jnp.where(lane < 16, gx_up, mid), 16)
         total = total + ahead(jnp.where(lane >= 112, gx_down, mid), -16)
-        total = total + jnp.where(lane % 16 == 15, ahead(gy_up, -15), ahead(mid, 1))
-        total = total + jnp.where(lane % 16 == 0, ahead(gy_down, 15), ahead(mid, -1))
+        total = total + jnp.where(lane & 15 == 15, ahead(gy_up, -15), ahead(mid, 1))
+        total = total + jnp.where(lane & 15 == 0, ahead(gy_down, 15), ahead(mid, -1))
         total = total + value[:-2] + value[2:]
         heat = joule[pl.ds(base * owners, group * owners), :].reshape(group, 4, 8, LANES)
         rate = rates[pl.ds(base, group)] * (total - 6.0 * mid) + heat
@@ -486,20 +503,19 @@
     ).astype(jnp.int32)
     my_owner = at_x * count_y + at_y
     my_length = jnp.sum(jnp.where(slab_ids == my_owner, slab_lengths, 0)).astype(jnp.int32)
-    low_open = (my_owner > 0) | (at_z > 0)
-    high_open = (my_owner < owners - 1) | (at_z < count_z - 1)
-    slab_info = jnp.stack([my_length, low_open.astype(jnp.int32), high_open.astype(jnp.int32)])
+    my_slab = at_z * owners + my_owner
+    slabs = owners * count_z
+    slab_info = jnp.stack(
+        [my_length, my_slab > 0, my_slab < slabs - 1, my_slab > 1, my_slab < slabs - 2]
+    ).astype(jnp.int32)
 
     field_bytes = 6 * CZ * LANES * 4
     plane_array = shape(CZ, LANES)
-    halves = pltpu.VMEM((6, 2, LANES, LANES), F32)
-    turned = pltpu.VMEM((2, 2, LANES, LANES), F32)
     field, face_low, face_high = pl.pallas_call(
         prepare_field,
         out_shape=(shape(6, CZ, LANES), plane_array, plane_array),
         in_specs=[VMEM],
         out_specs=[VMEM] * 3,
-        scratch_shapes=[halves, turned],
         compiler_params=params(),
         cost_estimate=cost(1 << 20, 2 * field_bytes),
         name="prepare_field",
@@ -509,7 +525,6 @@
         out_shape=(shape(6, CZ, LANES), shape(1, CZ, LANES), shape(512, segs)),
         in_specs=[VMEM] * 3,
         out_specs=[VMEM] * 3,
-        scratch_shapes=[halves, turned],
         compiler_params=params(),
         cost_estimate=cost(1 << 20, 2 * field_bytes),
         name="prepare_drive",
@@ -528,24 +543,25 @@
         name="prepare_slab",
     )(warming_amount[0, 0, 0], heat_spreading_coef[0, 0, 0])
 
-    def halo(field, face_low, face_high):
+    def halo(round_id, field, face_low, face_high, extra):
         x_plus, x_minus = turn(face_low, "gx", -1), turn(face_high, "gx", 1)
-        y_low, y_high = pl.pallas_call(
-            pack_y,
-            out_shape=(plane_array, plane_array),
-            in_specs=[SMEM] + [VMEM] * 3,
+        message = shape(HALF + 64 * (RING + 1 - round_id) + 8, LANES)
+        up, down = pl.pallas_call(
+            functools.partial(pack_y, round_id),
+            out_shape=(message, message),
+            in_specs=[SMEM] * 2 + [VMEM] * 5,
             out_specs=[VMEM] * 2,
             compiler_params=params(),
-            cost_estimate=cost(1 << 20, 2 * field_bytes),
+            cost_estimate=cost(1 << 20, field_bytes),
             name="pack_y",
-        )(flags, field, x_plus, x_minus)
-        y_plus, y_minus = turn(y_low, "gy", -1), turn(y_high, "gy", 1)
+        )(flags, slab_info, field, x_plus, x_minus, *extra)
+        y_plus, y_minus = ring(down, -1), ring(up, 1)
         sides = (x_plus, x_minus, y_plus, y_minus)
-        end = CZ // 8 - 1
         specs = []
-        for block in (0, end):
+        for block, half_block in ((0, 0), (CZ // 8 - 1, HALF // 8 - 1)):
             specs.append(pl.BlockSpec((6, 8, LANES), lambda i, block=block: (0, block, 0)))
-            specs += [pl.BlockSpec((8, LANES), lambda i, block=block: (block, 0))] * 4
+            specs += [pl.BlockSpec((8, LANES), lambda i, block=block: (block, 0))] * 2
+            specs += [pl.BlockSpec((8, LANES), lambda i, block=half_block: (block, 0))] * 2
         z_low, z_high = pl.pallas_call(
             pack_z,
             grid=(1,),
@@ -558,41 +574,23 @@
         z_plus, z_minus = turn(z_low, "gz", -1), turn(z_high, "gz", 1)
         return sides + (z_plus, z_minus)
 
+    solver = subdomain_inverse_full[0, 0, 0]
+    extra = (warming_amount[0, 0, 0], heat_spreading_coef[0, 0, 0])
     received = []
-    for round_id in range(1, RING + 1):
-        up, down = pl.pallas_call(
-            lambda length, *refs, round_id=round_id: choose_planes(length, round_id, *refs),
-            out_shape=(shape(2, 4, 8, LANES),) * 2,
-            in_specs=[SMEM] + [VMEM] * (1 + len(received)),
-            out_specs=[VMEM] * 2,
-            compiler_params=params(),
-            name="choose_planes",
-        )(slab_info, slab, *received)
-        below, above = ring(up, 1), ring(down, -1)
-        received += [jnp.where(low_open, below, 0.0), jnp.where(high_open, above, 0.0)]
-
-    solver = subdomain_inverse_full[0, 0, 0]
     for sweep_index in range(SWEEPS):
         final = sweep_index == SWEEPS - 1
-        ghosts = halo(field, face_low, face_high)
+        ghosts = halo(sweep_index + 1, field, face_low, face_high, extra)
+        extra = (ghosts[3], ghosts[2])
+        received += extra
         scratch = [
             pltpu.VMEM((10, CZ + 2 * HALO, LANES), F32),
             pltpu.VMEM(((CZ + 1 + WINDOW) * PLANE + 8, LANES), F32),
             pltpu.VMEM(((CZ + MAXSEG) * PLANE, LANES), F32),
-            pltpu.VMEM((segs, 512, 512), jnp.bfloat16),
-            pltpu.SemaphoreType.DMA((segs,)),
         ]
         inputs = [flags, seg_len, field, drive, conduct, *ghosts, diagonal, solver]
-        specs = [SMEM] * 2 + [VMEM] * 10 + [ANY]
+        specs = [SMEM] * 2 + [VMEM] * 11
         if final:
-            lane = jnp.arange(LANES, dtype=jnp.int32)
-            natural = (
-                (2 * ((lane // 8) % 4) + lane // 64) * 16 + 2 * (lane % 8) + (lane // 32) % 2
-            )
-            inputs.append((natural[:, None] == lane[None, :]).astype(F32))
-            specs.append(VMEM)
-            scratch.append(turned)
-            outs = (shape(6, LANES, CZ), plane_array)
+            outs = (shape(6, CZ, LANES), plane_array)
         else:
             outs = (shape(6, CZ, LANES), plane_array, plane_array)
         result = pl.pallas_call(
@@ -606,10 +604,29 @@
             name="sweep",
         )(*inputs)
         if final:
-            field_new, heat = result
+            field, heat = result
         else:
             field, face_low, face_high = result
 
+    field_new = pl.pallas_call(
+        finish_field,
+        out_shape=shape(6, LANES, CZ),
+        in_specs=[VMEM],
+        out_specs=VMEM,
+        compiler_params=params(),
+        cost_estimate=cost(1 << 20, 2 * field_bytes),
+        name="finish_field",
+    )(field)
+    far = shape(128, LANES)
+    far_up, far_down = pl.pallas_call(
+        choose_far,
+        out_shape=(far, far),
+        in_specs=[SMEM] + [VMEM] * 4,
+        out_specs=[VMEM] * 2,
+        compiler_params=params(),
+        name="choose_far",
+    )(slab_info, *received)
+    received += [ring(far_up, 2), ring(far_down, -2)]
     heat_above, heat_below = turn(heat[:8], "gz", -1), turn(heat[CZ - 8 :], "gz", 1)
     rows = slab_cap + 8
     outgoing = pl.pallas_call(
@@ -626,7 +643,7 @@
     factor, warm = pl.pallas_call(
         heat_step,
         out_shape=(shape(owners, slab_cap, LANES), shape(slab_cap, 4, 8, LANES)),
-        in_specs=[SMEM] + [VMEM] * 10,
+        in_specs=[SMEM] + [VMEM] * 8,
         out_specs=[VMEM] * 2,
         scratch_shapes=[
             pltpu.VMEM((2, planes, 4, 8, LANES), F32),

time: 158 us -> 137 us (0.87)
  Pallas kernels: 60.8 us -> 47.5 us
  starting transfers between devices: 61.7 us -> 49.8 us
  local copies, waits for them, and re-layouts: 10.1 us -> 12.8 us
  waiting for transfers between devices: 21.5 us -> 24.1 us
    ppermute x14 -> x10, starting transfers between devices: 27.8 us -> 12.2 us  [turn(): lax.ppermute(value, axis, [(i, (i + step) % count) for i in range(count)])]
    pallas_call x2, Pallas kernels: 33.2 us -> 19.5 us  [body(): pl.pallas_call(functools.partial(sweep, final), out_shape=outs, in_specs=...]
    ppermute x14 -> x10, waiting for transfers between devices: 5.9 us -> 11.5 us  [turn(): lax.ppermute(value, axis, [(i, (i + step) % count) for i in range(count)])]
    ppermute x8 -> x6, starting transfers between devices: 15 us -> 20.4 us  [ring(): return lax.ppermute(value, ('gx', 'gy', 'gz'), pairs)]
    all_to_all x1, starting transfers between devices: 9.09 us -> 4.17 us  [body(): lax.all_to_all(factor, ('gx', 'gy'), split_axis=0, concat_axis=0, tiled=T...]
    all_to_all x1, starting transfers between devices: 9.72 us -> 13.1 us  [body(): lax.all_to_all(outgoing, ('gx', 'gy'), split_axis=0, concat_axis=0, tiled...]
    all_to_all x1, waiting for transfers between devices: 2.51 us -> 0.01 us  [body(): lax.all_to_all(outgoing, ('gx', 'gy'), split_axis=0, concat_axis=0, tiled...]
    all_to_all x1, waiting for transfers between devices: 6.48 us -> 4.2 us  [body(): lax.all_to_all(factor, ('gx', 'gy'), split_axis=0, concat_axis=0, tiled=T...]
  transfers between devices with their start and end apart: 24 -> 18, of which waited for: 9 -> 12; matrix products, arithmetic and copies ran while one was open for 2% -> 2% of each run, Pallas kernels for 33% -> 9%
where the time goes in v1:
time: 137 us; the launch traced here: 136 us
  starting transfers between devices  49.8 us (36%)
  Pallas kernels  47.5 us (35%)
  waiting for transfers between devices  24.1 us (18%)
  local copies, waits for them, and re-layouts  12.8 us (9%)
  other arithmetic  1.41 us (1%)
    ppermute x6, starting transfers between devices, ring(): return lax.ppermute(value, ('gx', 'gy', 'gz'), pairs)  20.4 us
    pallas_call x2, Pallas kernels, body(): pl.pallas_call(functools.partial(sweep, final), out_shape=outs, in_specs=...  19.5 us
    all_to_all x1, starting transfers between devices, body(): lax.all_to_all(outgoing, ('gx', 'gy'), split_axis=0, concat_axis=0, tiled...  13.1 us
    ppermute x10, starting transfers between devices, turn(): lax.ppermute(value, axis, [(i, (i + step) % count) for i in range(count)])  12.2 us
    unnamed x30, local copies, waits for them, and re-layouts  12 us
    ppermute x10, waiting for transfers between devices, turn(): lax.ppermute(value, axis, [(i, (i + step) % count) for i in range(count)])  11.5 us
    ppermute x6, waiting for transfers between devices, ring(): return lax.ppermute(value, ('gx', 'gy', 'gz'), pairs)  8.39 us
    pallas_call x1, Pallas kernels, body(): pl.pallas_call(heat_step, out_shape=(shape(owners, slab_cap, LANES), shap...  6.95 us
  transfers between devices with their start and end apart: 18, of which 12 were waited for; matrix products, arithmetic and copies ran while one was open for 2% of the time, Pallas kernels for 9%

profile of v1, /device:TPU:1, one launch (start us, length us, event | category | flops | bytes accessed | tf_op | source)
XLA Modules:
  0.0 136.4 jit_solution(3466084391123017396)
XLA Ops:
  3.0 3.6 %collective-permute-start = (f32[256,128]{1,0:T(8,128)S(1)}, f32[256,128]{1,0:T(8,128)S(1)}, u32[]{:S(2)}, u32[]{:S(2)}) collective-permute-start(f32[256,128]{1,0:T(8,128)S(1)} %get-tuple-element.29), channel_id=1, source_target_pairs={{0,192},{64,0},{128,64},{192,128},{1,193},{65,1},{129,65},{193,129... | collective-permute-start | bytes 393224 | tf_op jit(solution)/shard_map/ppermute | solution.py:485
  8.8 2.9 %collective-permute-done.1.x_minus.refs_2_.refs_7_.xm = f32[256,128]{1,0:T(8,128)S(1)} collective-permute-done((f32[256,128]{1,0:T(8,128)S(1)}, f32[256,128]{1,0:T(8,128)S(1)}, u32[]{:S(2)}, u32[]{:S(2)}) %collective-permute-start.1) | collective-permute-done | bytes 131104 | tf_op jit(solution)/shard_map/ppermute | solution.py:485
  13.6 2.5 %pack_y.2 = (f32[392,128]{1,0:T(8,128)S(1)}, f32[392,128]{1,0:T(8,128)S(1)}) custom-call(s32[6]{0:T(128)S(1)} %convert_element_type.2.flags, s32[5]{0:T(128)S(1)} %stack.67.info.slab_info, f32[6,256,128]{2,1,0:T(8,128)S(1)} %get-tuple-element.26.field.refs_0_.refs_5_, f32[256,128]{1,0:T(8,128)S(1)} %collective-permute-done.x_plus.refs_1_.refs_6_.xp, ...), custom_call_target="tpu_custom_call" | custom-call | flops 1048576 | bytes 786432 | tf_op jit(solution)/shard_map/pack_y/pallas_call | solution.py:549
  16.2 2.2 %collective-permute-start.2 = (f32[392,128]{1,0:T(8,128)S(1)}, f32[392,128]{1,0:T(8,128)S(1)}, u32[]{:S(2)}, u32[]{:S(2)}) collective-permute-start(f32[392,128]{1,0:T(8,128)S(1)} %get-tuple-element.31), channel_id=1, source_target_pairs={{0,255},{8,0},{16,8},{24,16},{32,24},{40,32},{48,40},{56,48},{64,5... | collective-permute-start | bytes 602120 | tf_op jit(solution)/shard_map/ppermute | solution.py:493
  19.5 3.3 %collective-permute-done.2.refs_3_.refs_8_.yp.rest_1_.above1 = f32[392,128]{1,0:T(8,128)S(1)} collective-permute-done((f32[392,128]{1,0:T(8,128)S(1)}, f32[392,128]{1,0:T(8,128)S(1)}, u32[]{:S(2)}, u32[]{:S(2)}) %collective-permute-start.2) | collective-permute-done | bytes 200736 | tf_op jit(solution)/shard_map/ppermute | solution.py:493
  22.8 2.8 %collective-permute-done.3.refs_4_.refs_9_.ym.rest_0_.below1 = f32[392,128]{1,0:T(8,128)S(1)} collective-permute-done((f32[392,128]{1,0:T(8,128)S(1)}, f32[392,128]{1,0:T(8,128)S(1)}, u32[]{:S(2)}, u32[]{:S(2)}) %collective-permute-start.3) | collective-permute-done | bytes 200736 | tf_op jit(solution)/shard_map/ppermute | solution.py:493
  26.2 2.8 %collective-permute-start.4 = (f32[16,128]{1,0:T(8,128)S(1)}, f32[16,128]{1,0:T(8,128)S(1)}, u32[]{:S(2)}, u32[]{:S(2)}) collective-permute-start(f32[16,128]{1,0:T(8,128)S(1)} %get-tuple-element.33), channel_id=1, source_target_pairs={{0,7},{1,0},{2,1},{3,2},{4,3},{5,4},{6,5},{7,6},{8,15},{9,8},{10,9... | collective-permute-start | bytes 24584 | tf_op jit(solution)/shard_map/ppermute | solution.py:485
  33.1 3.4 %copy-done = bf16[1,1,1,16,512,512]{5,4,3,2,1,0:T(8,128)(2,1)S(1)} copy-done((bf16[1,1,1,16,512,512]{5,4,3,2,1,0:T(8,128)(2,1)S(1)}, bf16[1,1,1,16,512,512]{5,4,3,2,1,0:T(8,128)(2,1)}, u32[]{:S(2)}) %copy-start) | copy-done | bytes 8388632
  37.1 10.0 %sweep.2 = (f32[6,256,128]{2,1,0:T(8,128)S(1)}, f32[256,128]{1,0:T(8,128)S(1)}, f32[256,128]{1,0:T(8,128)S(1)}) custom-call(s32[6]{0:T(128)S(1)} %convert_element_type.2.flags, s32[16]{0:T(128)S(1)} %bitcast.36, f32[6,256,128]{2,1,0:T(8,128)S(1)} %get-tuple-element.26.field.refs_0_.refs_5_, f32[6,256,128]{2,1,0:T(8,128)S(1)} %get-tuple-element.27.drive, ...), custom_call_target="tpu_custom_call" | custom-call | flops 268435456 | bytes 3145728 | tf_op jit(solution)/shard_map/sweep/pallas_call | solution.py:596
  47.2 1.5 %collective-permute-start.7 = (f32[256,128]{1,0:T(8,128)S(1)}, f32[256,128]{1,0:T(8,128)S(1)}, u32[]{:S(2)}, u32[]{:S(2)}) collective-permute-start(f32[256,128]{1,0:T(8,128)S(1)} %get-tuple-element.38), channel_id=1, source_target_pairs={{0,64},{64,128},{128,192},{192,0},{1,65},{65,129},{129,193},{193,1... | collective-permute-start | bytes 393224 | tf_op jit(solution)/shard_map/ppermute | solution.py:485
  48.7 2.4 %collective-permute-done.6.x_plus.refs_1_.refs_6_.xp = f32[256,128]{1,0:T(8,128)S(1)} collective-permute-done((f32[256,128]{1,0:T(8,128)S(1)}, f32[256,128]{1,0:T(8,128)S(1)}, u32[]{:S(2)}, u32[]{:S(2)}) %collective-permute-start.6) | collective-permute-done | bytes 131104 | tf_op jit(solution)/shard_map/ppermute | solution.py:485
  53.7 9.3 %collective-permute-start.8 = (f32[328,128]{1,0:T(8,128)S(1)}, f32[328,128]{1,0:T(8,128)S(1)}, u32[]{:S(2)}, u32[]{:S(2)}) collective-permute-start(f32[328,128]{1,0:T(8,128)S(1)} %get-tuple-element.39), channel_id=1, source_target_pairs={{0,255},{8,0},{16,8},{24,16},{32,24},{40,32},{48,40},{56,48},{64,5... | collective-permute-start | bytes 503816 | tf_op jit(solution)/shard_map/ppermute | solution.py:493
  68.4 2.2 %collective-permute-done.11.zm = f32[16,128]{1,0:T(8,128)S(1)} collective-permute-done((f32[16,128]{1,0:T(8,128)S(1)}, f32[16,128]{1,0:T(8,128)S(1)}, u32[]{:S(2)}, u32[]{:S(2)}) %collective-permute-start.11) | collective-permute-done | bytes 8224 | tf_op jit(solution)/shard_map/ppermute | solution.py:485
  70.7 9.5 %sweep.3 = (f32[6,256,128]{2,1,0:T(8,128)S(1)}, f32[256,128]{1,0:T(8,128)S(1)}) custom-call(s32[6]{0:T(128)S(1)} %convert_element_type.2.flags, s32[16]{0:T(128)S(1)} %bitcast.37, f32[6,256,128]{2,1,0:T(8,128)S(1)} %get-tuple-element.36.field.refs_0_.refs_5_, f32[6,256,128]{2,1,0:T(8,128)S(1)} %get-tuple-element.27.drive, ...), custom_call_target="tpu_custom_call" | custom-call | flops 268435456 | bytes 3145728 | tf_op jit(solution)/shard_map/sweep/pallas_call | solution.py:596
  81.1 2.7 %collective-permute-start.15 = (f32[8,128]{1,0:T(8,128)S(1)}, f32[8,128]{1,0:T(8,128)S(1)}, u32[]{:S(2)}, u32[]{:S(2)}) collective-permute-start(f32[8,128]{1,0:T(8,128)S(1)} %get-tuple-element.49), channel_id=1, source_target_pairs={{0,7},{1,0},{2,1},{3,2},{4,3},{5,4},{6,5},{7,6},{8,15},{9,8},{10,9... | collective-permute-start | bytes 12296 | tf_op jit(solution)/shard_map/ppermute | solution.py:485
  84.7 1.4 %pack_heat.1 = f32[32,32,128]{2,1,0:T(8,128)} custom-call(s32[6]{0:T(128)S(1)} %convert_element_type.2.flags, s32[32]{0:T(128)S(1)} %select_reduce_fusion.starts, f32[256,128]{1,0:T(8,128)S(1)} %get-tuple-element.46.heat, f32[8,128]{1,0:T(8,128)S(1)} %collective-permute-done.14.below, f32[8,128]{1,0:T(8,128)S(1)} %collective-permute-done.15.above), custom_call_target="tpu_custom_call" | custom-call | tf_op jit(solution)/shard_map/pack_heat/pallas_call | solution.py:632
  86.1 13.1 %all-to-all-start = ((f32[32,32,128]{2,1,0:T(8,128)}), f32[32,32,128]{2,1,0:T(8,128)S(1)}, u32[]{:S(2)}, u32[]{:S(2)}) async-start(f32[32,32,128]{2,1,0:T(8,128)} %pack_heat.1), calls=%async_computation | async-start | bytes 1048576 | tf_op jit(solution)/shard_map/all_to_all | solution.py:641
  99.8 1.5 %collective-permute-start.12 = (f32[128,128]{1,0:T(8,128)S(1)}, f32[128,128]{1,0:T(8,128)S(1)}, u32[]{:S(2)}, u32[]{:S(2)}) collective-permute-start(f32[128,128]{1,0:T(8,128)S(1)} %get-tuple-element.44), channel_id=1, source_target_pairs={{0,16},{8,24},{16,32},{24,40},{32,48},{40,56},{48,64},{56,72},{64,... | collective-permute-start | bytes 196616 | tf_op jit(solution)/shard_map/ppermute | solution.py:493
  101.3 6.3 %collective-permute-start.13 = (f32[128,128]{1,0:T(8,128)S(1)}, f32[128,128]{1,0:T(8,128)S(1)}, u32[]{:S(2)}, u32[]{:S(2)}) collective-permute-start(f32[128,128]{1,0:T(8,128)S(1)} %get-tuple-element.45), channel_id=1, source_target_pairs={{0,247},{8,255},{16,0},{24,8},{32,16},{40,24},{48,32},{56,40},{64,... | collective-permute-start | bytes 196616 | tf_op jit(solution)/shard_map/ppermute | solution.py:493
  107.5 6.1 %prepare_slab.1.slab = f32[24,2,4,8,128]{4,3,2,1,0:T(8,128)S(1)} custom-call(f32[24,32,128]{2,1,0:T(8,128)S(1)} %bitcast.28, f32[24,32,128]{2,1,0:T(8,128)S(1)} %bitcast.30), custom_call_target="tpu_custom_call" | custom-call | flops 1048576 | bytes 1572864 | tf_op jit(solution)/shard_map/prepare_slab/pallas_call | solution.py:536
  113.7 6.9 %heat_step.1 = (f32[32,24,128]{2,1,0:T(8,128)}, f32[24,4,8,128]{3,2,1,0:T(8,128)S(1)}) custom-call(s32[5]{0:T(128)S(1)} %stack.67.info.slab_info, f32[24,2,4,8,128]{4,3,2,1,0:T(8,128)S(1)} %prepare_slab.1.slab, f32[392,128]{1,0:T(8,128)S(1)} %collective-permute-done.3.refs_4_.refs_9_.ym.rest_0_.below1, ...), custom_call_target="tpu_custom_call" | custom-call | tf_op jit(solution)/shard_map/heat_step/pallas_call | solution.py:643
  120.6 4.2 %all-to-all-start.1 = ((f32[32,24,128]{2,1,0:T(8,128)}), f32[32,24,128]{2,1,0:T(8,128)S(1)}, u32[]{:S(2)}, u32[]{:S(2)}) async-start(f32[32,24,128]{2,1,0:T(8,128)} %get-tuple-element.48), calls=%async_computation.1 | async-start | bytes 786432 | tf_op jit(solution)/shard_map/all_to_all | solution.py:656
  127.1 3.8 %finish_slab.1 = f32[24,32,128]{2,1,0:T(8,128)} custom-call(s32[5]{0:T(128)S(1)} %stack.67.info.slab_info, f32[24,4,8,128]{3,2,1,0:T(8,128)S(1)} %get-tuple-element.47.warm), custom_call_target="tpu_custom_call" | custom-call | tf_op jit(solution)/shard_map/finish_slab/pallas_call | solution.py:657
  130.9 4.2 %all-to-all-done.1.returned = f32[32,24,128]{2,1,0:T(8,128)S(1)} async-done(((f32[32,24,128]{2,1,0:T(8,128)}), f32[32,24,128]{2,1,0:T(8,128)S(1)}, u32[]{:S(2)}, u32[]{:S(2)}) %all-to-all-start.1) | async-done | bytes 393248 | tf_op jit(solution)/shard_map/all_to_all | solution.py:656
  (63 shorter events, 27.2 us)
Async XLA Ops:
  3.0 5.8 %collective-permute-start = (f32[256,128]{1,0:T(8,128)S(1)}, f32[256,128]{1,0:T(8,128)S(1)}, u32[]{:S(2)}, u32[]{:S(2)}) collective-permute-start(f32[256,128]{1,0:T(8,128)S(1)} %get-tuple-element.29), channel_id=1, source_target_pairs={{0,192},{64,0},{128,64},{192,128},{1,193},{65,1},{129,65},{193,129... | collective-permute-start | bytes 393224 | tf_op jit(solution)/shard_map/ppermute | solution.py:485
  6.6 5.0 %collective-permute-start.1 = (f32[256,128]{1,0:T(8,128)S(1)}, f32[256,128]{1,0:T(8,128)S(1)}, u32[]{:S(2)}, u32[]{:S(2)}) collective-permute-start(f32[256,128]{1,0:T(8,128)S(1)} %get-tuple-element.30), channel_id=1, source_target_pairs={{0,64},{64,128},{128,192},{192,0},{1,65},{65,129},{129,193},{193,1... | collective-permute-start | bytes 393224 | tf_op jit(solution)/shard_map/ppermute | solution.py:485
  16.2 6.7 %collective-permute-start.2 = (f32[392,128]{1,0:T(8,128)S(1)}, f32[392,128]{1,0:T(8,128)S(1)}, u32[]{:S(2)}, u32[]{:S(2)}) collective-permute-start(f32[392,128]{1,0:T(8,128)S(1)} %get-tuple-element.31), channel_id=1, source_target_pairs={{0,255},{8,0},{16,8},{24,16},{32,24},{40,32},{48,40},{56,48},{64,5... | collective-permute-start | bytes 602120 | tf_op jit(solution)/shard_map/ppermute | solution.py:493
  18.3 7.3 %collective-permute-start.3 = (f32[392,128]{1,0:T(8,128)S(1)}, f32[392,128]{1,0:T(8,128)S(1)}, u32[]{:S(2)}, u32[]{:S(2)}) collective-permute-start(f32[392,128]{1,0:T(8,128)S(1)} %get-tuple-element.32), channel_id=1, source_target_pairs={{0,8},{8,16},{16,24},{24,32},{32,40},{40,48},{48,56},{56,64},{64,7... | collective-permute-start | bytes 602120 | tf_op jit(solution)/shard_map/ppermute | solution.py:493
  26.2 6.0 %collective-permute-start.4 = (f32[16,128]{1,0:T(8,128)S(1)}, f32[16,128]{1,0:T(8,128)S(1)}, u32[]{:S(2)}, u32[]{:S(2)}) collective-permute-start(f32[16,128]{1,0:T(8,128)S(1)} %get-tuple-element.33), channel_id=1, source_target_pairs={{0,7},{1,0},{2,1},{3,2},{4,3},{5,4},{6,5},{7,6},{8,15},{9,8},{10,9... | collective-permute-start | bytes 24584 | tf_op jit(solution)/shard_map/ppermute | solution.py:485
  29.1 4.0 %collective-permute-start.5 = (f32[16,128]{1,0:T(8,128)S(1)}, f32[16,128]{1,0:T(8,128)S(1)}, u32[]{:S(2)}, u32[]{:S(2)}) collective-permute-start(f32[16,128]{1,0:T(8,128)S(1)} %get-tuple-element.34), channel_id=1, source_target_pairs={{0,1},{1,2},{2,3},{3,4},{4,5},{5,6},{6,7},{7,0},{8,9},{9,10},{10,1... | collective-permute-start | bytes 24584 | tf_op jit(solution)/shard_map/ppermute | solution.py:485
  33.1 3.4 %copy-start = (bf16[1,1,1,16,512,512]{5,4,3,2,1,0:T(8,128)(2,1)S(1)}, bf16[1,1,1,16,512,512]{5,4,3,2,1,0:T(8,128)(2,1)}, u32[]{:S(2)}) copy-start(bf16[1,1,1,16,512,512]{5,4,3,2,1,0:T(8,128)(2,1)} %param.12) | copy-start | bytes 25165828
  37.1 33.6 %copy-start.1 = (bf16[1,1,1,16,512,512]{5,4,3,2,1,0:T(8,128)(2,1)S(1)}, bf16[1,1,1,16,512,512]{5,4,3,2,1,0:T(8,128)(2,1)}, u32[]{:S(2)}) copy-start(bf16[1,1,1,16,512,512]{5,4,3,2,1,0:T(8,128)(2,1)} %param.12) | copy-start | bytes 25165828
  47.1 36.6 %copy-start.14 = (s32[1,32]{1,0:T(1,128)S(1)}, s32[1,32]{1,0:T(1,128)}, u32[]{:S(2)}) copy-start(s32[1,32]{1,0:T(1,128)} %param.15) | copy-start | bytes 388
  47.2 3.9 %collective-permute-start.6 = (f32[256,128]{1,0:T(8,128)S(1)}, f32[256,128]{1,0:T(8,128)S(1)}, u32[]{:S(2)}, u32[]{:S(2)}) collective-permute-start(f32[256,128]{1,0:T(8,128)S(1)} %get-tuple-element.37), channel_id=1, source_target_pairs={{0,192},{64,0},{128,64},{192,128},{1,193},{65,1},{129,65},{193,129... | collective-permute-start | bytes 393224 | tf_op jit(solution)/shard_map/ppermute | solution.py:485
  47.2 5.1 %collective-permute-start.7 = (f32[256,128]{1,0:T(8,128)S(1)}, f32[256,128]{1,0:T(8,128)S(1)}, u32[]{:S(2)}, u32[]{:S(2)}) collective-permute-start(f32[256,128]{1,0:T(8,128)S(1)} %get-tuple-element.38), channel_id=1, source_target_pairs={{0,64},{64,128},{128,192},{192,0},{1,65},{65,129},{129,193},{193,1... | collective-permute-start | bytes 393224 | tf_op jit(solution)/shard_map/ppermute | solution.py:485
  53.7 53.8 %copy-start.3 = (f32[1,1,1,24,32,128]{5,4,3,2,1,0:T(8,128)S(1)}, f32[1,1,1,24,32,128]{5,4,3,2,1,0:T(8,128)}, u32[]{:S(2)}) copy-start(f32[1,1,1,24,32,128]{5,4,3,2,1,0:T(8,128)} %param.16) | copy-start | bytes 1179652
  53.7 53.8 %copy-start.5 = (f32[1,1,1,24,32,128]{5,4,3,2,1,0:T(8,128)S(1)}, f32[1,1,1,24,32,128]{5,4,3,2,1,0:T(8,128)}, u32[]{:S(2)}) copy-start(f32[1,1,1,24,32,128]{5,4,3,2,1,0:T(8,128)} %param.17) | copy-start | bytes 1179652
  53.7 10.3 %collective-permute-start.8 = (f32[328,128]{1,0:T(8,128)S(1)}, f32[328,128]{1,0:T(8,128)S(1)}, u32[]{:S(2)}, u32[]{:S(2)}) collective-permute-start(f32[328,128]{1,0:T(8,128)S(1)} %get-tuple-element.39), channel_id=1, source_target_pairs={{0,255},{8,0},{16,8},{24,16},{32,24},{40,32},{48,40},{56,48},{64,5... | collective-permute-start | bytes 503816 | tf_op jit(solution)/shard_map/ppermute | solution.py:493
  63.0 2.3 %collective-permute-start.9 = (f32[328,128]{1,0:T(8,128)S(1)}, f32[328,128]{1,0:T(8,128)S(1)}, u32[]{:S(2)}, u32[]{:S(2)}) collective-permute-start(f32[328,128]{1,0:T(8,128)S(1)} %get-tuple-element.40), channel_id=1, source_target_pairs={{0,8},{8,16},{16,24},{24,32},{32,40},{40,48},{48,56},{56,64},{64,7... | collective-permute-start | bytes 503816 | tf_op jit(solution)/shard_map/ppermute | solution.py:493
  65.9 2.5 %collective-permute-start.10 = (f32[16,128]{1,0:T(8,128)S(1)}, f32[16,128]{1,0:T(8,128)S(1)}, u32[]{:S(2)}, u32[]{:S(2)}) collective-permute-start(f32[16,128]{1,0:T(8,128)S(1)} %get-tuple-element.41), channel_id=1, source_target_pairs={{0,7},{1,0},{2,1},{3,2},{4,3},{5,4},{6,5},{7,6},{8,15},{9,8},{10,9... | collective-permute-start | bytes 24584 | tf_op jit(solution)/shard_map/ppermute | solution.py:485
  67.0 68.2 %copy-start.11 = (f32[8,16,256]{2,1,0:T(8,128)S(1)}, f32[8,16,256]{2,1,0:T(8,128)}, u32[]{:S(2)}) copy-start(f32[8,16,256]{2,1,0:T(8,128)} %param.11) | copy-start | bytes 393220
  67.0 3.7 %collective-permute-start.11 = (f32[16,128]{1,0:T(8,128)S(1)}, f32[16,128]{1,0:T(8,128)S(1)}, u32[]{:S(2)}, u32[]{:S(2)}) collective-permute-start(f32[16,128]{1,0:T(8,128)S(1)} %get-tuple-element.42), channel_id=1, source_target_pairs={{0,1},{1,2},{2,3},{3,4},{4,5},{5,6},{6,7},{7,0},{8,9},{9,10},{10,1... | collective-permute-start | bytes 24584 | tf_op jit(solution)/shard_map/ppermute | solution.py:485
  81.1 3.7 %collective-permute-start.14 = (f32[8,128]{1,0:T(8,128)S(1)}, f32[8,128]{1,0:T(8,128)S(1)}, u32[]{:S(2)}, u32[]{:S(2)}) collective-permute-start(f32[8,128]{1,0:T(8,128)S(1)} %get-tuple-element.50), channel_id=1, source_target_pairs={{0,1},{1,2},{2,3},{3,4},{4,5},{5,6},{6,7},{7,0},{8,9},{9,10},{10,1... | collective-permute-start | bytes 12296 | tf_op jit(solution)/shard_map/ppermute | solution.py:485
  81.1 3.7 %collective-permute-start.15 = (f32[8,128]{1,0:T(8,128)S(1)}, f32[8,128]{1,0:T(8,128)S(1)}, u32[]{:S(2)}, u32[]{:S(2)}) collective-permute-start(f32[8,128]{1,0:T(8,128)S(1)} %get-tuple-element.49), channel_id=1, source_target_pairs={{0,7},{1,0},{2,1},{3,2},{4,3},{5,4},{6,5},{7,6},{8,15},{9,8},{10,9... | collective-permute-start | bytes 12296 | tf_op jit(solution)/shard_map/ppermute | solution.py:485
  86.1 27.6 %all-to-all-start = ((f32[32,32,128]{2,1,0:T(8,128)}), f32[32,32,128]{2,1,0:T(8,128)S(1)}, u32[]{:S(2)}, u32[]{:S(2)}) async-start(f32[32,32,128]{2,1,0:T(8,128)} %pack_heat.1), calls=%async_computation | async-start | bytes 1048576 | tf_op jit(solution)/shard_map/all_to_all | solution.py:641
  99.8 13.9 %collective-permute-start.12 = (f32[128,128]{1,0:T(8,128)S(1)}, f32[128,128]{1,0:T(8,128)S(1)}, u32[]{:S(2)}, u32[]{:S(2)}) collective-permute-start(f32[128,128]{1,0:T(8,128)S(1)} %get-tuple-element.44), channel_id=1, source_target_pairs={{0,16},{8,24},{16,32},{24,40},{32,48},{40,56},{48,64},{56,72},{64,... | collective-permute-start | bytes 196616 | tf_op jit(solution)/shard_map/ppermute | solution.py:493
  101.3 12.4 %collective-permute-start.13 = (f32[128,128]{1,0:T(8,128)S(1)}, f32[128,128]{1,0:T(8,128)S(1)}, u32[]{:S(2)}, u32[]{:S(2)}) collective-permute-start(f32[128,128]{1,0:T(8,128)S(1)} %get-tuple-element.45), channel_id=1, source_target_pairs={{0,247},{8,255},{16,0},{24,8},{32,16},{40,24},{48,32},{56,40},{64,... | collective-permute-start | bytes 196616 | tf_op jit(solution)/shard_map/ppermute | solution.py:493
  120.6 14.5 %all-to-all-start.1 = ((f32[32,24,128]{2,1,0:T(8,128)}), f32[32,24,128]{2,1,0:T(8,128)S(1)}, u32[]{:S(2)}, u32[]{:S(2)}) async-start(f32[32,24,128]{2,1,0:T(8,128)} %get-tuple-element.48), calls=%async_computation.1 | async-start | bytes 786432 | tf_op jit(solution)/shard_map/all_to_all | solution.py:656
  (9 other events, 8.6 us)

commit v2 on v1

--- a/solution.py
+++ b/solution.py
@@ -28,9 +28,12 @@
 X_BITS, Y_BITS = 112, 15
 RING = SECTIONS
 HALF = CZ // 2
+N_X, N_Y, N_Z = 4, 8, 8
+OWNERS = N_X * N_Y
 CORNER = (0, 1, 16, 17)
 VMEM = pl.BlockSpec(memory_space=pltpu.VMEM)
 SMEM = pl.BlockSpec(memory_space=pltpu.SMEM)
+HBM = pl.BlockSpec(memory_space=pltpu.HBM)
 
 
 def params(mib=24):
@@ -102,15 +105,35 @@
     return first, last
 
 
+def sides(place):
+    x, y, z = place[0], place[1], place[2]
+    return x > 0, x < N_X - 1, y > 0, y < N_Y - 1, z > 0, z < N_Z - 1
+
+
+def own_slab(place):
+    owner = place[0] * N_Y + place[1]
+    slab = place[2] * OWNERS + owner
+    last = OWNERS * N_Z - 1
+    return owner, (slab > 0, slab < last, slab > 1, slab < last - 1)
+
+
+def kept(flag, value):
+    return jnp.where(flag, value, jnp.zeros_like(value))
+
+
 def to_planes(source, index, target):
     for half in range(CZ // LANES):
         lanes = slice(half * LANES, (half + 1) * LANES)
         target[index, lanes, :] = source[index, :, lanes].T
 
 
-def prepare_field(field, planes, first, last):
+def prepare_field(field, planes, first, last, loaded, sems):
+    copies = [pltpu.make_async_copy(field.at[c], loaded.at[c], sems.at[c]) for c in range(6)]
+    for copy in copies:
+        copy.start()
     for comp in range(6):
-        to_planes(field, comp, planes)
+        copies[comp].wait()
+        to_planes(loaded, comp, planes)
 
     def chunk(i, carry):
         rows = pl.ds(pl.multiple_of(i * CHUNK, CHUNK), CHUNK)
@@ -122,23 +145,43 @@
     lax.fori_loop(0, CZ // CHUNK, chunk, 0)
 
 
-def prepare_drive(drive, conduct, diagonal, drive_planes, conduct_planes, diagonal_turned):
+def prepare_rest(
+    drive, conduct, diagonal, warm, rates, solver,
+    drive_planes, conduct_planes, diagonal_turned, slab, solver_here,
+    drive_in, conduct_in, diagonal_in, slab_in, sems,
+):
+    copies = [pltpu.make_async_copy(warm, slab_in.at[0], sems.at[0])]
+    copies.append(pltpu.make_async_copy(rates, slab_in.at[1], sems.at[1]))
+    copies.append(pltpu.make_async_copy(drive, drive_in, sems.at[2]))
+    copies.append(pltpu.make_async_copy(conduct, conduct_in, sems.at[3]))
+    copies.append(pltpu.make_async_copy(diagonal, diagonal_in, sems.at[4]))
+    parts = 4
+    size = solver.shape[0] // parts
+    for part in range(parts):
+        at = pl.ds(part * size, size)
+        copies.append(pltpu.make_async_copy(solver.at[at], solver_here.at[at], sems.at[5 + part]))
+    for copy in copies:
+        copy.start()
+    batch = 4
+    for which in range(2):
+        copies[which].wait()
+        for base in range(0, slab.shape[0], batch):
+            value = slab_in[which, base : base + batch].reshape(4 * batch, 8, LANES)
+            slab[base : base + batch, which] = swap_tiles(value).reshape(batch, 4, 8, LANES)
+    for copy in copies[2:5]:
+        copy.wait()
     for comp in range(6):
-        to_planes(drive, comp, drive_planes)
-    to_planes(conduct, 0, conduct_planes)
-    diagonal_turned[...] = diagonal[...].T
-
-
-def kept(flag, value):
-    return jnp.where(flag > 0, value, jnp.zeros_like(value))
-
-
-def tiled(plane):
-    return swap_tiles(plane.reshape(4, 8, LANES)).reshape(32, LANES)
-
-
-def pack_y(round_id, flags, info, field, x_plus, x_minus, *rest):
+        to_planes(drive_in, comp, drive_planes)
+    to_planes(conduct_in, 0, conduct_planes)
+    diagonal_turned[...] = diagonal_in[...].T
+    for copy in copies[5:]:
+        copy.wait()
+
+
+def pack_y(round_id, place, lookup, field, x_plus, x_minus, *rest):
     up, down = rest[-2:]
+    flags = sides(place)
+    owner, near = own_slab(place)
 
     def chunk(i, carry):
         parts = []
@@ -154,20 +197,20 @@
 
     lax.fori_loop(0, HALF // CHUNK, chunk, 0)
     if round_id == 1:
+        slab = rest[0]
         for depth in range(RING):
-            top = jnp.maximum(info[0] - 1 - depth, 0)
-            for which in range(2):
-                at = HALF + 64 * depth + 32 * which
-                up[at : at + 32, :] = tiled(rest[which][top])
-                down[at : at + 32, :] = tiled(rest[which][depth])
-        count = jnp.full((8, LANES), info[0], jnp.int32).astype(F32)
+            top = jnp.maximum(lookup[owner] - 1 - depth, 0)
+            at = slice(HALF + 64 * depth, HALF + 64 * (depth + 1))
+            up[at, :] = slab[top].reshape(64, LANES)
+            down[at, :] = slab[depth].reshape(64, LANES)
+        count = jnp.full((8, LANES), lookup[owner], jnp.int32).astype(F32)
         up[-8:, :] = count
         down[-8:, :] = count
     else:
         below, above = rest[:2]
         size = 64 * (RING - 1)
-        up[HALF : HALF + size, :] = kept(info[1], below[HALF : HALF + size, :])
-        down[HALF : HALF + size, :] = kept(info[2], above[HALF : HALF + size, :])
+        up[HALF : HALF + size, :] = kept(near[0], below[HALF : HALF + size, :])
+        down[HALF : HALF + size, :] = kept(near[1], above[HALF : HALF + size, :])
         up[-8:, :] = below[-8:, :]
         down[-8:, :] = above[-8:, :]
 
@@ -179,8 +222,9 @@
     ]
 
 
-def choose_far(info, below1, above1, below2, above2, up, down):
-    for one, two, out, flag in ((below1, below2, up, info[1]), (above1, above2, down, info[2])):
+def choose_far(place, below1, above1, below2, above2, up, down):
+    near = own_slab(place)[1]
+    for one, two, out, flag in ((below1, below2, up, near[0]), (above1, above2, down, near[1])):
         first = planes_of(one, HALF, 2, flag)
         second = planes_of(two, HALF, 1, flag)
         out[0:64, :] = first[0].reshape(64, LANES)
@@ -209,7 +253,8 @@
     return ahead(value, 8) if upper else value
 
 
-def pack_z(flags, *refs):
+def pack_z(place, *refs):
+    flags = sides(place)
     lows, highs, (first, last) = refs[:5], refs[5:10], refs[10:]
     for (field, xp, xm, yp, ym), row, out in ((lows, 0, first), (highs, 7, last)):
         for comp in range(6):
@@ -264,12 +309,13 @@
     return (kx, ky, kz), (ex0, ey0, ez0)
 
 
-def sweep(last_sweep, flags, seg_len, field, drive, conduct, xp, xm, yp, ym, zp, zm, diagonal, solver, *rest):
+def sweep(last_sweep, place, seg_len, field, drive, conduct, xp, xm, yp, ym, zp, zm, diagonal, solver, *rest):
     if last_sweep:
         field_out, heat_out, ext, columns, solved = rest
     else:
         field_out, first, last, ext, columns, solved = rest
     segs = solver.shape[0]
+    flags = sides(place)
 
     for base in range(0, CZ, CHUNK):
         rows = slice(base, base + CHUNK)
@@ -357,13 +403,16 @@
             out[comp, :, lanes] = planes[comp, lanes, :].T
 
 
-def pack_heat(flags, starts, heat, below, above, out, ext):
+def pack_heat(place, lookup, heat, below, above, out, ext):
+    flags = sides(place)
     ext[0:8, :] = kept(flags[4], below[...])
     ext[8 : 8 + CZ, :] = heat[...]
     ext[8 + CZ : 16 + CZ, :] = kept(flags[5], above[...])
     ext[16 + CZ :, :] = jnp.zeros((ext.shape[0] - 16 - CZ, LANES), F32)
+    start = 8 - (RING - 1)
     for owner in range(out.shape[0]):
-        out[owner] = ext[pl.ds(starts[owner] + 8 - (RING - 1), out.shape[1]), :]
+        out[owner] = ext[pl.ds(start, out.shape[1]), :]
+        start = start + lookup[owner]
 
 
 def swap_tiles(value):
@@ -380,21 +429,16 @@
     return value
 
 
-def prepare_slab(warm, rates, out):
-    for plane in range(out.shape[0]):
-        for which, source in enumerate((warm, rates)):
-            out[plane, which] = swap_tiles(source[plane].reshape(4, 8, LANES))
-
-
-def heat_step(info, slab, below1, above1, below2, above2, below3, above3, arrived, factor_out, warm_out, temp, rates, joule):
-    count = info[0]
+def heat_step(place, lookup, slab, below1, above1, below2, above2, below3, above3, arrived, factor_out, warm_out, temp, rates, joule):
+    owner, near = own_slab(place)
+    count = lookup[owner]
     planes = temp.shape[1]
     owners = arrived.shape[0]
     for plane in range(planes - 2 * RING):
         temp[0, plane + RING] = slab[plane, 0]
         rates[plane + RING] = slab[plane, 1]
-    lower = beyond(below1, below2, below3, info[1], info[3])
-    upper = beyond(above1, above2, above3, info[2], info[4])
+    lower = beyond(below1, below2, below3, near[0], near[2])
+    upper = beyond(above1, above2, above3, near[1], near[3])
     for depth in range(RING):
         for at, plane in ((RING - 1 - depth, lower[depth]), (RING + count + depth, upper[depth])):
             temp[0, at] = plane[:4]
@@ -402,7 +446,7 @@
     for owner in range(owners):
         joule[pl.ds(owners + owner, arrived.shape[1], stride=owners), :] = arrived[owner]
 
-    group = 6
+    group = 2
     section = time_step / (SECTIONS * SECTIONS)
 
     def one(step, now, before, base):
@@ -432,10 +476,11 @@
         now, before = (step - 1) % 2, step % 2
 
         def loop(g, carry):
-            one(step, now, before, 1 + g * group)
+            one(step, now, before, step + g * group)
             return carry
 
-        lax.fori_loop(0, (planes - 2) // group, loop, 0)
+        trips = (planes - 2 * step) // group
+        lax.fori_loop(0, trips, loop, 0, unroll={15: 5, 14: 7, 13: 13, 12: 6}[trips])
     final = SECTIONS % 2
     for plane in range(warm_out.shape[0]):
         result = temp[final, plane + RING]
@@ -445,15 +490,21 @@
         factor_out[owner] = joule[pl.ds(owner, factor_out.shape[1], stride=owners), :]
 
 
-def finish_slab(slab_info, warm, out):
-    count = slab_info[0]
-    for plane in range(out.shape[0]):
-        out[plane] = kept(count - plane, swap_tiles(warm[plane])).reshape(32, LANES)
-
-
-def finish_conduct(starts, returned, conduct, out, rows):
+def finish_slab(place, lookup, warm, out):
+    count = lookup[own_slab(place)[0]]
+    batch = 4
+    for base in range(0, out.shape[0], batch):
+        value = swap_tiles(warm[base : base + batch].reshape(4 * batch, 8, LANES))
+        value = value.reshape(batch, 32, LANES)
+        for plane in range(batch):
+            out[base + plane] = kept(count > base + plane, value[plane])
+
+
+def finish_conduct(lookup, returned, conduct, out, rows):
+    start = 0
     for owner in range(returned.shape[0]):
-        rows[pl.ds(starts[owner], returned.shape[1]), :] = returned[owner]
+        rows[pl.ds(start, returned.shape[1]), :] = returned[owner]
+        start = start + lookup[owner]
     for half in range(CZ // LANES):
         lanes = slice(half * LANES, (half + 1) * LANES)
         out[:, lanes] = conduct[:, lanes] * rows[half * LANES : (half + 1) * LANES, :].T
@@ -475,7 +526,6 @@
     heat_spreading_coef,
 ):
     count_x, count_y, count_z = (lax.axis_size(axis) for axis in ("gx", "gy", "gz"))
-    at_x, at_y, at_z = (lax.axis_index(axis) for axis in ("gx", "gy", "gz"))
     owners = count_x * count_y
     segs = subdomain_layer_counts.shape[3]
     slab_cap = warming_amount.shape[3]
@@ -492,71 +542,70 @@
         pairs = [(device(i), device((i + step) % total)) for i in range(total)]
         return lax.ppermute(value, ("gx", "gy", "gz"), pairs)
 
-    flags = jnp.stack(
-        [at_x > 0, at_x < count_x - 1, at_y > 0, at_y < count_y - 1, at_z > 0, at_z < count_z - 1]
-    ).astype(jnp.int32)
+    place = jnp.stack([lax.axis_index(axis) for axis in ("gx", "gy", "gz")]).astype(jnp.int32)
     seg_len = subdomain_layer_counts[0, 0, 0]
-    slab_lengths = heat_layer_lookup[0]
-    slab_ids = jnp.arange(owners, dtype=jnp.int32)
-    starts = jnp.sum(
-        jnp.where(slab_ids[None, :] < slab_ids[:, None], slab_lengths[None, :], 0), axis=1
-    ).astype(jnp.int32)
-    my_owner = at_x * count_y + at_y
-    my_length = jnp.sum(jnp.where(slab_ids == my_owner, slab_lengths, 0)).astype(jnp.int32)
-    my_slab = at_z * owners + my_owner
-    slabs = owners * count_z
-    slab_info = jnp.stack(
-        [my_length, my_slab > 0, my_slab < slabs - 1, my_slab > 1, my_slab < slabs - 2]
-    ).astype(jnp.int32)
+    lookup = heat_layer_lookup[0]
 
     field_bytes = 6 * CZ * LANES * 4
     plane_array = shape(CZ, LANES)
     field, face_low, face_high = pl.pallas_call(
         prepare_field,
         out_shape=(shape(6, CZ, LANES), plane_array, plane_array),
-        in_specs=[VMEM],
+        in_specs=[HBM],
         out_specs=[VMEM] * 3,
+        scratch_shapes=[pltpu.VMEM((6, LANES, CZ), F32), pltpu.SemaphoreType.DMA((6,))],
         compiler_params=params(),
         cost_estimate=cost(1 << 20, 2 * field_bytes),
         name="prepare_field",
     )(earlier_edge_voltage.reshape(6, LANES, CZ))
-    drive, conduct, diagonal = pl.pallas_call(
-        prepare_drive,
-        out_shape=(shape(6, CZ, LANES), shape(1, CZ, LANES), shape(512, segs)),
-        in_specs=[VMEM] * 3,
-        out_specs=[VMEM] * 3,
+    x_ghosts = turn(face_low, "gx", -1), turn(face_high, "gx", 1)
+    solver = subdomain_inverse_full[0, 0, 0]
+    drive, conduct, diagonal, slab, solver = pl.pallas_call(
+        prepare_rest,
+        out_shape=(
+            shape(6, CZ, LANES),
+            shape(1, CZ, LANES),
+            shape(512, segs),
+            shape(slab_cap, 2, 4, 8, LANES),
+            jax.ShapeDtypeStruct(solver.shape, solver.dtype),
+        ),
+        in_specs=[HBM] * 6,
+        out_specs=[VMEM] * 5,
+        scratch_shapes=[
+            pltpu.VMEM((6, LANES, CZ), F32),
+            pltpu.VMEM((1, LANES, CZ), F32),
+            pltpu.VMEM((segs, 512), F32),
+            pltpu.VMEM((2, slab_cap, 32, LANES), F32),
+            pltpu.SemaphoreType.DMA((9,)),
+        ],
         compiler_params=params(),
-        cost_estimate=cost(1 << 20, 2 * field_bytes),
-        name="prepare_drive",
+        cost_estimate=cost(1 << 20, 16 * field_bytes),
+        name="prepare_rest",
     )(
         coil_drive_current.reshape(6, LANES, CZ),
         sigma_omega_cellwise.reshape(1, LANES, CZ),
         subdomain_inverse_main[0, 0, 0],
+        warming_amount[0, 0, 0],
+        heat_spreading_coef[0, 0, 0],
+        solver,
     )
-    slab = pl.pallas_call(
-        prepare_slab,
-        out_shape=shape(slab_cap, 2, 4, 8, LANES),
-        in_specs=[VMEM] * 2,
-        out_specs=VMEM,
-        compiler_params=params(),
-        cost_estimate=cost(1 << 20, 2 * field_bytes),
-        name="prepare_slab",
-    )(warming_amount[0, 0, 0], heat_spreading_coef[0, 0, 0])
-
-    def halo(round_id, field, face_low, face_high, extra):
-        x_plus, x_minus = turn(face_low, "gx", -1), turn(face_high, "gx", 1)
+    x_ghosts, drive, conduct, diagonal, slab, solver = lax.optimization_barrier(
+        (x_ghosts, drive, conduct, diagonal, slab, solver)
+    )
+
+    def halo(round_id, field, x_plus, x_minus, extra):
         message = shape(HALF + 64 * (RING + 1 - round_id) + 8, LANES)
         up, down = pl.pallas_call(
             functools.partial(pack_y, round_id),
             out_shape=(message, message),
-            in_specs=[SMEM] * 2 + [VMEM] * 5,
+            in_specs=[SMEM] * 2 + [VMEM] * (3 + len(extra)),
             out_specs=[VMEM] * 2,
             compiler_params=params(),
             cost_estimate=cost(1 << 20, field_bytes),
             name="pack_y",
-        )(flags, slab_info, field, x_plus, x_minus, *extra)
+        )(place, lookup, field, x_plus, x_minus, *extra)
         y_plus, y_minus = ring(down, -1), ring(up, 1)
-        sides = (x_plus, x_minus, y_plus, y_minus)
+        ghosts = (x_plus, x_minus, y_plus, y_minus)
         specs = []
         for block, half_block in ((0, 0), (CZ // 8 - 1, HALF // 8 - 1)):
             specs.append(pl.BlockSpec((6, 8, LANES), lambda i, block=block: (0, block, 0)))
@@ -570,16 +619,15 @@
             out_specs=[pl.BlockSpec((16, LANES), lambda i: (0, 0))] * 2,
             compiler_params=params(),
             name="pack_z",
-        )(flags, field, *sides, field, *sides)
+        )(place, field, *ghosts, field, *ghosts)
         z_plus, z_minus = turn(z_low, "gz", -1), turn(z_high, "gz", 1)
-        return sides + (z_plus, z_minus)
-
-    solver = subdomain_inverse_full[0, 0, 0]
-    extra = (warming_amount[0, 0, 0], heat_spreading_coef[0, 0, 0])
+        return ghosts + (z_plus, z_minus)
+
+    extra = (slab,)
     received = []
     for sweep_index in range(SWEEPS):
         final = sweep_index == SWEEPS - 1
-        ghosts = halo(sweep_index + 1, field, face_low, face_high, extra)
+        ghosts = halo(sweep_index + 1, field, *x_ghosts, extra)
         extra = (ghosts[3], ghosts[2])
         received += extra
         scratch = [
@@ -587,7 +635,7 @@
             pltpu.VMEM(((CZ + 1 + WINDOW) * PLANE + 8, LANES), F32),
             pltpu.VMEM(((CZ + MAXSEG) * PLANE, LANES), F32),
         ]
-        inputs = [flags, seg_len, field, drive, conduct, *ghosts, diagonal, solver]
+        inputs = [place, seg_len, field, drive, conduct, *ghosts, diagonal, solver]
         specs = [SMEM] * 2 + [VMEM] * 11
         if final:
             outs = (shape(6, CZ, LANES), plane_array)
@@ -607,6 +655,7 @@
             field, heat = result
         else:
             field, face_low, face_high = result
+            x_ghosts = turn(face_low, "gx", -1), turn(face_high, "gx", 1)
 
     field_new = pl.pallas_call(
         finish_field,
@@ -625,9 +674,13 @@
         out_specs=[VMEM] * 2,
         compiler_params=params(),
         name="choose_far",
-    )(slab_info, *received)
+    )(place, *received)
     received += [ring(far_up, 2), ring(far_down, -2)]
     heat_above, heat_below = turn(heat[:8], "gz", -1), turn(heat[CZ - 8 :], "gz", 1)
+    heat_above, heat_below, field_new, *far_planes = lax.optimization_barrier(
+        (heat_above, heat_below, field_new, *received[-2:])
+    )
+    received[-2:] = far_planes
     rows = slab_cap + 8
     outgoing = pl.pallas_call(
         pack_heat,
@@ -637,13 +690,13 @@
         scratch_shapes=[pltpu.VMEM((CZ + 16 + rows, LANES), F32)],
         compiler_params=params(),
         name="pack_heat",
-    )(flags, starts, heat, heat_below, heat_above)
+    )(place, lookup, heat, heat_below, heat_above)
     arrived = lax.all_to_all(outgoing, ("gx", "gy"), split_axis=0, concat_axis=0, tiled=True)
     planes = slab_cap + 2 * RING
     factor, warm = pl.pallas_call(
         heat_step,
         out_shape=(shape(owners, slab_cap, LANES), shape(slab_cap, 4, 8, LANES)),
-        in_specs=[SMEM] + [VMEM] * 8,
+        in_specs=[SMEM] * 2 + [VMEM] * 8,
         out_specs=[VMEM] * 2,
         scratch_shapes=[
             pltpu.VMEM((2, planes, 4, 8, LANES), F32),
@@ -652,16 +705,16 @@
         ],
         compiler_params=params(),
         name="heat_step",
-    )(slab_info, slab, *received, arrived)
+    )(place, lookup, slab, *received, arrived)
     returned = lax.all_to_all(factor, ("gx", "gy"), split_axis=0, concat_axis=0, tiled=True)
     renewed_heat_rise = pl.pallas_call(
         finish_slab,
         out_shape=shape(slab_cap, 32, LANES),
-        in_specs=[SMEM, VMEM],
+        in_specs=[SMEM, SMEM, VMEM],
         out_specs=VMEM,
         compiler_params=params(),
         name="finish_slab",
-    )(slab_info, warm)
+    )(place, lookup, warm)
     renewed_sigma_omega = pl.pallas_call(
         finish_conduct,
         out_shape=shape(LANES, CZ),
@@ -670,7 +723,7 @@
         scratch_shapes=[pltpu.VMEM((CZ + slab_cap, LANES), F32)],
         compiler_params=params(),
         name="finish_conduct",
-    )(starts, returned, sigma_omega_cellwise.reshape(LANES, CZ))
+    )(lookup, returned, sigma_omega_cellwise.reshape(LANES, CZ))
     return (
         field_new.reshape(6, CX, CY, CZ),
         renewed_heat_rise[None, None, None],

time: 137 us -> 138 us (level)
  blocking collectives: 0 us -> 22.5 us
  starting transfers between devices: 49.8 us -> 36.2 us
  Pallas kernels: 47.5 us -> 41.4 us
  waiting for transfers between devices: 24.1 us -> 27.6 us
  local copies, waits for them, and re-layouts: 12.8 us -> 9.32 us
    all_to_all x0 -> x1, blocking collectives: none -> 22.5 us  [body(): lax.all_to_all(outgoing, ('gx', 'gy'), split_axis=0, concat_axis=0, tiled...]
    all_to_all x1 -> x0, starting transfers between devices: 13.1 us -> none  [body(): lax.all_to_all(outgoing, ('gx', 'gy'), split_axis=0, concat_axis=0, tiled...]
    all_to_all x1, waiting for transfers between devices: 4.2 us -> 7.92 us  [body(): lax.all_to_all(factor, ('gx', 'gy'), split_axis=0, concat_axis=0, tiled=T...]
    ppermute x10, waiting for transfers between devices: 11.5 us -> 8.01 us  [turn(): lax.ppermute(value, axis, [(i, (i + step) % count) for i in range(count)])]
    ppermute x6, waiting for transfers between devices: 8.39 us -> 11.7 us  [ring(): return lax.ppermute(value, ('gx', 'gy', 'gz'), pairs)]
    pallas_call x2 -> x1, Pallas kernels: 6.48 us -> 3.79 us  [body(): pl.pallas_call(prepare_rest, out_shape=(shape(6, CZ, LANES), shape(1, CZ,...]
    unnamed x30 -> x20, local copies, waits for them, and re-layouts: 12 us -> 9.32 us
    pallas_call x1, Pallas kernels: 3.8 us -> 2.36 us  [body(): pl.pallas_call(finish_slab, out_shape=shape(slab_cap, 32, LANES), in_spec...]
  transfers between devices with their start and end apart: 18 -> 17, of which waited for: 12 -> 9; matrix products, arithmetic and copies ran while one was open for 2% -> 0% of each run, Pallas kernels for 9% -> 13%
where the time goes in v2:
time: 138 us
  Pallas kernels  41.4 us (30%)
  starting transfers between devices  36.2 us (26%)
  waiting for transfers between devices  27.6 us (20%)
  blocking collectives  22.5 us (16%)
  local copies, waits for them, and re-layouts  9.32 us (7%)
    all_to_all x1, blocking collectives, body(): lax.all_to_all(outgoing, ('gx', 'gy'), split_axis=0, concat_axis=0, tiled...  22.5 us
    ppermute x6, starting transfers between devices, ring(): return lax.ppermute(value, ('gx', 'gy', 'gz'), pairs)  21 us
    pallas_call x2, Pallas kernels, body(): pl.pallas_call(functools.partial(sweep, final), out_shape=outs, in_specs=...  19.6 us
    ppermute x6, waiting for transfers between devices, ring(): return lax.ppermute(value, ('gx', 'gy', 'gz'), pairs)  11.7 us
    ppermute x10, starting transfers between devices, turn(): lax.ppermute(value, axis, [(i, (i + step) % count) for i in range(count)])  11.2 us
    unnamed x20, local copies, waits for them, and re-layouts  9.32 us
    ppermute x10, waiting for transfers between devices, turn(): lax.ppermute(value, axis, [(i, (i + step) % count) for i in range(count)])  8.01 us
    all_to_all x1, waiting for transfers between devices, body(): lax.all_to_all(factor, ('gx', 'gy'), split_axis=0, concat_axis=0, tiled=T...  7.92 us
  transfers between devices with their start and end apart: 17, of which 9 were waited for; matrix products, arithmetic and copies ran while one was open for 0% of the time, Pallas kernels for 13%

profile of v2, /device:TPU:1, one launch (start us, length us, event | category | flops | bytes accessed | tf_op | source)
XLA Modules:
  0.0 137.9 jit_solution(14628664533939611149)
XLA Ops:
  1.8 2.6 %prepare_field.1 = (f32[6,256,128]{2,1,0:T(8,128)S(1)}, f32[256,128]{1,0:T(8,128)S(1)}, f32[256,128]{1,0:T(8,128)S(1)}) custom-call(f32[6,128,256]{2,1,0:T(8,128)S(1)} %bitcast.18), custom_call_target="tpu_custom_call" | custom-call | flops 1048576 | bytes 1572864 | tf_op jit(solution)/shard_map/prepare_field/pallas_call | solution.py:551
  4.4 3.6 %collective-permute-start = (f32[256,128]{1,0:T(8,128)S(1)}, f32[256,128]{1,0:T(8,128)S(1)}, u32[]{:S(2)}, u32[]{:S(2)}) collective-permute-start(f32[256,128]{1,0:T(8,128)S(1)} %get-tuple-element.41), channel_id=1, source_target_pairs={{0,192},{64,0},{128,64},{192,128},{1,193},{65,1},{129,65},{193,129... | collective-permute-start | bytes 393224 | tf_op jit(solution)/shard_map/ppermute | solution.py:535
  8.0 3.4 %copy-done = bf16[1,1,1,16,512,512]{5,4,3,2,1,0:T(8,128)(2,1)S(1)} copy-done((bf16[1,1,1,16,512,512]{5,4,3,2,1,0:T(8,128)(2,1)S(1)}, bf16[1,1,1,16,512,512]{5,4,3,2,1,0:T(8,128)(2,1)}, u32[]{:S(2)}) %copy-start) | copy-done | bytes 8388632
  16.2 3.8 %prepare_rest.1 = (f32[6,256,128]{2,1,0:T(8,128)S(1)}, f32[1,256,128]{2,1,0:T(8,128)S(1)}, f32[512,16]{1,0:T(8,128)S(1)}, f32[24,2,4,8,128]{4,3,2,1,0:T(8,128)S(1)}, bf16[16,512,512]{2,1,0:T(8,128)(2,1)S(1)}) custom-call(f32[6,128,256]{2,1,0:T(8,128)S(1)} %bitcast.17, f32[1,128,256]{2,1,0:T(8,128)S(1)} %bitcast.19, f32[16,512]{1,0:T(8,128)S(1)} %bitcast.23, ...), custom_call_target="tpu_custom_call" | custom-call | flops 1048576 | bytes 12582912 | tf_op jit(solution)/shard_map/prepare_rest/pallas_call | solution.py:563
  20.1 1.3 pack_y.2
  21.4 1.8 %collective-permute-start.2 = (f32[392,128]{1,0:T(8,128)S(1)}, f32[392,128]{1,0:T(8,128)S(1)}, u32[]{:S(2)}, u32[]{:S(2)}) collective-permute-start(f32[392,128]{1,0:T(8,128)S(1)} %get-tuple-element.53), channel_id=1, source_target_pairs={{0,255},{8,0},{16,8},{24,16},{32,24},{40,32},{48,40},{56,48},{64,5... | collective-permute-start | bytes 602120 | tf_op jit(solution)/shard_map/ppermute | solution.py:543
  23.6 3.3 %collective-permute-done.2.refs_3_.refs_8_.yp.rest_1_.above1 = f32[392,128]{1,0:T(8,128)S(1)} collective-permute-done((f32[392,128]{1,0:T(8,128)S(1)}, f32[392,128]{1,0:T(8,128)S(1)}, u32[]{:S(2)}, u32[]{:S(2)}) %collective-permute-start.2) | collective-permute-done | bytes 200736 | tf_op jit(solution)/shard_map/ppermute | solution.py:543
  27.0 6.0 %collective-permute-done.3.refs_4_.refs_9_.ym.rest_0_.below1 = f32[392,128]{1,0:T(8,128)S(1)} collective-permute-done((f32[392,128]{1,0:T(8,128)S(1)}, f32[392,128]{1,0:T(8,128)S(1)}, u32[]{:S(2)}, u32[]{:S(2)}) %collective-permute-start.3) | collective-permute-done | bytes 200736 | tf_op jit(solution)/shard_map/ppermute | solution.py:543
  36.1 1.9 %collective-permute-done.5.zm = f32[16,128]{1,0:T(8,128)S(1)} collective-permute-done((f32[16,128]{1,0:T(8,128)S(1)}, f32[16,128]{1,0:T(8,128)S(1)}, u32[]{:S(2)}, u32[]{:S(2)}) %collective-permute-start.5) | collective-permute-done | bytes 8224 | tf_op jit(solution)/shard_map/ppermute | solution.py:535
  38.1 10.0 %sweep.2 = (f32[6,256,128]{2,1,0:T(8,128)S(1)}, f32[256,128]{1,0:T(8,128)S(1)}, f32[256,128]{1,0:T(8,128)S(1)}) custom-call(s32[3]{0:T(128)S(1)} %pad_add_fusion.place, s32[16]{0:T(128)S(1)} %bitcast.30, f32[6,256,128]{2,1,0:T(8,128)S(1)} %get-tuple-element.40.field.refs_0_.refs_5_, f32[6,256,128]{2,1,0:T(8,128)S(1)} %get-tuple-element.48.drive, ...), custom_call_target="tpu_custom_call" | custom-call | flops 268435456 | bytes 3145728 | tf_op jit(solution)/shard_map/sweep/pallas_call | solution.py:644
  48.1 1.8 %collective-permute-start.6 = (f32[256,128]{1,0:T(8,128)S(1)}, f32[256,128]{1,0:T(8,128)S(1)}, u32[]{:S(2)}, u32[]{:S(2)}) collective-permute-start(f32[256,128]{1,0:T(8,128)S(1)} %get-tuple-element.60), channel_id=1, source_target_pairs={{0,192},{64,0},{128,64},{192,128},{1,193},{65,1},{129,65},{193,129... | collective-permute-start | bytes 393224 | tf_op jit(solution)/shard_map/ppermute | solution.py:535
  49.9 2.1 %collective-permute-done.6.x_plus.refs_1_.refs_6_.xp = f32[256,128]{1,0:T(8,128)S(1)} collective-permute-done((f32[256,128]{1,0:T(8,128)S(1)}, f32[256,128]{1,0:T(8,128)S(1)}, u32[]{:S(2)}, u32[]{:S(2)}) %collective-permute-start.6) | collective-permute-done | bytes 131104 | tf_op jit(solution)/shard_map/ppermute | solution.py:535
  52.0 2.9 %collective-permute-done.7.x_minus.refs_2_.refs_7_.xm = f32[256,128]{1,0:T(8,128)S(1)} collective-permute-done((f32[256,128]{1,0:T(8,128)S(1)}, f32[256,128]{1,0:T(8,128)S(1)}, u32[]{:S(2)}, u32[]{:S(2)}) %collective-permute-start.7) | collective-permute-done | bytes 131104 | tf_op jit(solution)/shard_map/ppermute | solution.py:535
  55.0 1.3 pack_y.3
  56.3 9.9 %collective-permute-start.8 = (f32[328,128]{1,0:T(8,128)S(1)}, f32[328,128]{1,0:T(8,128)S(1)}, u32[]{:S(2)}, u32[]{:S(2)}) collective-permute-start(f32[328,128]{1,0:T(8,128)S(1)} %get-tuple-element.62), channel_id=1, source_target_pairs={{0,255},{8,0},{16,8},{24,16},{32,24},{40,32},{48,40},{56,48},{64,5... | collective-permute-start | bytes 503816 | tf_op jit(solution)/shard_map/ppermute | solution.py:543
  69.2 1.5 %collective-permute-start.11 = (f32[16,128]{1,0:T(8,128)S(1)}, f32[16,128]{1,0:T(8,128)S(1)}, u32[]{:S(2)}, u32[]{:S(2)}) collective-permute-start(f32[16,128]{1,0:T(8,128)S(1)} %get-tuple-element.65), channel_id=1, source_target_pairs={{0,1},{1,2},{2,3},{3,4},{4,5},{5,6},{6,7},{7,0},{8,9},{9,10},{10,1... | collective-permute-start | bytes 24584 | tf_op jit(solution)/shard_map/ppermute | solution.py:535
  71.3 8.8 %collective-permute-start.15 = (f32[128,128]{1,0:T(8,128)S(1)}, f32[128,128]{1,0:T(8,128)S(1)}, u32[]{:S(2)}, u32[]{:S(2)}) collective-permute-start(f32[128,128]{1,0:T(8,128)S(1)} %get-tuple-element.69), channel_id=1, source_target_pairs={{0,247},{8,255},{16,0},{24,8},{32,16},{40,24},{48,32},{56,40},{64,... | collective-permute-start | bytes 196616 | tf_op jit(solution)/shard_map/ppermute | solution.py:543
  80.2 9.5 %sweep.3 = (f32[6,256,128]{2,1,0:T(8,128)S(1)}, f32[256,128]{1,0:T(8,128)S(1)}) custom-call(s32[3]{0:T(128)S(1)} %pad_add_fusion.place, s32[16]{0:T(128)S(1)} %bitcast.31, f32[6,256,128]{2,1,0:T(8,128)S(1)} %get-tuple-element.59.field.refs_0_.refs_5_, f32[6,256,128]{2,1,0:T(8,128)S(1)} %get-tuple-element.48.drive, ...), custom_call_target="tpu_custom_call" | custom-call | flops 268435456 | bytes 3145728 | tf_op jit(solution)/shard_map/sweep/pallas_call | solution.py:644
  89.8 2.7 %collective-permute-start.12 = (f32[8,128]{1,0:T(8,128)S(1)}, f32[8,128]{1,0:T(8,128)S(1)}, u32[]{:S(2)}, u32[]{:S(2)}) collective-permute-start(f32[8,128]{1,0:T(8,128)S(1)} %get-tuple-element.78), channel_id=1, source_target_pairs={{0,7},{1,0},{2,1},{3,2},{4,3},{5,4},{6,5},{7,6},{8,15},{9,8},{10,9... | collective-permute-start | bytes 12296 | tf_op jit(solution)/shard_map/ppermute | solution.py:535
  94.2 22.5 %all_to_all.10.arrived = f32[32,32,128]{2,1,0:T(8,128)S(1)} all-to-all(f32[32,32,128]{2,1,0:T(8,128)S(1)} %pack_heat.1), channel_id=1, replica_groups=mesh['gx'=4,'gy'=8,'gz'=8] {'gx','gy'}, dimensions={0} | all-to-all | bytes 1048576 | tf_op jit(solution)/shard_map/all_to_all | solution.py:694
  116.7 5.6 %heat_step.1 = (f32[32,24,128]{2,1,0:T(8,128)}, f32[24,4,8,128]{3,2,1,0:T(8,128)S(1)}) custom-call(s32[3]{0:T(128)S(1)} %pad_add_fusion.place, s32[32]{0:T(128)S(1)} %bitcast.27, f32[24,2,4,8,128]{4,3,2,1,0:T(8,128)S(1)} %get-tuple-element.52.rest_0_.slab, f32[392,128]{1,0:T(8,128)S(1)} %collective-permute-done.3.refs_4_.refs_9_.ym.rest_0_.below1, ...), custom_call_target="tpu_custom_call" | custom-call | tf_op jit(solution)/shard_map/heat_step/pallas_call | solution.py:696
  122.3 4.0 %all-to-all-start.1 = ((f32[32,24,128]{2,1,0:T(8,128)}), f32[32,24,128]{2,1,0:T(8,128)S(1)}, u32[]{:S(2)}, u32[]{:S(2)}) async-start(f32[32,24,128]{2,1,0:T(8,128)} %get-tuple-element.76), calls=%async_computation.1 | async-start | bytes 786432 | tf_op jit(solution)/shard_map/all_to_all | solution.py:709
  126.3 2.4 %finish_slab.1 = f32[24,32,128]{2,1,0:T(8,128)} custom-call(s32[3]{0:T(128)S(1)} %pad_add_fusion.place, s32[32]{0:T(128)S(1)} %bitcast.28, f32[24,4,8,128]{3,2,1,0:T(8,128)S(1)} %get-tuple-element.75.warm), custom_call_target="tpu_custom_call" | custom-call | tf_op jit(solution)/shard_map/finish_slab/pallas_call | solution.py:710
  128.6 7.9 %all-to-all-done.1.returned = f32[32,24,128]{2,1,0:T(8,128)S(1)} async-done(((f32[32,24,128]{2,1,0:T(8,128)}), f32[32,24,128]{2,1,0:T(8,128)S(1)}, u32[]{:S(2)}, u32[]{:S(2)}) %all-to-all-start.1) | async-done | bytes 393248 | tf_op jit(solution)/shard_map/all_to_all | solution.py:709
  (47 shorter events, 16.4 us)
Async XLA Ops:
  0.6 19.4 %copy-start.8 = (s32[1,32]{1,0:T(1,128)S(1)}, s32[1,32]{1,0:T(1,128)}, u32[]{:S(2)}) copy-start(s32[1,32]{1,0:T(1,128)} %param.15) | copy-start | bytes 388
  0.6 37.4 %copy-start.9 = (s32[1,1,1,16]{3,2,1,0:T(1,128)S(1)}, s32[1,1,1,16]{3,2,1,0:T(1,128)}, u32[]{:S(2)}) copy-start(s32[1,1,1,16]{3,2,1,0:T(1,128)} %param.14) | copy-start | bytes 196
  0.7 1.1 copy-start.2
  4.4 15.7 %collective-permute-start = (f32[256,128]{1,0:T(8,128)S(1)}, f32[256,128]{1,0:T(8,128)S(1)}, u32[]{:S(2)}, u32[]{:S(2)}) collective-permute-start(f32[256,128]{1,0:T(8,128)S(1)} %get-tuple-element.41), channel_id=1, source_target_pairs={{0,192},{64,0},{128,64},{192,128},{1,193},{65,1},{129,65},{193,129... | collective-permute-start | bytes 393224 | tf_op jit(solution)/shard_map/ppermute | solution.py:535
  8.0 12.1 %collective-permute-start.1 = (f32[256,128]{1,0:T(8,128)S(1)}, f32[256,128]{1,0:T(8,128)S(1)}, u32[]{:S(2)}, u32[]{:S(2)}) collective-permute-start(f32[256,128]{1,0:T(8,128)S(1)} %get-tuple-element.42), channel_id=1, source_target_pairs={{0,64},{64,128},{128,192},{192,0},{1,65},{65,129},{129,193},{193,1... | collective-permute-start | bytes 393224 | tf_op jit(solution)/shard_map/ppermute | solution.py:535
  8.0 3.4 %copy-start = (bf16[1,1,1,16,512,512]{5,4,3,2,1,0:T(8,128)(2,1)S(1)}, bf16[1,1,1,16,512,512]{5,4,3,2,1,0:T(8,128)(2,1)}, u32[]{:S(2)}) copy-start(bf16[1,1,1,16,512,512]{5,4,3,2,1,0:T(8,128)(2,1)} %param.12) | copy-start | bytes 25165828
  11.4 1.1 copy-start.1
  13.4 1.0 copy-start.5
  21.4 5.5 %collective-permute-start.2 = (f32[392,128]{1,0:T(8,128)S(1)}, f32[392,128]{1,0:T(8,128)S(1)}, u32[]{:S(2)}, u32[]{:S(2)}) collective-permute-start(f32[392,128]{1,0:T(8,128)S(1)} %get-tuple-element.53), channel_id=1, source_target_pairs={{0,255},{8,0},{16,8},{24,16},{32,24},{40,32},{48,40},{56,48},{64,5... | collective-permute-start | bytes 602120 | tf_op jit(solution)/shard_map/ppermute | solution.py:543
  23.2 9.8 %collective-permute-start.3 = (f32[392,128]{1,0:T(8,128)S(1)}, f32[392,128]{1,0:T(8,128)S(1)}, u32[]{:S(2)}, u32[]{:S(2)}) collective-permute-start(f32[392,128]{1,0:T(8,128)S(1)} %get-tuple-element.54), channel_id=1, source_target_pairs={{0,8},{8,16},{16,24},{24,32},{32,40},{40,48},{48,56},{56,64},{64,7... | collective-permute-start | bytes 602120 | tf_op jit(solution)/shard_map/ppermute | solution.py:543
  33.6 2.5 %collective-permute-start.4 = (f32[16,128]{1,0:T(8,128)S(1)}, f32[16,128]{1,0:T(8,128)S(1)}, u32[]{:S(2)}, u32[]{:S(2)}) collective-permute-start(f32[16,128]{1,0:T(8,128)S(1)} %get-tuple-element.55), channel_id=1, source_target_pairs={{0,7},{1,0},{2,1},{3,2},{4,3},{5,4},{6,5},{7,6},{8,15},{9,8},{10,9... | collective-permute-start | bytes 24584 | tf_op jit(solution)/shard_map/ppermute | solution.py:535
  34.4 3.7 %collective-permute-start.5 = (f32[16,128]{1,0:T(8,128)S(1)}, f32[16,128]{1,0:T(8,128)S(1)}, u32[]{:S(2)}, u32[]{:S(2)}) collective-permute-start(f32[16,128]{1,0:T(8,128)S(1)} %get-tuple-element.56), channel_id=1, source_target_pairs={{0,1},{1,2},{2,3},{3,4},{4,5},{5,6},{6,7},{7,0},{8,9},{9,10},{10,1... | collective-permute-start | bytes 24584 | tf_op jit(solution)/shard_map/ppermute | solution.py:535
  48.1 3.9 %collective-permute-start.6 = (f32[256,128]{1,0:T(8,128)S(1)}, f32[256,128]{1,0:T(8,128)S(1)}, u32[]{:S(2)}, u32[]{:S(2)}) collective-permute-start(f32[256,128]{1,0:T(8,128)S(1)} %get-tuple-element.60), channel_id=1, source_target_pairs={{0,192},{64,0},{128,64},{192,128},{1,193},{65,1},{129,65},{193,129... | collective-permute-start | bytes 393224 | tf_op jit(solution)/shard_map/ppermute | solution.py:535
  49.9 5.0 %collective-permute-start.7 = (f32[256,128]{1,0:T(8,128)S(1)}, f32[256,128]{1,0:T(8,128)S(1)}, u32[]{:S(2)}, u32[]{:S(2)}) collective-permute-start(f32[256,128]{1,0:T(8,128)S(1)} %get-tuple-element.61), channel_id=1, source_target_pairs={{0,64},{64,128},{128,192},{192,0},{1,65},{65,129},{129,193},{193,1... | collective-permute-start | bytes 393224 | tf_op jit(solution)/shard_map/ppermute | solution.py:535
  56.3 11.0 %collective-permute-start.8 = (f32[328,128]{1,0:T(8,128)S(1)}, f32[328,128]{1,0:T(8,128)S(1)}, u32[]{:S(2)}, u32[]{:S(2)}) collective-permute-start(f32[328,128]{1,0:T(8,128)S(1)} %get-tuple-element.62), channel_id=1, source_target_pairs={{0,255},{8,0},{16,8},{24,16},{32,24},{40,32},{48,40},{56,48},{64,5... | collective-permute-start | bytes 503816 | tf_op jit(solution)/shard_map/ppermute | solution.py:543
  66.2 2.3 %collective-permute-start.9 = (f32[328,128]{1,0:T(8,128)S(1)}, f32[328,128]{1,0:T(8,128)S(1)}, u32[]{:S(2)}, u32[]{:S(2)}) collective-permute-start(f32[328,128]{1,0:T(8,128)S(1)} %get-tuple-element.63), channel_id=1, source_target_pairs={{0,8},{8,16},{16,24},{24,32},{32,40},{40,48},{48,56},{56,64},{64,7... | collective-permute-start | bytes 503816 | tf_op jit(solution)/shard_map/ppermute | solution.py:543
  69.2 11.0 %collective-permute-start.10 = (f32[16,128]{1,0:T(8,128)S(1)}, f32[16,128]{1,0:T(8,128)S(1)}, u32[]{:S(2)}, u32[]{:S(2)}) collective-permute-start(f32[16,128]{1,0:T(8,128)S(1)} %get-tuple-element.64), channel_id=1, source_target_pairs={{0,7},{1,0},{2,1},{3,2},{4,3},{5,4},{6,5},{7,6},{8,15},{9,8},{10,9... | collective-permute-start | bytes 24584 | tf_op jit(solution)/shard_map/ppermute | solution.py:535
  69.2 10.9 %collective-permute-start.11 = (f32[16,128]{1,0:T(8,128)S(1)}, f32[16,128]{1,0:T(8,128)S(1)}, u32[]{:S(2)}, u32[]{:S(2)}) collective-permute-start(f32[16,128]{1,0:T(8,128)S(1)} %get-tuple-element.65), channel_id=1, source_target_pairs={{0,1},{1,2},{2,3},{3,4},{4,5},{5,6},{6,7},{7,0},{8,9},{9,10},{10,1... | collective-permute-start | bytes 24584 | tf_op jit(solution)/shard_map/ppermute | solution.py:535
  71.2 22.4 %collective-permute-start.14 = (f32[128,128]{1,0:T(8,128)S(1)}, f32[128,128]{1,0:T(8,128)S(1)}, u32[]{:S(2)}, u32[]{:S(2)}) collective-permute-start(f32[128,128]{1,0:T(8,128)S(1)} %get-tuple-element.68), channel_id=1, source_target_pairs={{0,16},{8,24},{16,32},{24,40},{32,48},{40,56},{48,64},{56,72},{64,... | collective-permute-start | bytes 196616 | tf_op jit(solution)/shard_map/ppermute | solution.py:543
  71.3 65.2 %copy-start.4 = (f32[8,16,256]{2,1,0:T(8,128)S(1)}, f32[8,16,256]{2,1,0:T(8,128)}, u32[]{:S(2)}) copy-start(f32[8,16,256]{2,1,0:T(8,128)} %param.11) | copy-start | bytes 393220
  71.3 22.3 %collective-permute-start.15 = (f32[128,128]{1,0:T(8,128)S(1)}, f32[128,128]{1,0:T(8,128)S(1)}, u32[]{:S(2)}, u32[]{:S(2)}) collective-permute-start(f32[128,128]{1,0:T(8,128)S(1)} %get-tuple-element.69), channel_id=1, source_target_pairs={{0,247},{8,255},{16,0},{24,8},{32,16},{40,24},{48,32},{56,40},{64,... | collective-permute-start | bytes 196616 | tf_op jit(solution)/shard_map/ppermute | solution.py:543
  89.7 3.9 %collective-permute-start.13 = (f32[8,128]{1,0:T(8,128)S(1)}, f32[8,128]{1,0:T(8,128)S(1)}, u32[]{:S(2)}, u32[]{:S(2)}) collective-permute-start(f32[8,128]{1,0:T(8,128)S(1)} %get-tuple-element.77), channel_id=1, source_target_pairs={{0,1},{1,2},{2,3},{3,4},{4,5},{5,6},{6,7},{7,0},{8,9},{9,10},{10,1... | collective-permute-start | bytes 12296 | tf_op jit(solution)/shard_map/ppermute | solution.py:535
  89.8 3.8 %collective-permute-start.12 = (f32[8,128]{1,0:T(8,128)S(1)}, f32[8,128]{1,0:T(8,128)S(1)}, u32[]{:S(2)}, u32[]{:S(2)}) collective-permute-start(f32[8,128]{1,0:T(8,128)S(1)} %get-tuple-element.78), channel_id=1, source_target_pairs={{0,7},{1,0},{2,1},{3,2},{4,3},{5,4},{6,5},{7,6},{8,15},{9,8},{10,9... | collective-permute-start | bytes 12296 | tf_op jit(solution)/shard_map/ppermute | solution.py:535
  122.3 14.3 %all-to-all-start.1 = ((f32[32,24,128]{2,1,0:T(8,128)}), f32[32,24,128]{2,1,0:T(8,128)S(1)}, u32[]{:S(2)}, u32[]{:S(2)}) async-start(f32[32,24,128]{2,1,0:T(8,128)} %get-tuple-element.76), calls=%async_computation.1 | async-start | bytes 786432 | tf_op jit(solution)/shard_map/all_to_all | solution.py:709
  (3 other events, 2.7 us)

commit v3 on v2

--- a/solution.py
+++ b/solution.py
@@ -178,10 +178,8 @@
         copy.wait()
 
 
-def pack_y(round_id, place, lookup, field, x_plus, x_minus, *rest):
-    up, down = rest[-2:]
+def pack_y(place, field, x_plus, x_minus, down, up):
     flags = sides(place)
-    owner, near = own_slab(place)
 
     def chunk(i, carry):
         parts = []
@@ -196,28 +194,31 @@
         return carry
 
     lax.fori_loop(0, HALF // CHUNK, chunk, 0)
-    if round_id == 1:
-        slab = rest[0]
-        for depth in range(RING):
-            top = jnp.maximum(lookup[owner] - 1 - depth, 0)
-            at = slice(HALF + 64 * depth, HALF + 64 * (depth + 1))
-            up[at, :] = slab[top].reshape(64, LANES)
-            down[at, :] = slab[depth].reshape(64, LANES)
-        count = jnp.full((8, LANES), lookup[owner], jnp.int32).astype(F32)
-        up[-8:, :] = count
-        down[-8:, :] = count
-    else:
-        below, above = rest[:2]
-        size = 64 * (RING - 1)
-        up[HALF : HALF + size, :] = kept(near[0], below[HALF : HALF + size, :])
-        down[HALF : HALF + size, :] = kept(near[1], above[HALF : HALF + size, :])
-        up[-8:, :] = below[-8:, :]
-        down[-8:, :] = above[-8:, :]
-
-
-def planes_of(message, start, count, flag):
+
+
+def choose_near(place, lookup, slab, up, down):
+    count = lookup[own_slab(place)[0]]
+    for depth in range(RING):
+        at = slice(64 * depth, 64 * (depth + 1))
+        up[at, :] = slab[jnp.maximum(count - 1 - depth, 0)].reshape(64, LANES)
+        down[at, :] = slab[depth].reshape(64, LANES)
+    count = jnp.full((8, LANES), count, jnp.int32).astype(F32)
+    up[-8:, :] = count
+    down[-8:, :] = count
+
+
+def choose_next(place, below, above, up, down):
+    near = own_slab(place)[1]
+    size = 64 * (RING - 1)
+    up[:size, :] = kept(near[0], below[:size, :])
+    down[:size, :] = kept(near[1], above[:size, :])
+    up[-8:, :] = below[-8:, :]
+    down[-8:, :] = above[-8:, :]
+
+
+def planes_of(message, count, flag):
     return [
-        kept(flag, message[start + 64 * d : start + 64 * (d + 1), :]).reshape(8, 8, LANES)
+        kept(flag, message[64 * d : 64 * (d + 1), :]).reshape(8, 8, LANES)
         for d in range(count)
     ]
 
@@ -225,14 +226,14 @@
 def choose_far(place, below1, above1, below2, above2, up, down):
     near = own_slab(place)[1]
     for one, two, out, flag in ((below1, below2, up, near[0]), (above1, above2, down, near[1])):
-        first = planes_of(one, HALF, 2, flag)
-        second = planes_of(two, HALF, 1, flag)
+        first = planes_of(one, 2, flag)
+        second = planes_of(two, 1, flag)
         out[0:64, :] = first[0].reshape(64, LANES)
         out[64:128, :] = jnp.where(one[-8:, :] > 1.5, first[1], second[0]).reshape(64, LANES)
 
 
 def beyond(one, two, three, near, far):
-    a, b, c = planes_of(one, HALF, 4, near), planes_of(two, HALF, 3, near), planes_of(three, 0, 2, far)
+    a, b, c = planes_of(one, 4, near), planes_of(two, 3, near), planes_of(three, 2, far)
     first, second = one[-8:, :], two[-8:, :]
     two_left = jnp.where(second > 1.5, b[1], c[0])
     three_left = jnp.where(second > 2.5, b[2], jnp.where(second > 1.5, c[0], c[1]))
@@ -510,6 +511,10 @@
         out[:, lanes] = conduct[:, lanes] * rows[half * LANES : (half + 1) * LANES, :].T
 
 
+def in_hbm(value):
+    return pltpu.with_memory_space_constraint(value, pltpu.HBM)
+
+
 def shape(*dims):
     return jax.ShapeDtypeStruct(dims, F32)
 
@@ -557,7 +562,7 @@
         compiler_params=params(),
         cost_estimate=cost(1 << 20, 2 * field_bytes),
         name="prepare_field",
-    )(earlier_edge_voltage.reshape(6, LANES, CZ))
+    )(in_hbm(earlier_edge_voltage.reshape(6, LANES, CZ)))
     x_ghosts = turn(face_low, "gx", -1), turn(face_high, "gx", 1)
     solver = subdomain_inverse_full[0, 0, 0]
     drive, conduct, diagonal, slab, solver = pl.pallas_call(
@@ -582,29 +587,43 @@
         cost_estimate=cost(1 << 20, 16 * field_bytes),
         name="prepare_rest",
     )(
-        coil_drive_current.reshape(6, LANES, CZ),
-        sigma_omega_cellwise.reshape(1, LANES, CZ),
-        subdomain_inverse_main[0, 0, 0],
-        warming_amount[0, 0, 0],
-        heat_spreading_coef[0, 0, 0],
-        solver,
+        in_hbm(coil_drive_current.reshape(6, LANES, CZ)),
+        in_hbm(sigma_omega_cellwise.reshape(1, LANES, CZ)),
+        in_hbm(subdomain_inverse_main[0, 0, 0]),
+        in_hbm(warming_amount[0, 0, 0]),
+        in_hbm(heat_spreading_coef[0, 0, 0]),
+        in_hbm(solver),
     )
     x_ghosts, drive, conduct, diagonal, slab, solver = lax.optimization_barrier(
         (x_ghosts, drive, conduct, diagonal, slab, solver)
     )
 
-    def halo(round_id, field, x_plus, x_minus, extra):
-        message = shape(HALF + 64 * (RING + 1 - round_id) + 8, LANES)
+    def chosen(kernel, rows, *inputs):
+        message = shape(rows, LANES)
+        small = inputs[1].ndim == 1
         up, down = pl.pallas_call(
-            functools.partial(pack_y, round_id),
+            kernel,
             out_shape=(message, message),
-            in_specs=[SMEM] * 2 + [VMEM] * (3 + len(extra)),
+            in_specs=[SMEM] * (1 + small) + [VMEM] * (len(inputs) - 1 - small),
+            out_specs=[VMEM] * 2,
+            compiler_params=params(),
+            name=kernel.__name__,
+        )(*inputs)
+        step = 2 if kernel is choose_far else 1
+        return ring(up, step), ring(down, -step)
+
+    def halo(field, x_plus, x_minus):
+        message = shape(HALF, LANES)
+        down, up = pl.pallas_call(
+            pack_y,
+            out_shape=(message, message),
+            in_specs=[SMEM] + [VMEM] * 3,
             out_specs=[VMEM] * 2,
             compiler_params=params(),
             cost_estimate=cost(1 << 20, field_bytes),
             name="pack_y",
-        )(place, lookup, field, x_plus, x_minus, *extra)
-        y_plus, y_minus = ring(down, -1), ring(up, 1)
+        )(place, field, x_plus, x_minus)
+        y_plus, y_minus = turn(down, "gy", -1), turn(up, "gy", 1)
         ghosts = (x_plus, x_minus, y_plus, y_minus)
         specs = []
         for block, half_block in ((0, 0), (CZ // 8 - 1, HALF // 8 - 1)):
@@ -623,13 +642,12 @@
         z_plus, z_minus = turn(z_low, "gz", -1), turn(z_high, "gz", 1)
         return ghosts + (z_plus, z_minus)
 
-    extra = (slab,)
-    received = []
+    near_planes = chosen(choose_near, 64 * RING + 8, place, lookup, slab)
     for sweep_index in range(SWEEPS):
         final = sweep_index == SWEEPS - 1
-        ghosts = halo(sweep_index + 1, field, *x_ghosts, extra)
-        extra = (ghosts[3], ghosts[2])
-        received += extra
+        if final:
+            next_planes = chosen(choose_next, 64 * (RING - 1) + 8, place, *near_planes)
+        ghosts = halo(field, *x_ghosts)
         scratch = [
             pltpu.VMEM((10, CZ + 2 * HALO, LANES), F32),
             pltpu.VMEM(((CZ + 1 + WINDOW) * PLANE + 8, LANES), F32),
@@ -666,16 +684,8 @@
         cost_estimate=cost(1 << 20, 2 * field_bytes),
         name="finish_field",
     )(field)
-    far = shape(128, LANES)
-    far_up, far_down = pl.pallas_call(
-        choose_far,
-        out_shape=(far, far),
-        in_specs=[SMEM] + [VMEM] * 4,
-        out_specs=[VMEM] * 2,
-        compiler_params=params(),
-        name="choose_far",
-    )(place, *received)
-    received += [ring(far_up, 2), ring(far_down, -2)]
+    received = [*near_planes, *next_planes]
+    received += chosen(choose_far, 128, place, *received)
     heat_above, heat_below = turn(heat[:8], "gz", -1), turn(heat[CZ - 8 :], "gz", 1)
     heat_above, heat_below, field_new, *far_planes = lax.optimization_barrier(
         (heat_above, heat_below, field_new, *received[-2:])

time: 138 us -> 123 us (0.89)
  waiting for transfers between devices: 27.6 us -> 12.2 us
  starting transfers between devices: 36.2 us -> 47.1 us
  local copies, waits for them, and re-layouts: 9.32 us -> 0.02 us
  blocking collectives: 22.5 us -> 20 us
    ppermute x10 -> x14, starting transfers between devices: 11.2 us -> 25.5 us  [turn(): lax.ppermute(value, axis, [(i, (i + step) % count) for i in range(count)])]
    ppermute x6, waiting for transfers between devices: 11.7 us -> 0.02 us  [ring(): return lax.ppermute(value, ('gx', 'gy', 'gz'), pairs)]
    unnamed x20 -> x6, local copies, waits for them, and re-layouts: 9.32 us -> 0.01 us
    ppermute x10 -> x14, waiting for transfers between devices: 8.01 us -> 4.22 us  [turn(): lax.ppermute(value, axis, [(i, (i + step) % count) for i in range(count)])]
    ppermute x6, starting transfers between devices: 21 us -> 17.7 us  [ring(): return lax.ppermute(value, ('gx', 'gy', 'gz'), pairs)]
    all_to_all x1, blocking collectives: 22.5 us -> 20 us  [body(): lax.all_to_all(outgoing, ('gx', 'gy'), split_axis=0, concat_axis=0, tiled...]
    pallas_call x3 -> x5, Pallas kernels: 3.25 us -> 4.34 us  [the longest x2 2.63 us: halo(): pl.pallas_call(pack_y, out_shape=(message, message), in_specs=[SMEM] + [V...]
  transfers between devices with their start and end apart: 17 -> 21, of which waited for: 9 -> 6; matrix products, arithmetic and copies ran while one was open for 0% -> 0% of each run, Pallas kernels for 13% -> 25%
where the time goes in v3:
time: 123 us
  starting transfers between devices  47.1 us (38%)
  Pallas kernels  42.4 us (34%)
  blocking collectives  20 us (16%)
  waiting for transfers between devices  12.2 us (10%)
    ppermute x14, starting transfers between devices, turn(): lax.ppermute(value, axis, [(i, (i + step) % count) for i in range(count)])  25.5 us
    all_to_all x1, blocking collectives, body(): lax.all_to_all(outgoing, ('gx', 'gy'), split_axis=0, concat_axis=0, tiled...  20 us
    pallas_call x2, Pallas kernels, body(): pl.pallas_call(functools.partial(sweep, final), out_shape=outs, in_specs=...  19.3 us
    ppermute x6, starting transfers between devices, ring(): return lax.ppermute(value, ('gx', 'gy', 'gz'), pairs)  17.7 us
    all_to_all x1, waiting for transfers between devices, body(): lax.all_to_all(factor, ('gx', 'gy'), split_axis=0, concat_axis=0, tiled=T...  7.92 us
    pallas_call x1, Pallas kernels, body(): pl.pallas_call(heat_step, out_shape=(shape(owners, slab_cap, LANES), shap...  5.56 us
    ppermute x14, waiting for transfers between devices, turn(): lax.ppermute(value, axis, [(i, (i + step) % count) for i in range(count)])  4.22 us
    pallas_call x1, Pallas kernels, body(): pl.pallas_call(prepare_rest, out_shape=(shape(6, CZ, LANES), shape(1, CZ,...  4.06 us
  transfers between devices with their start and end apart: 21, of which 6 were waited for; matrix products, arithmetic and copies ran while one was open for 0% of the time, Pallas kernels for 25%

profile of v3, /device:TPU:1, one launch (start us, length us, event | category | flops | bytes accessed | tf_op | source)
XLA Modules:
  0.0 122.6 jit_solution(10306956619569228383)
XLA Ops:
  0.7 2.5 %prepare_field.1 = (f32[6,256,128]{2,1,0:T(8,128)S(1)}, f32[256,128]{1,0:T(8,128)S(1)}, f32[256,128]{1,0:T(8,128)S(1)}) custom-call(f32[6,128,256]{2,1,0:T(8,128)} %bitcast.27), custom_call_target="tpu_custom_call" | custom-call | flops 1048576 | bytes 1572864 | tf_op jit(solution)/shard_map/prepare_field/pallas_call | solution.py:556
  3.2 3.6 %collective-permute-start = (f32[256,128]{1,0:T(8,128)S(1)}, f32[256,128]{1,0:T(8,128)S(1)}, u32[]{:S(2)}, u32[]{:S(2)}) collective-permute-start(f32[256,128]{1,0:T(8,128)S(1)} %get-tuple-element.45), channel_id=1, source_target_pairs={{0,192},{64,0},{128,64},{192,128},{1,193},{65,1},{129,65},{193,129... | collective-permute-start | bytes 393224 | tf_op jit(solution)/shard_map/ppermute | solution.py:540
  6.8 4.1 %prepare_rest.1 = (f32[6,256,128]{2,1,0:T(8,128)S(1)}, f32[1,256,128]{2,1,0:T(8,128)S(1)}, f32[512,16]{1,0:T(8,128)S(1)}, f32[24,2,4,8,128]{4,3,2,1,0:T(8,128)S(1)}, bf16[16,512,512]{2,1,0:T(8,128)(2,1)S(1)}) custom-call(f32[6,128,256]{2,1,0:T(8,128)} %bitcast.26, f32[1,128,256]{2,1,0:T(8,128)} %bitcast.16, f32[16,512]{1,0:T(8,128)} %bitcast.33, ...), custom_call_target="tpu_custom_call" | custom-call | flops 1048576 | bytes 12582912 | tf_op jit(solution)/shard_map/prepare_rest/pallas_call | solution.py:568
  11.8 1.3 %pack_y.2 = (f32[128,128]{1,0:T(8,128)S(1)}, f32[128,128]{1,0:T(8,128)S(1)}) custom-call(s32[3]{0:T(128)S(1)} %pad_add_fusion.place, f32[6,256,128]{2,1,0:T(8,128)S(1)} %get-tuple-element.44.field.refs_0_.refs_5_, f32[256,128]{1,0:T(8,128)S(1)} %collective-permute-done.x_plus.refs_1_.refs_6_.xp, f32[256,128]{1,0:T(8,128)S(1)} %collective-permute-done.1.x_minus.refs_2_.refs_7_.xm), custom_call_target="tpu_custom_call" | custom-call | flops 1048576 | bytes 786432 | tf_op jit(solution)/shard_map/pack_y/pallas_call | solution.py:617
  13.2 2.1 %collective-permute-start.2 = (f32[128,128]{1,0:T(8,128)S(1)}, f32[128,128]{1,0:T(8,128)S(1)}, u32[]{:S(2)}, u32[]{:S(2)}) collective-permute-start(f32[128,128]{1,0:T(8,128)S(1)} %get-tuple-element.56), channel_id=1, source_target_pairs={{0,56},{8,0},{16,8},{24,16},{32,24},{40,32},{48,40},{56,48},{1,57}... | collective-permute-start | bytes 196616 | tf_op jit(solution)/shard_map/ppermute | solution.py:540
  16.4 1.9 %collective-permute-done.2.refs_3_.refs_8_.yp = f32[128,128]{1,0:T(8,128)S(1)} collective-permute-done((f32[128,128]{1,0:T(8,128)S(1)}, f32[128,128]{1,0:T(8,128)S(1)}, u32[]{:S(2)}, u32[]{:S(2)}) %collective-permute-start.2) | collective-permute-done | bytes 65568 | tf_op jit(solution)/shard_map/ppermute | solution.py:540
  18.9 5.6 %collective-permute-start.4 = (f32[16,128]{1,0:T(8,128)S(1)}, f32[16,128]{1,0:T(8,128)S(1)}, u32[]{:S(2)}, u32[]{:S(2)}) collective-permute-start(f32[16,128]{1,0:T(8,128)S(1)} %get-tuple-element.58), channel_id=1, source_target_pairs={{0,7},{1,0},{2,1},{3,2},{4,3},{5,4},{6,5},{7,6},{8,15},{9,8},{10,9... | collective-permute-start | bytes 24584 | tf_op jit(solution)/shard_map/ppermute | solution.py:540
  25.1 2.1 %collective-permute-start.14 = (f32[264,128]{1,0:T(8,128)S(1)}, f32[264,128]{1,0:T(8,128)S(1)}, u32[]{:S(2)}, u32[]{:S(2)}) collective-permute-start(f32[264,128]{1,0:T(8,128)S(1)} %get-tuple-element.72), channel_id=1, source_target_pairs={{0,8},{8,16},{16,24},{24,32},{32,40},{40,48},{48,56},{56,64},{64,7... | collective-permute-start | bytes 405512 | tf_op jit(solution)/shard_map/ppermute | solution.py:548
  28.2 9.9 %sweep.2 = (f32[6,256,128]{2,1,0:T(8,128)S(1)}, f32[256,128]{1,0:T(8,128)S(1)}, f32[256,128]{1,0:T(8,128)S(1)}) custom-call(s32[3]{0:T(128)S(1)} %pad_add_fusion.place, s32[16]{0:T(128)S(1)} %bitcast.23, f32[6,256,128]{2,1,0:T(8,128)S(1)} %get-tuple-element.44.field.refs_0_.refs_5_, f32[6,256,128]{2,1,0:T(8,128)S(1)} %get-tuple-element.52.drive, ...), custom_call_target="tpu_custom_call" | custom-call | flops 268435456 | bytes 3145728 | tf_op jit(solution)/shard_map/sweep/pallas_call | solution.py:662
  38.2 1.8 %collective-permute-start.6 = (f32[256,128]{1,0:T(8,128)S(1)}, f32[256,128]{1,0:T(8,128)S(1)}, u32[]{:S(2)}, u32[]{:S(2)}) collective-permute-start(f32[256,128]{1,0:T(8,128)S(1)} %get-tuple-element.63), channel_id=1, source_target_pairs={{0,192},{64,0},{128,64},{192,128},{1,193},{65,1},{129,65},{193,129... | collective-permute-start | bytes 393224 | tf_op jit(solution)/shard_map/ppermute | solution.py:540
  40.6 3.5 %collective-permute-start.16 = (f32[200,128]{1,0:T(8,128)S(1)}, f32[200,128]{1,0:T(8,128)S(1)}, u32[]{:S(2)}, u32[]{:S(2)}) collective-permute-start(f32[200,128]{1,0:T(8,128)S(1)} %get-tuple-element.74), channel_id=1, source_target_pairs={{0,8},{8,16},{16,24},{24,32},{32,40},{40,48},{48,56},{56,64},{64,7... | collective-permute-start | bytes 307208 | tf_op jit(solution)/shard_map/ppermute | solution.py:548
  44.1 4.1 %collective-permute-start.17 = (f32[200,128]{1,0:T(8,128)S(1)}, f32[200,128]{1,0:T(8,128)S(1)}, u32[]{:S(2)}, u32[]{:S(2)}) collective-permute-start(f32[200,128]{1,0:T(8,128)S(1)} %get-tuple-element.75), channel_id=1, source_target_pairs={{0,255},{8,0},{16,8},{24,16},{32,24},{40,32},{48,40},{56,48},{64,5... | collective-permute-start | bytes 307208 | tf_op jit(solution)/shard_map/ppermute | solution.py:548
  48.2 1.3 %pack_y.3 = (f32[128,128]{1,0:T(8,128)S(1)}, f32[128,128]{1,0:T(8,128)S(1)}) custom-call(s32[3]{0:T(128)S(1)} %pad_add_fusion.place, f32[6,256,128]{2,1,0:T(8,128)S(1)} %get-tuple-element.62.field.refs_0_.refs_5_, f32[256,128]{1,0:T(8,128)S(1)} %collective-permute-done.6.x_plus.refs_1_.refs_6_.xp, ...), custom_call_target="tpu_custom_call" | custom-call | flops 1048576 | bytes 786432 | tf_op jit(solution)/shard_map/pack_y/pallas_call | solution.py:617
  49.5 6.9 %collective-permute-start.8 = (f32[128,128]{1,0:T(8,128)S(1)}, f32[128,128]{1,0:T(8,128)S(1)}, u32[]{:S(2)}, u32[]{:S(2)}) collective-permute-start(f32[128,128]{1,0:T(8,128)S(1)} %get-tuple-element.65), channel_id=1, source_target_pairs={{0,56},{8,0},{16,8},{24,16},{32,24},{40,32},{48,40},{56,48},{1,57}... | collective-permute-start | bytes 196616 | tf_op jit(solution)/shard_map/ppermute | solution.py:540
  60.6 6.9 %collective-permute-start.19 = (f32[128,128]{1,0:T(8,128)S(1)}, f32[128,128]{1,0:T(8,128)S(1)}, u32[]{:S(2)}, u32[]{:S(2)}) collective-permute-start(f32[128,128]{1,0:T(8,128)S(1)} %get-tuple-element.77), channel_id=1, source_target_pairs={{0,247},{8,255},{16,0},{24,8},{32,16},{40,24},{48,32},{56,40},{64,... | collective-permute-start | bytes 196616 | tf_op jit(solution)/shard_map/ppermute | solution.py:548
  67.5 9.4 %sweep.3 = (f32[6,256,128]{2,1,0:T(8,128)S(1)}, f32[256,128]{1,0:T(8,128)S(1)}) custom-call(s32[3]{0:T(128)S(1)} %pad_add_fusion.place, s32[16]{0:T(128)S(1)} %bitcast.24, f32[6,256,128]{2,1,0:T(8,128)S(1)} %get-tuple-element.62.field.refs_0_.refs_5_, f32[6,256,128]{2,1,0:T(8,128)S(1)} %get-tuple-element.52.drive, ...), custom_call_target="tpu_custom_call" | custom-call | flops 268435456 | bytes 3145728 | tf_op jit(solution)/shard_map/sweep/pallas_call | solution.py:662
  77.0 2.7 %collective-permute-start.12 = (f32[8,128]{1,0:T(8,128)S(1)}, f32[8,128]{1,0:T(8,128)S(1)}, u32[]{:S(2)}, u32[]{:S(2)}) collective-permute-start(f32[8,128]{1,0:T(8,128)S(1)} %get-tuple-element.86), channel_id=1, source_target_pairs={{0,7},{1,0},{2,1},{3,2},{4,3},{5,4},{6,5},{7,6},{8,15},{9,8},{10,9... | collective-permute-start | bytes 12296 | tf_op jit(solution)/shard_map/ppermute | solution.py:540
  79.6 1.1 finish_field.1
  81.4 20.0 %all_to_all.10.arrived = f32[32,32,128]{2,1,0:T(8,128)S(1)} all-to-all(f32[32,32,128]{2,1,0:T(8,128)S(1)} %pack_heat.1), channel_id=1, replica_groups=mesh['gx'=4,'gy'=8,'gz'=8] {'gx','gy'}, dimensions={0} | all-to-all | bytes 1048576 | tf_op jit(solution)/shard_map/all_to_all | solution.py:704
  101.4 5.6 %heat_step.1 = (f32[32,24,128]{2,1,0:T(8,128)}, f32[24,4,8,128]{3,2,1,0:T(8,128)S(1)}) custom-call(s32[3]{0:T(128)S(1)} %pad_add_fusion.place, s32[32]{0:T(128)S(1)} %bitcast.20, f32[24,2,4,8,128]{4,3,2,1,0:T(8,128)S(1)} %get-tuple-element.71.slab, f32[264,128]{1,0:T(8,128)S(1)} %collective-permute-done.14.below.below1, ...), custom_call_target="tpu_custom_call" | custom-call | tf_op jit(solution)/shard_map/heat_step/pallas_call | solution.py:706
  106.9 4.0 %all-to-all-start.1 = ((f32[32,24,128]{2,1,0:T(8,128)}), f32[32,24,128]{2,1,0:T(8,128)S(1)}, u32[]{:S(2)}, u32[]{:S(2)}) async-start(f32[32,24,128]{2,1,0:T(8,128)} %get-tuple-element.84), calls=%async_computation.1 | async-start | bytes 786432 | tf_op jit(solution)/shard_map/all_to_all | solution.py:719
  110.9 2.4 %finish_slab.1 = f32[24,32,128]{2,1,0:T(8,128)} custom-call(s32[3]{0:T(128)S(1)} %pad_add_fusion.place, s32[32]{0:T(128)S(1)} %bitcast.21, f32[24,4,8,128]{3,2,1,0:T(8,128)S(1)} %get-tuple-element.83.warm), custom_call_target="tpu_custom_call" | custom-call | tf_op jit(solution)/shard_map/finish_slab/pallas_call | solution.py:720
  113.3 7.9 %all-to-all-done.1.returned = f32[32,24,128]{2,1,0:T(8,128)S(1)} async-done(((f32[32,24,128]{2,1,0:T(8,128)}), f32[32,24,128]{2,1,0:T(8,128)S(1)}, u32[]{:S(2)}, u32[]{:S(2)}) %all-to-all-start.1) | async-done | bytes 393248 | tf_op jit(solution)/shard_map/all_to_all | solution.py:719
  121.2 1.3 %finish_conduct.1 = f32[128,256]{1,0:T(8,128)} custom-call(s32[32]{0:T(128)S(1)} %bitcast.22, f32[32,24,128]{2,1,0:T(8,128)S(1)} %all-to-all-done.1.returned, f32[128,256]{1,0:T(8,128)S(1)} %bitcast.17), custom_call_target="tpu_custom_call" | custom-call | tf_op jit(solution)/shard_map/finish_conduct/pallas_call | solution.py:728
  (43 shorter events, 9.7 us)
Async XLA Ops:
  0.6 23.9 %copy-start.1 = (s32[1,32]{1,0:T(1,128)S(1)}, s32[1,32]{1,0:T(1,128)}, u32[]{:S(2)}) copy-start(s32[1,32]{1,0:T(1,128)} %param.15) | copy-start | bytes 388
  0.6 27.6 %copy-start.2 = (s32[1,1,1,16]{3,2,1,0:T(1,128)S(1)}, s32[1,1,1,16]{3,2,1,0:T(1,128)}, u32[]{:S(2)}) copy-start(s32[1,1,1,16]{3,2,1,0:T(1,128)} %param.14) | copy-start | bytes 196
  3.2 7.8 %collective-permute-start = (f32[256,128]{1,0:T(8,128)S(1)}, f32[256,128]{1,0:T(8,128)S(1)}, u32[]{:S(2)}, u32[]{:S(2)}) collective-permute-start(f32[256,128]{1,0:T(8,128)S(1)} %get-tuple-element.45), channel_id=1, source_target_pairs={{0,192},{64,0},{128,64},{192,128},{1,193},{65,1},{129,65},{193,129... | collective-permute-start | bytes 393224 | tf_op jit(solution)/shard_map/ppermute | solution.py:540
  6.8 5.0 %collective-permute-start.1 = (f32[256,128]{1,0:T(8,128)S(1)}, f32[256,128]{1,0:T(8,128)S(1)}, u32[]{:S(2)}, u32[]{:S(2)}) collective-permute-start(f32[256,128]{1,0:T(8,128)S(1)} %get-tuple-element.46), channel_id=1, source_target_pairs={{0,64},{64,128},{128,192},{192,0},{1,65},{65,129},{129,193},{193,1... | collective-permute-start | bytes 393224 | tf_op jit(solution)/shard_map/ppermute | solution.py:540
  13.2 5.2 %collective-permute-start.2 = (f32[128,128]{1,0:T(8,128)S(1)}, f32[128,128]{1,0:T(8,128)S(1)}, u32[]{:S(2)}, u32[]{:S(2)}) collective-permute-start(f32[128,128]{1,0:T(8,128)S(1)} %get-tuple-element.56), channel_id=1, source_target_pairs={{0,56},{8,0},{16,8},{24,16},{32,24},{40,32},{48,40},{56,48},{1,57}... | collective-permute-start | bytes 196616 | tf_op jit(solution)/shard_map/ppermute | solution.py:540
  15.3 3.0 %collective-permute-start.3 = (f32[128,128]{1,0:T(8,128)S(1)}, f32[128,128]{1,0:T(8,128)S(1)}, u32[]{:S(2)}, u32[]{:S(2)}) collective-permute-start(f32[128,128]{1,0:T(8,128)S(1)} %get-tuple-element.57), channel_id=1, source_target_pairs={{0,8},{8,16},{16,24},{24,32},{32,40},{40,48},{48,56},{56,0},{1,9},... | collective-permute-start | bytes 196616 | tf_op jit(solution)/shard_map/ppermute | solution.py:540
  18.9 9.2 %collective-permute-start.4 = (f32[16,128]{1,0:T(8,128)S(1)}, f32[16,128]{1,0:T(8,128)S(1)}, u32[]{:S(2)}, u32[]{:S(2)}) collective-permute-start(f32[16,128]{1,0:T(8,128)S(1)} %get-tuple-element.58), channel_id=1, source_target_pairs={{0,7},{1,0},{2,1},{3,2},{4,3},{5,4},{6,5},{7,6},{8,15},{9,8},{10,9... | collective-permute-start | bytes 24584 | tf_op jit(solution)/shard_map/ppermute | solution.py:540
  24.5 3.7 %collective-permute-start.5 = (f32[16,128]{1,0:T(8,128)S(1)}, f32[16,128]{1,0:T(8,128)S(1)}, u32[]{:S(2)}, u32[]{:S(2)}) collective-permute-start(f32[16,128]{1,0:T(8,128)S(1)} %get-tuple-element.59), channel_id=1, source_target_pairs={{0,1},{1,2},{2,3},{3,4},{4,5},{5,6},{6,7},{7,0},{8,9},{9,10},{10,1... | collective-permute-start | bytes 24584 | tf_op jit(solution)/shard_map/ppermute | solution.py:540
  25.1 14.9 %collective-permute-start.14 = (f32[264,128]{1,0:T(8,128)S(1)}, f32[264,128]{1,0:T(8,128)S(1)}, u32[]{:S(2)}, u32[]{:S(2)}) collective-permute-start(f32[264,128]{1,0:T(8,128)S(1)} %get-tuple-element.72), channel_id=1, source_target_pairs={{0,8},{8,16},{16,24},{24,32},{32,40},{40,48},{48,56},{56,64},{64,7... | collective-permute-start | bytes 405512 | tf_op jit(solution)/shard_map/ppermute | solution.py:548
  27.2 12.8 %collective-permute-start.15 = (f32[264,128]{1,0:T(8,128)S(1)}, f32[264,128]{1,0:T(8,128)S(1)}, u32[]{:S(2)}, u32[]{:S(2)}) collective-permute-start(f32[264,128]{1,0:T(8,128)S(1)} %get-tuple-element.73), channel_id=1, source_target_pairs={{0,255},{8,0},{16,8},{24,16},{32,24},{40,32},{48,40},{56,48},{64,5... | collective-permute-start | bytes 405512 | tf_op jit(solution)/shard_map/ppermute | solution.py:548
  38.2 10.0 %collective-permute-start.6 = (f32[256,128]{1,0:T(8,128)S(1)}, f32[256,128]{1,0:T(8,128)S(1)}, u32[]{:S(2)}, u32[]{:S(2)}) collective-permute-start(f32[256,128]{1,0:T(8,128)S(1)} %get-tuple-element.63), channel_id=1, source_target_pairs={{0,192},{64,0},{128,64},{192,128},{1,193},{65,1},{129,65},{193,129... | collective-permute-start | bytes 393224 | tf_op jit(solution)/shard_map/ppermute | solution.py:540
  40.0 8.2 %collective-permute-start.7 = (f32[256,128]{1,0:T(8,128)S(1)}, f32[256,128]{1,0:T(8,128)S(1)}, u32[]{:S(2)}, u32[]{:S(2)}) collective-permute-start(f32[256,128]{1,0:T(8,128)S(1)} %get-tuple-element.64), channel_id=1, source_target_pairs={{0,64},{64,128},{128,192},{192,0},{1,65},{65,129},{129,193},{193,1... | collective-permute-start | bytes 393224 | tf_op jit(solution)/shard_map/ppermute | solution.py:540
  40.6 19.3 %collective-permute-start.16 = (f32[200,128]{1,0:T(8,128)S(1)}, f32[200,128]{1,0:T(8,128)S(1)}, u32[]{:S(2)}, u32[]{:S(2)}) collective-permute-start(f32[200,128]{1,0:T(8,128)S(1)} %get-tuple-element.74), channel_id=1, source_target_pairs={{0,8},{8,16},{16,24},{24,32},{32,40},{40,48},{48,56},{56,64},{64,7... | collective-permute-start | bytes 307208 | tf_op jit(solution)/shard_map/ppermute | solution.py:548
  44.1 15.8 %collective-permute-start.17 = (f32[200,128]{1,0:T(8,128)S(1)}, f32[200,128]{1,0:T(8,128)S(1)}, u32[]{:S(2)}, u32[]{:S(2)}) collective-permute-start(f32[200,128]{1,0:T(8,128)S(1)} %get-tuple-element.75), channel_id=1, source_target_pairs={{0,255},{8,0},{16,8},{24,16},{32,24},{40,32},{48,40},{56,48},{64,5... | collective-permute-start | bytes 307208 | tf_op jit(solution)/shard_map/ppermute | solution.py:548
  49.5 7.8 %collective-permute-start.8 = (f32[128,128]{1,0:T(8,128)S(1)}, f32[128,128]{1,0:T(8,128)S(1)}, u32[]{:S(2)}, u32[]{:S(2)}) collective-permute-start(f32[128,128]{1,0:T(8,128)S(1)} %get-tuple-element.65), channel_id=1, source_target_pairs={{0,56},{8,0},{16,8},{24,16},{32,24},{40,32},{48,40},{56,48},{1,57}... | collective-permute-start | bytes 196616 | tf_op jit(solution)/shard_map/ppermute | solution.py:540
  56.5 1.3 %collective-permute-start.9 = (f32[128,128]{1,0:T(8,128)S(1)}, f32[128,128]{1,0:T(8,128)S(1)}, u32[]{:S(2)}, u32[]{:S(2)}) collective-permute-start(f32[128,128]{1,0:T(8,128)S(1)} %get-tuple-element.66), channel_id=1, source_target_pairs={{0,8},{8,16},{16,24},{24,32},{32,40},{40,48},{48,56},{56,0},{1,9},... | collective-permute-start | bytes 196616 | tf_op jit(solution)/shard_map/ppermute | solution.py:540
  58.4 9.1 %collective-permute-start.10 = (f32[16,128]{1,0:T(8,128)S(1)}, f32[16,128]{1,0:T(8,128)S(1)}, u32[]{:S(2)}, u32[]{:S(2)}) collective-permute-start(f32[16,128]{1,0:T(8,128)S(1)} %get-tuple-element.67), channel_id=1, source_target_pairs={{0,7},{1,0},{2,1},{3,2},{4,3},{5,4},{6,5},{7,6},{8,15},{9,8},{10,9... | collective-permute-start | bytes 24584 | tf_op jit(solution)/shard_map/ppermute | solution.py:540
  58.9 8.5 %collective-permute-start.11 = (f32[16,128]{1,0:T(8,128)S(1)}, f32[16,128]{1,0:T(8,128)S(1)}, u32[]{:S(2)}, u32[]{:S(2)}) collective-permute-start(f32[16,128]{1,0:T(8,128)S(1)} %get-tuple-element.68), channel_id=1, source_target_pairs={{0,1},{1,2},{2,3},{3,4},{4,5},{5,6},{6,7},{7,0},{8,9},{9,10},{10,1... | collective-permute-start | bytes 24584 | tf_op jit(solution)/shard_map/ppermute | solution.py:540
  60.5 20.3 %collective-permute-start.18 = (f32[128,128]{1,0:T(8,128)S(1)}, f32[128,128]{1,0:T(8,128)S(1)}, u32[]{:S(2)}, u32[]{:S(2)}) collective-permute-start(f32[128,128]{1,0:T(8,128)S(1)} %get-tuple-element.76), channel_id=1, source_target_pairs={{0,16},{8,24},{16,32},{24,40},{32,48},{40,56},{48,64},{56,72},{64,... | collective-permute-start | bytes 196616 | tf_op jit(solution)/shard_map/ppermute | solution.py:548
  60.6 60.6 %copy-start = (f32[8,16,256]{2,1,0:T(8,128)S(1)}, f32[8,16,256]{2,1,0:T(8,128)}, u32[]{:S(2)}) copy-start(f32[8,16,256]{2,1,0:T(8,128)} %param.11) | copy-start | bytes 393220
  60.6 20.2 %collective-permute-start.19 = (f32[128,128]{1,0:T(8,128)S(1)}, f32[128,128]{1,0:T(8,128)S(1)}, u32[]{:S(2)}, u32[]{:S(2)}) collective-permute-start(f32[128,128]{1,0:T(8,128)S(1)} %get-tuple-element.77), channel_id=1, source_target_pairs={{0,247},{8,255},{16,0},{24,8},{32,16},{40,24},{48,32},{56,40},{64,... | collective-permute-start | bytes 196616 | tf_op jit(solution)/shard_map/ppermute | solution.py:548
  76.9 3.9 %collective-permute-start.13 = (f32[8,128]{1,0:T(8,128)S(1)}, f32[8,128]{1,0:T(8,128)S(1)}, u32[]{:S(2)}, u32[]{:S(2)}) collective-permute-start(f32[8,128]{1,0:T(8,128)S(1)} %get-tuple-element.85), channel_id=1, source_target_pairs={{0,1},{1,2},{2,3},{3,4},{4,5},{5,6},{6,7},{7,0},{8,9},{9,10},{10,1... | collective-permute-start | bytes 12296 | tf_op jit(solution)/shard_map/ppermute | solution.py:540
  77.0 3.8 %collective-permute-start.12 = (f32[8,128]{1,0:T(8,128)S(1)}, f32[8,128]{1,0:T(8,128)S(1)}, u32[]{:S(2)}, u32[]{:S(2)}) collective-permute-start(f32[8,128]{1,0:T(8,128)S(1)} %get-tuple-element.86), channel_id=1, source_target_pairs={{0,7},{1,0},{2,1},{3,2},{4,3},{5,4},{6,5},{7,6},{8,15},{9,8},{10,9... | collective-permute-start | bytes 12296 | tf_op jit(solution)/shard_map/ppermute | solution.py:540
  106.9 14.3 %all-to-all-start.1 = ((f32[32,24,128]{2,1,0:T(8,128)}), f32[32,24,128]{2,1,0:T(8,128)S(1)}, u32[]{:S(2)}, u32[]{:S(2)}) async-start(f32[32,24,128]{2,1,0:T(8,128)} %get-tuple-element.84), calls=%async_computation.1 | async-start | bytes 786432 | tf_op jit(solution)/shard_map/all_to_all | solution.py:719

commit v4 on v3

--- a/solution.py
+++ b/solution.py
@@ -207,15 +207,6 @@
     down[-8:, :] = count
 
 
-def choose_next(place, below, above, up, down):
-    near = own_slab(place)[1]
-    size = 64 * (RING - 1)
-    up[:size, :] = kept(near[0], below[:size, :])
-    down[:size, :] = kept(near[1], above[:size, :])
-    up[-8:, :] = below[-8:, :]
-    down[-8:, :] = above[-8:, :]
-
-
 def planes_of(message, count, flag):
     return [
         kept(flag, message[64 * d : 64 * (d + 1), :]).reshape(8, 8, LANES)
@@ -224,16 +215,16 @@
 
 
 def choose_far(place, below1, above1, below2, above2, up, down):
-    near = own_slab(place)[1]
-    for one, two, out, flag in ((below1, below2, up, near[0]), (above1, above2, down, near[1])):
-        first = planes_of(one, 2, flag)
-        second = planes_of(two, 1, flag)
+    flags = own_slab(place)[1]
+    for one, two, out, side in ((below1, below2, up, 0), (above1, above2, down, 1)):
+        first = planes_of(one, 2, flags[side])
+        second = planes_of(two, 1, flags[side + 2])
         out[0:64, :] = first[0].reshape(64, LANES)
         out[64:128, :] = jnp.where(one[-8:, :] > 1.5, first[1], second[0]).reshape(64, LANES)
 
 
 def beyond(one, two, three, near, far):
-    a, b, c = planes_of(one, 4, near), planes_of(two, 3, near), planes_of(three, 2, far)
+    a, b, c = planes_of(one, 4, near), planes_of(two, 3, far), planes_of(three, 2, far)
     first, second = one[-8:, :], two[-8:, :]
     two_left = jnp.where(second > 1.5, b[1], c[0])
     three_left = jnp.where(second > 2.5, b[2], jnp.where(second > 1.5, c[0], c[1]))
@@ -599,20 +590,17 @@
     )
 
     def chosen(kernel, rows, *inputs):
-        message = shape(rows, LANES)
         small = inputs[1].ndim == 1
-        up, down = pl.pallas_call(
+        return pl.pallas_call(
             kernel,
-            out_shape=(message, message),
+            out_shape=(shape(rows, LANES),) * 2,
             in_specs=[SMEM] * (1 + small) + [VMEM] * (len(inputs) - 1 - small),
             out_specs=[VMEM] * 2,
             compiler_params=params(),
             name=kernel.__name__,
         )(*inputs)
-        step = 2 if kernel is choose_far else 1
-        return ring(up, step), ring(down, -step)
-
-    def halo(field, x_plus, x_minus):
+
+    def halo(field, x_plus, x_minus, early, late):
         message = shape(HALF, LANES)
         down, up = pl.pallas_call(
             pack_y,
@@ -624,6 +612,8 @@
             name="pack_y",
         )(place, field, x_plus, x_minus)
         y_plus, y_minus = turn(down, "gy", -1), turn(up, "gy", 1)
+        (y_plus, y_minus), early, late = lax.optimization_barrier(((y_plus, y_minus), early, late))
+        late = [ring(value, step) for value, step in zip(late, (2, -2))]
         ghosts = (x_plus, x_minus, y_plus, y_minus)
         specs = []
         for block, half_block in ((0, 0), (CZ // 8 - 1, HALF // 8 - 1)):
@@ -640,14 +630,21 @@
             name="pack_z",
         )(place, field, *ghosts, field, *ghosts)
         z_plus, z_minus = turn(z_low, "gz", -1), turn(z_high, "gz", 1)
-        return ghosts + (z_plus, z_minus)
-
-    near_planes = chosen(choose_near, 64 * RING + 8, place, lookup, slab)
+        (z_plus, z_minus), late = lax.optimization_barrier(((z_plus, z_minus), late))
+        return ghosts + (z_plus, z_minus), early + late
+
+    received = []
     for sweep_index in range(SWEEPS):
         final = sweep_index == SWEEPS - 1
         if final:
-            next_planes = chosen(choose_next, 64 * (RING - 1) + 8, place, *near_planes)
-        ghosts = halo(field, *x_ghosts)
+            up, down = chosen(choose_far, 128, place, *received)
+            early, late = [ring(up, 2), ring(down, -2)], []
+        else:
+            up, down = chosen(choose_near, 64 * RING + 8, place, lookup, slab)
+            early, late = [ring(up, 1), ring(down, -1)], [up, down]
+        x_ghosts, _, _ = lax.optimization_barrier((x_ghosts, up, down))
+        ghosts, arrivals = halo(field, *x_ghosts, early, late)
+        received += arrivals
         scratch = [
             pltpu.VMEM((10, CZ + 2 * HALO, LANES), F32),
             pltpu.VMEM(((CZ + 1 + WINDOW) * PLANE + 8, LANES), F32),
@@ -684,13 +681,10 @@
         cost_estimate=cost(1 << 20, 2 * field_bytes),
         name="finish_field",
     )(field)
-    received = [*near_planes, *next_planes]
-    received += chosen(choose_far, 128, place, *received)
     heat_above, heat_below = turn(heat[:8], "gz", -1), turn(heat[CZ - 8 :], "gz", 1)
-    heat_above, heat_below, field_new, *far_planes = lax.optimization_barrier(
-        (heat_above, heat_below, field_new, *received[-2:])
+    heat_above, heat_below, field_new = lax.optimization_barrier(
+        (heat_above, heat_below, field_new)
     )
-    received[-2:] = far_planes
     rows = slab_cap + 8
     outgoing = pl.pallas_call(
         pack_heat,

time: 123 us -> 129 us (1.049)
  waiting for transfers between devices: 12.2 us -> 17.5 us
  blocking collectives: 20 us -> 22.4 us
    ppermute x14, waiting for transfers between devices: 4.22 us -> 9.59 us  [turn(): lax.ppermute(value, axis, [(i, (i + step) % count) for i in range(count)])]
    all_to_all x1, blocking collectives: 20 us -> 22.4 us  [body(): lax.all_to_all(outgoing, ('gx', 'gy'), split_axis=0, concat_axis=0, tiled...]
  transfers between devices with their start and end apart: 21 -> 21, of which waited for: 6 -> 10; matrix products, arithmetic and copies ran while one was open for 0% -> 0% of each run, Pallas kernels for 25% -> 9%
where the time goes in v4:
time: 129 us
  starting transfers between devices  46.5 us (36%)
  Pallas kernels  41.8 us (32%)
  blocking collectives  22.4 us (17%)
  waiting for transfers between devices  17.5 us (14%)
    ppermute x14, starting transfers between devices, turn(): lax.ppermute(value, axis, [(i, (i + step) % count) for i in range(count)])  25.4 us
    all_to_all x1, blocking collectives, body(): lax.all_to_all(outgoing, ('gx', 'gy'), split_axis=0, concat_axis=0, tiled...  22.4 us
    pallas_call x2, Pallas kernels, body(): pl.pallas_call(functools.partial(sweep, final), out_shape=outs, in_specs=...  19.3 us
    ppermute x6, starting transfers between devices, ring(): return lax.ppermute(value, ('gx', 'gy', 'gz'), pairs)  17.1 us
    ppermute x14, waiting for transfers between devices, turn(): lax.ppermute(value, axis, [(i, (i + step) % count) for i in range(count)])  9.59 us
    all_to_all x1, waiting for transfers between devices, body(): lax.all_to_all(factor, ('gx', 'gy'), split_axis=0, concat_axis=0, tiled=T...  7.92 us
    pallas_call x1, Pallas kernels, body(): pl.pallas_call(heat_step, out_shape=(shape(owners, slab_cap, LANES), shap...  5.55 us
    pallas_call x1, Pallas kernels, body(): pl.pallas_call(prepare_rest, out_shape=(shape(6, CZ, LANES), shape(1, CZ,...  4.06 us
  transfers between devices with their start and end apart: 21, of which 10 were waited for; matrix products, arithmetic and copies ran while one was open for 0% of the time, Pallas kernels for 9%

profile of v4, /device:TPU:1, one launch (start us, length us, event | category | flops | bytes accessed | tf_op | source)
XLA Modules:
  0.0 129.1 jit_solution(15567380307240423937)
XLA Ops:
  0.7 2.5 %prepare_field.1 = (f32[6,256,128]{2,1,0:T(8,128)S(1)}, f32[256,128]{1,0:T(8,128)S(1)}, f32[256,128]{1,0:T(8,128)S(1)}) custom-call(f32[6,128,256]{2,1,0:T(8,128)} %bitcast.27), custom_call_target="tpu_custom_call" | custom-call | flops 1048576 | bytes 1572864 | tf_op jit(solution)/shard_map/prepare_field/pallas_call | solution.py:547
  3.2 3.6 %collective-permute-start = (f32[256,128]{1,0:T(8,128)S(1)}, f32[256,128]{1,0:T(8,128)S(1)}, u32[]{:S(2)}, u32[]{:S(2)}) collective-permute-start(f32[256,128]{1,0:T(8,128)S(1)} %get-tuple-element.61), channel_id=1, source_target_pairs={{0,192},{64,0},{128,64},{192,128},{1,193},{65,1},{129,65},{193,129... | collective-permute-start | bytes 393224 | tf_op jit(solution)/shard_map/ppermute | solution.py:531
  6.8 4.1 %prepare_rest.1 = (f32[6,256,128]{2,1,0:T(8,128)S(1)}, f32[1,256,128]{2,1,0:T(8,128)S(1)}, f32[512,16]{1,0:T(8,128)S(1)}, f32[24,2,4,8,128]{4,3,2,1,0:T(8,128)S(1)}, bf16[16,512,512]{2,1,0:T(8,128)(2,1)S(1)}) custom-call(f32[6,128,256]{2,1,0:T(8,128)} %bitcast.26, f32[1,128,256]{2,1,0:T(8,128)} %bitcast.16, f32[16,512]{1,0:T(8,128)} %bitcast.33, ...), custom_call_target="tpu_custom_call" | custom-call | flops 1048576 | bytes 12582912 | tf_op jit(solution)/shard_map/prepare_rest/pallas_call | solution.py:559
  12.4 3.3 %collective-permute-start.4 = (f32[264,128]{1,0:T(8,128)S(1)}, f32[264,128]{1,0:T(8,128)S(1)}, u32[]{:S(2)}, u32[]{:S(2)}) collective-permute-start(f32[264,128]{1,0:T(8,128)S(1)} %get-tuple-element.83), channel_id=1, source_target_pairs={{0,8},{8,16},{16,24},{24,32},{32,40},{40,48},{48,56},{56,64},{64,7... | collective-permute-start | bytes 405512 | tf_op jit(solution)/shard_map/ppermute | solution.py:539
  15.7 1.3 %pack_y.2 = (f32[128,128]{1,0:T(8,128)S(1)}, f32[128,128]{1,0:T(8,128)S(1)}) custom-call(s32[3]{0:T(128)S(1)} %pad_add_fusion.place, f32[6,256,128]{2,1,0:T(8,128)S(1)} %get-tuple-element.60.field.refs_0_.refs_5_, f32[256,128]{1,0:T(8,128)S(1)} %collective-permute-done.x_plus.refs_1_.refs_6_.xp, f32[256,128]{1,0:T(8,128)S(1)} %collective-permute-done.1.x_minus.refs_2_.refs_7_.xm), custom_call_target="tpu_custom_call" | custom-call | flops 1048576 | bytes 786432 | tf_op jit(solution)/shard_map/pack_y/pallas_call | solution.py:605
  17.0 6.6 %collective-permute-start.2 = (f32[128,128]{1,0:T(8,128)S(1)}, f32[128,128]{1,0:T(8,128)S(1)}, u32[]{:S(2)}, u32[]{:S(2)}) collective-permute-start(f32[128,128]{1,0:T(8,128)S(1)} %get-tuple-element.77), channel_id=1, source_target_pairs={{0,56},{8,0},{16,8},{24,16},{32,24},{40,32},{48,40},{56,48},{1,57}... | collective-permute-start | bytes 196616 | tf_op jit(solution)/shard_map/ppermute | solution.py:531
  24.9 6.9 %collective-permute-start.9 = (f32[264,128]{1,0:T(8,128)S(1)}, f32[264,128]{1,0:T(8,128)S(1)}, u32[]{:S(2)}, u32[]{:S(2)}) collective-permute-start(f32[264,128]{1,0:T(8,128)S(1)} %get-tuple-element.84), channel_id=1, source_target_pairs={{0,247},{8,255},{16,0},{24,8},{32,16},{40,24},{48,32},{56,40},{64,... | collective-permute-start | bytes 405512 | tf_op jit(solution)/shard_map/ppermute | solution.py:539
  32.4 2.7 %collective-permute-start.6 = (f32[16,128]{1,0:T(8,128)S(1)}, f32[16,128]{1,0:T(8,128)S(1)}, u32[]{:S(2)}, u32[]{:S(2)}) collective-permute-start(f32[16,128]{1,0:T(8,128)S(1)} %get-tuple-element.81), channel_id=1, source_target_pairs={{0,7},{1,0},{2,1},{3,2},{4,3},{5,4},{6,5},{7,6},{8,15},{9,8},{10,9... | collective-permute-start | bytes 24584 | tf_op jit(solution)/shard_map/ppermute | solution.py:531
  35.9 2.9 %collective-permute-done.7.zm = f32[16,128]{1,0:T(8,128)S(1)} collective-permute-done((f32[16,128]{1,0:T(8,128)S(1)}, f32[16,128]{1,0:T(8,128)S(1)}, u32[]{:S(2)}, u32[]{:S(2)}) %collective-permute-start.7) | collective-permute-done | bytes 8224 | tf_op jit(solution)/shard_map/ppermute | solution.py:531
  38.9 9.9 %sweep.2 = (f32[6,256,128]{2,1,0:T(8,128)S(1)}, f32[256,128]{1,0:T(8,128)S(1)}, f32[256,128]{1,0:T(8,128)S(1)}) custom-call(s32[3]{0:T(128)S(1)} %pad_add_fusion.place, s32[16]{0:T(128)S(1)} %bitcast.23, f32[6,256,128]{2,1,0:T(8,128)S(1)} %get-tuple-element.60.field.refs_0_.refs_5_, f32[6,256,128]{2,1,0:T(8,128)S(1)} %get-tuple-element.68.drive, ...), custom_call_target="tpu_custom_call" | custom-call | flops 268435456 | bytes 3145728 | tf_op jit(solution)/shard_map/sweep/pallas_call | solution.py:659
  48.9 1.5 %collective-permute-start.11 = (f32[256,128]{1,0:T(8,128)S(1)}, f32[256,128]{1,0:T(8,128)S(1)}, u32[]{:S(2)}, u32[]{:S(2)}) collective-permute-start(f32[256,128]{1,0:T(8,128)S(1)} %get-tuple-element.91), channel_id=1, source_target_pairs={{0,64},{64,128},{128,192},{192,0},{1,65},{65,129},{129,193},{193,1... | collective-permute-start | bytes 393224 | tf_op jit(solution)/shard_map/ppermute | solution.py:531
  51.0 6.9 %collective-permute-start.15 = (f32[128,128]{1,0:T(8,128)S(1)}, f32[128,128]{1,0:T(8,128)S(1)}, u32[]{:S(2)}, u32[]{:S(2)}) collective-permute-start(f32[128,128]{1,0:T(8,128)S(1)} %get-tuple-element.97), channel_id=1, source_target_pairs={{0,247},{8,255},{16,0},{24,8},{32,16},{40,24},{48,32},{56,40},{64,... | collective-permute-start | bytes 196616 | tf_op jit(solution)/shard_map/ppermute | solution.py:539
  57.9 1.3 %pack_y.3 = (f32[128,128]{1,0:T(8,128)S(1)}, f32[128,128]{1,0:T(8,128)S(1)}) custom-call(s32[3]{0:T(128)S(1)} %pad_add_fusion.place, f32[6,256,128]{2,1,0:T(8,128)S(1)} %get-tuple-element.89.field.refs_0_.refs_5_, f32[256,128]{1,0:T(8,128)S(1)} %collective-permute-done.10.x_plus.refs_1_.refs_6_.xp, ...), custom_call_target="tpu_custom_call" | custom-call | flops 1048576 | bytes 786432 | tf_op jit(solution)/shard_map/pack_y/pallas_call | solution.py:605
  59.2 6.7 %collective-permute-start.12 = (f32[128,128]{1,0:T(8,128)S(1)}, f32[128,128]{1,0:T(8,128)S(1)}, u32[]{:S(2)}, u32[]{:S(2)}) collective-permute-start(f32[128,128]{1,0:T(8,128)S(1)} %get-tuple-element.100), channel_id=1, source_target_pairs={{0,56},{8,0},{16,8},{24,16},{32,24},{40,32},{48,40},{56,48},{1,57}... | collective-permute-start | bytes 196616 | tf_op jit(solution)/shard_map/ppermute | solution.py:531
  67.9 1.4 %collective-permute-start.17 = (f32[16,128]{1,0:T(8,128)S(1)}, f32[16,128]{1,0:T(8,128)S(1)}, u32[]{:S(2)}, u32[]{:S(2)}) collective-permute-start(f32[16,128]{1,0:T(8,128)S(1)} %get-tuple-element.105), channel_id=1, source_target_pairs={{0,1},{1,2},{2,3},{3,4},{4,5},{5,6},{6,7},{7,0},{8,9},{9,10},{10,1... | collective-permute-start | bytes 24584 | tf_op jit(solution)/shard_map/ppermute | solution.py:531
  70.4 1.3 collective-permute-done.17.zm
  71.7 9.4 %sweep.3 = (f32[6,256,128]{2,1,0:T(8,128)S(1)}, f32[256,128]{1,0:T(8,128)S(1)}) custom-call(s32[3]{0:T(128)S(1)} %pad_add_fusion.place, s32[16]{0:T(128)S(1)} %bitcast.24, f32[6,256,128]{2,1,0:T(8,128)S(1)} %get-tuple-element.89.field.refs_0_.refs_5_, f32[6,256,128]{2,1,0:T(8,128)S(1)} %get-tuple-element.68.drive, ...), custom_call_target="tpu_custom_call" | custom-call | flops 268435456 | bytes 3145728 | tf_op jit(solution)/shard_map/sweep/pallas_call | solution.py:659
  81.5 2.4 %collective-permute-start.18 = (f32[8,128]{1,0:T(8,128)S(1)}, f32[8,128]{1,0:T(8,128)S(1)}, u32[]{:S(2)}, u32[]{:S(2)}) collective-permute-start(f32[8,128]{1,0:T(8,128)S(1)} %get-tuple-element.118), channel_id=1, source_target_pairs={{0,7},{1,0},{2,1},{3,2},{4,3},{5,4},{6,5},{7,6},{8,15},{9,8},{10,9... | collective-permute-start | bytes 12296 | tf_op jit(solution)/shard_map/ppermute | solution.py:531
  85.6 22.4 %all_to_all.10.arrived = f32[32,32,128]{2,1,0:T(8,128)S(1)} all-to-all(f32[32,32,128]{2,1,0:T(8,128)S(1)} %pack_heat.1), channel_id=1, replica_groups=mesh['gx'=4,'gy'=8,'gz'=8] {'gx','gy'}, dimensions={0} | all-to-all | bytes 1048576 | tf_op jit(solution)/shard_map/all_to_all | solution.py:698
  108.0 5.6 %heat_step.1 = (f32[32,24,128]{2,1,0:T(8,128)}, f32[24,4,8,128]{3,2,1,0:T(8,128)S(1)}) custom-call(s32[3]{0:T(128)S(1)} %pad_add_fusion.place, s32[32]{0:T(128)S(1)} %bitcast.20, f32[24,2,4,8,128]{4,3,2,1,0:T(8,128)S(1)} %get-tuple-element.72.slab, f32[264,128]{1,0:T(8,128)S(1)} %collective-permute-done.4.below1, ...), custom_call_target="tpu_custom_call" | custom-call | tf_op jit(solution)/shard_map/heat_step/pallas_call | solution.py:700
  113.5 4.0 %all-to-all-start.1 = ((f32[32,24,128]{2,1,0:T(8,128)}), f32[32,24,128]{2,1,0:T(8,128)S(1)}, u32[]{:S(2)}, u32[]{:S(2)}) async-start(f32[32,24,128]{2,1,0:T(8,128)} %get-tuple-element.116), calls=%async_computation.1 | async-start | bytes 786432 | tf_op jit(solution)/shard_map/all_to_all | solution.py:713
  117.5 2.4 %finish_slab.1 = f32[24,32,128]{2,1,0:T(8,128)} custom-call(s32[3]{0:T(128)S(1)} %pad_add_fusion.place, s32[32]{0:T(128)S(1)} %bitcast.21, f32[24,4,8,128]{3,2,1,0:T(8,128)S(1)} %get-tuple-element.115.warm), custom_call_target="tpu_custom_call" | custom-call | tf_op jit(solution)/shard_map/finish_slab/pallas_call | solution.py:714
  119.9 7.9 %all-to-all-done.1.returned = f32[32,24,128]{2,1,0:T(8,128)S(1)} async-done(((f32[32,24,128]{2,1,0:T(8,128)}), f32[32,24,128]{2,1,0:T(8,128)S(1)}, u32[]{:S(2)}, u32[]{:S(2)}) %all-to-all-start.1) | async-done | bytes 393248 | tf_op jit(solution)/shard_map/all_to_all | solution.py:713
  127.8 1.3 %finish_conduct.1 = f32[128,256]{1,0:T(8,128)} custom-call(s32[32]{0:T(128)S(1)} %bitcast.22, f32[32,24,128]{2,1,0:T(8,128)S(1)} %all-to-all-done.1.returned, f32[128,256]{1,0:T(8,128)S(1)} %bitcast.17), custom_call_target="tpu_custom_call" | custom-call | tf_op jit(solution)/shard_map/finish_conduct/pallas_call | solution.py:722
  (42 shorter events, 10.2 us)
Async XLA Ops:
  0.6 11.2 %copy-start.1 = (s32[1,32]{1,0:T(1,128)S(1)}, s32[1,32]{1,0:T(1,128)}, u32[]{:S(2)}) copy-start(s32[1,32]{1,0:T(1,128)} %param.15) | copy-start | bytes 388
  0.6 38.2 %copy-start.2 = (s32[1,1,1,16]{3,2,1,0:T(1,128)S(1)}, s32[1,1,1,16]{3,2,1,0:T(1,128)}, u32[]{:S(2)}) copy-start(s32[1,1,1,16]{3,2,1,0:T(1,128)} %param.14) | copy-start | bytes 196
  3.2 7.8 %collective-permute-start = (f32[256,128]{1,0:T(8,128)S(1)}, f32[256,128]{1,0:T(8,128)S(1)}, u32[]{:S(2)}, u32[]{:S(2)}) collective-permute-start(f32[256,128]{1,0:T(8,128)S(1)} %get-tuple-element.61), channel_id=1, source_target_pairs={{0,192},{64,0},{128,64},{192,128},{1,193},{65,1},{129,65},{193,129... | collective-permute-start | bytes 393224 | tf_op jit(solution)/shard_map/ppermute | solution.py:531
  6.8 5.0 %collective-permute-start.1 = (f32[256,128]{1,0:T(8,128)S(1)}, f32[256,128]{1,0:T(8,128)S(1)}, u32[]{:S(2)}, u32[]{:S(2)}) collective-permute-start(f32[256,128]{1,0:T(8,128)S(1)} %get-tuple-element.62), channel_id=1, source_target_pairs={{0,64},{64,128},{128,192},{192,0},{1,65},{65,129},{129,193},{193,1... | collective-permute-start | bytes 393224 | tf_op jit(solution)/shard_map/ppermute | solution.py:531
  12.4 12.5 %collective-permute-start.4 = (f32[264,128]{1,0:T(8,128)S(1)}, f32[264,128]{1,0:T(8,128)S(1)}, u32[]{:S(2)}, u32[]{:S(2)}) collective-permute-start(f32[264,128]{1,0:T(8,128)S(1)} %get-tuple-element.83), channel_id=1, source_target_pairs={{0,8},{8,16},{16,24},{24,32},{32,40},{40,48},{48,56},{56,64},{64,7... | collective-permute-start | bytes 405512 | tf_op jit(solution)/shard_map/ppermute | solution.py:539
  15.7 9.3 %collective-permute-start.5 = (f32[264,128]{1,0:T(8,128)S(1)}, f32[264,128]{1,0:T(8,128)S(1)}, u32[]{:S(2)}, u32[]{:S(2)}) collective-permute-start(f32[264,128]{1,0:T(8,128)S(1)} %get-tuple-element.84), channel_id=1, source_target_pairs={{0,255},{8,0},{16,8},{24,16},{32,24},{40,32},{48,40},{56,48},{64,5... | collective-permute-start | bytes 405512 | tf_op jit(solution)/shard_map/ppermute | solution.py:539
  17.0 7.5 %collective-permute-start.2 = (f32[128,128]{1,0:T(8,128)S(1)}, f32[128,128]{1,0:T(8,128)S(1)}, u32[]{:S(2)}, u32[]{:S(2)}) collective-permute-start(f32[128,128]{1,0:T(8,128)S(1)} %get-tuple-element.77), channel_id=1, source_target_pairs={{0,56},{8,0},{16,8},{24,16},{32,24},{40,32},{48,40},{56,48},{1,57}... | collective-permute-start | bytes 196616 | tf_op jit(solution)/shard_map/ppermute | solution.py:531
  23.6 1.3 %collective-permute-start.3 = (f32[128,128]{1,0:T(8,128)S(1)}, f32[128,128]{1,0:T(8,128)S(1)}, u32[]{:S(2)}, u32[]{:S(2)}) collective-permute-start(f32[128,128]{1,0:T(8,128)S(1)} %get-tuple-element.78), channel_id=1, source_target_pairs={{0,8},{8,16},{16,24},{24,32},{32,40},{40,48},{48,56},{56,0},{1,9},... | collective-permute-start | bytes 196616 | tf_op jit(solution)/shard_map/ppermute | solution.py:531
  24.9 13.9 %collective-permute-start.8 = (f32[264,128]{1,0:T(8,128)S(1)}, f32[264,128]{1,0:T(8,128)S(1)}, u32[]{:S(2)}, u32[]{:S(2)}) collective-permute-start(f32[264,128]{1,0:T(8,128)S(1)} %get-tuple-element.83), channel_id=1, source_target_pairs={{0,16},{8,24},{16,32},{24,40},{32,48},{40,56},{48,64},{56,72},{64,... | collective-permute-start | bytes 405512 | tf_op jit(solution)/shard_map/ppermute | solution.py:539
  24.9 13.9 %collective-permute-start.9 = (f32[264,128]{1,0:T(8,128)S(1)}, f32[264,128]{1,0:T(8,128)S(1)}, u32[]{:S(2)}, u32[]{:S(2)}) collective-permute-start(f32[264,128]{1,0:T(8,128)S(1)} %get-tuple-element.84), channel_id=1, source_target_pairs={{0,247},{8,255},{16,0},{24,8},{32,16},{40,24},{48,32},{56,40},{64,... | collective-permute-start | bytes 405512 | tf_op jit(solution)/shard_map/ppermute | solution.py:539
  32.4 3.5 %collective-permute-start.6 = (f32[16,128]{1,0:T(8,128)S(1)}, f32[16,128]{1,0:T(8,128)S(1)}, u32[]{:S(2)}, u32[]{:S(2)}) collective-permute-start(f32[16,128]{1,0:T(8,128)S(1)} %get-tuple-element.81), channel_id=1, source_target_pairs={{0,7},{1,0},{2,1},{3,2},{4,3},{5,4},{6,5},{7,6},{8,15},{9,8},{10,9... | collective-permute-start | bytes 24584 | tf_op jit(solution)/shard_map/ppermute | solution.py:531
  35.1 3.7 %collective-permute-start.7 = (f32[16,128]{1,0:T(8,128)S(1)}, f32[16,128]{1,0:T(8,128)S(1)}, u32[]{:S(2)}, u32[]{:S(2)}) collective-permute-start(f32[16,128]{1,0:T(8,128)S(1)} %get-tuple-element.82), channel_id=1, source_target_pairs={{0,1},{1,2},{2,3},{3,4},{4,5},{5,6},{6,7},{7,0},{8,9},{9,10},{10,1... | collective-permute-start | bytes 24584 | tf_op jit(solution)/shard_map/ppermute | solution.py:531
  48.8 9.1 %collective-permute-start.10 = (f32[256,128]{1,0:T(8,128)S(1)}, f32[256,128]{1,0:T(8,128)S(1)}, u32[]{:S(2)}, u32[]{:S(2)}) collective-permute-start(f32[256,128]{1,0:T(8,128)S(1)} %get-tuple-element.90), channel_id=1, source_target_pairs={{0,192},{64,0},{128,64},{192,128},{1,193},{65,1},{129,65},{193,129... | collective-permute-start | bytes 393224 | tf_op jit(solution)/shard_map/ppermute | solution.py:531
  48.9 9.0 %collective-permute-start.11 = (f32[256,128]{1,0:T(8,128)S(1)}, f32[256,128]{1,0:T(8,128)S(1)}, u32[]{:S(2)}, u32[]{:S(2)}) collective-permute-start(f32[256,128]{1,0:T(8,128)S(1)} %get-tuple-element.91), channel_id=1, source_target_pairs={{0,64},{64,128},{128,192},{192,0},{1,65},{65,129},{129,193},{193,1... | collective-permute-start | bytes 393224 | tf_op jit(solution)/shard_map/ppermute | solution.py:531
  50.9 15.0 %collective-permute-start.14 = (f32[128,128]{1,0:T(8,128)S(1)}, f32[128,128]{1,0:T(8,128)S(1)}, u32[]{:S(2)}, u32[]{:S(2)}) collective-permute-start(f32[128,128]{1,0:T(8,128)S(1)} %get-tuple-element.96), channel_id=1, source_target_pairs={{0,16},{8,24},{16,32},{24,40},{32,48},{40,56},{48,64},{56,72},{64,... | collective-permute-start | bytes 196616 | tf_op jit(solution)/shard_map/ppermute | solution.py:539
  51.0 14.9 %collective-permute-start.15 = (f32[128,128]{1,0:T(8,128)S(1)}, f32[128,128]{1,0:T(8,128)S(1)}, u32[]{:S(2)}, u32[]{:S(2)}) collective-permute-start(f32[128,128]{1,0:T(8,128)S(1)} %get-tuple-element.97), channel_id=1, source_target_pairs={{0,247},{8,255},{16,0},{24,8},{32,16},{40,24},{48,32},{56,40},{64,... | collective-permute-start | bytes 196616 | tf_op jit(solution)/shard_map/ppermute | solution.py:539
  59.2 7.6 %collective-permute-start.12 = (f32[128,128]{1,0:T(8,128)S(1)}, f32[128,128]{1,0:T(8,128)S(1)}, u32[]{:S(2)}, u32[]{:S(2)}) collective-permute-start(f32[128,128]{1,0:T(8,128)S(1)} %get-tuple-element.100), channel_id=1, source_target_pairs={{0,56},{8,0},{16,8},{24,16},{32,24},{40,32},{48,40},{56,48},{1,57}... | collective-permute-start | bytes 196616 | tf_op jit(solution)/shard_map/ppermute | solution.py:531
  65.9 1.3 %collective-permute-start.13 = (f32[128,128]{1,0:T(8,128)S(1)}, f32[128,128]{1,0:T(8,128)S(1)}, u32[]{:S(2)}, u32[]{:S(2)}) collective-permute-start(f32[128,128]{1,0:T(8,128)S(1)} %get-tuple-element.101), channel_id=1, source_target_pairs={{0,8},{8,16},{16,24},{24,32},{32,40},{40,48},{48,56},{56,0},{1,9},... | collective-permute-start | bytes 196616 | tf_op jit(solution)/shard_map/ppermute | solution.py:531
  67.8 2.6 %collective-permute-start.16 = (f32[16,128]{1,0:T(8,128)S(1)}, f32[16,128]{1,0:T(8,128)S(1)}, u32[]{:S(2)}, u32[]{:S(2)}) collective-permute-start(f32[16,128]{1,0:T(8,128)S(1)} %get-tuple-element.104), channel_id=1, source_target_pairs={{0,7},{1,0},{2,1},{3,2},{4,3},{5,4},{6,5},{7,6},{8,15},{9,8},{10,9... | collective-permute-start | bytes 24584 | tf_op jit(solution)/shard_map/ppermute | solution.py:531
  67.9 59.9 %copy-start = (f32[8,16,256]{2,1,0:T(8,128)S(1)}, f32[8,16,256]{2,1,0:T(8,128)}, u32[]{:S(2)}) copy-start(f32[8,16,256]{2,1,0:T(8,128)} %param.11) | copy-start | bytes 393220
  67.9 3.8 %collective-permute-start.17 = (f32[16,128]{1,0:T(8,128)S(1)}, f32[16,128]{1,0:T(8,128)S(1)}, u32[]{:S(2)}, u32[]{:S(2)}) collective-permute-start(f32[16,128]{1,0:T(8,128)S(1)} %get-tuple-element.105), channel_id=1, source_target_pairs={{0,1},{1,2},{2,3},{3,4},{4,5},{5,6},{6,7},{7,0},{8,9},{9,10},{10,1... | collective-permute-start | bytes 24584 | tf_op jit(solution)/shard_map/ppermute | solution.py:531
  81.1 3.9 %collective-permute-start.19 = (f32[8,128]{1,0:T(8,128)S(1)}, f32[8,128]{1,0:T(8,128)S(1)}, u32[]{:S(2)}, u32[]{:S(2)}) collective-permute-start(f32[8,128]{1,0:T(8,128)S(1)} %get-tuple-element.117), channel_id=1, source_target_pairs={{0,1},{1,2},{2,3},{3,4},{4,5},{5,6},{6,7},{7,0},{8,9},{9,10},{10,1... | collective-permute-start | bytes 12296 | tf_op jit(solution)/shard_map/ppermute | solution.py:531
  81.5 3.5 %collective-permute-start.18 = (f32[8,128]{1,0:T(8,128)S(1)}, f32[8,128]{1,0:T(8,128)S(1)}, u32[]{:S(2)}, u32[]{:S(2)}) collective-permute-start(f32[8,128]{1,0:T(8,128)S(1)} %get-tuple-element.118), channel_id=1, source_target_pairs={{0,7},{1,0},{2,1},{3,2},{4,3},{5,4},{6,5},{7,6},{8,15},{9,8},{10,9... | collective-permute-start | bytes 12296 | tf_op jit(solution)/shard_map/ppermute | solution.py:531
  113.5 14.3 %all-to-all-start.1 = ((f32[32,24,128]{2,1,0:T(8,128)}), f32[32,24,128]{2,1,0:T(8,128)S(1)}, u32[]{:S(2)}, u32[]{:S(2)}) async-start(f32[32,24,128]{2,1,0:T(8,128)} %get-tuple-element.116), calls=%async_computation.1 | async-start | bytes 786432 | tf_op jit(solution)/shard_map/all_to_all | solution.py:713

commit v5 on v3

--- a/solution.py
+++ b/solution.py
@@ -599,20 +599,17 @@
     )
 
     def chosen(kernel, rows, *inputs):
-        message = shape(rows, LANES)
         small = inputs[1].ndim == 1
-        up, down = pl.pallas_call(
+        return pl.pallas_call(
             kernel,
-            out_shape=(message, message),
+            out_shape=(shape(rows, LANES),) * 2,
             in_specs=[SMEM] * (1 + small) + [VMEM] * (len(inputs) - 1 - small),
             out_specs=[VMEM] * 2,
             compiler_params=params(),
             name=kernel.__name__,
         )(*inputs)
-        step = 2 if kernel is choose_far else 1
-        return ring(up, step), ring(down, -step)
-
-    def halo(field, x_plus, x_minus):
+
+    def halo(field, x_plus, x_minus, source):
         message = shape(HALF, LANES)
         down, up = pl.pallas_call(
             pack_y,
@@ -624,6 +621,11 @@
             name="pack_y",
         )(place, field, x_plus, x_minus)
         y_plus, y_minus = turn(down, "gy", -1), turn(up, "gy", 1)
+        planes = []
+        if source:
+            _, source = lax.optimization_barrier(((down, up), source))
+            slab_up, slab_down = chosen(choose_far, 128, place, *source)
+            planes = [ring(slab_up, 2), ring(slab_down, -2)]
         ghosts = (x_plus, x_minus, y_plus, y_minus)
         specs = []
         for block, half_block in ((0, 0), (CZ // 8 - 1, HALF // 8 - 1)):
@@ -640,14 +642,20 @@
             name="pack_z",
         )(place, field, *ghosts, field, *ghosts)
         z_plus, z_minus = turn(z_low, "gz", -1), turn(z_high, "gz", 1)
-        return ghosts + (z_plus, z_minus)
-
-    near_planes = chosen(choose_near, 64 * RING + 8, place, lookup, slab)
+        if source:
+            (z_plus, z_minus), planes = lax.optimization_barrier(((z_plus, z_minus), planes))
+        return ghosts + (z_plus, z_minus), planes
+
+    up, down = chosen(choose_near, 64 * RING + 8, place, lookup, slab)
+    received = [ring(up, 1), ring(down, -1)]
     for sweep_index in range(SWEEPS):
         final = sweep_index == SWEEPS - 1
         if final:
-            next_planes = chosen(choose_next, 64 * (RING - 1) + 8, place, *near_planes)
-        ghosts = halo(field, *x_ghosts)
+            up, down = chosen(choose_next, 64 * (RING - 1) + 8, place, *received)
+            received += [ring(up, 1), ring(down, -1)]
+            x_ghosts, _, _ = lax.optimization_barrier((x_ghosts, up, down))
+        ghosts, planes = halo(field, *x_ghosts, received if final else [])
+        received += planes
         scratch = [
             pltpu.VMEM((10, CZ + 2 * HALO, LANES), F32),
             pltpu.VMEM(((CZ + 1 + WINDOW) * PLANE + 8, LANES), F32),
@@ -684,13 +692,10 @@
         cost_estimate=cost(1 << 20, 2 * field_bytes),
         name="finish_field",
     )(field)
-    received = [*near_planes, *next_planes]
-    received += chosen(choose_far, 128, place, *received)
     heat_above, heat_below = turn(heat[:8], "gz", -1), turn(heat[CZ - 8 :], "gz", 1)
-    heat_above, heat_below, field_new, *far_planes = lax.optimization_barrier(
-        (heat_above, heat_below, field_new, *received[-2:])
+    heat_above, heat_below, field_new = lax.optimization_barrier(
+        (heat_above, heat_below, field_new)
     )
-    received[-2:] = far_planes
     rows = slab_cap + 8
     outgoing = pl.pallas_call(
         pack_heat,

time: 123 us -> 120 us (0.976)
  waiting for transfers between devices: 12.2 us -> 15.9 us
  starting transfers between devices: 47.1 us -> 44 us
  blocking collectives: 20 us -> 17 us
    ppermute x14, waiting for transfers between devices: 4.22 us -> 8.01 us  [turn(): lax.ppermute(value, axis, [(i, (i + step) % count) for i in range(count)])]
    all_to_all x1, blocking collectives: 20 us -> 17 us  [body(): lax.all_to_all(outgoing, ('gx', 'gy'), split_axis=0, concat_axis=0, tiled...]
    ppermute x6, starting transfers between devices: 17.7 us -> 14.9 us  [ring(): return lax.ppermute(value, ('gx', 'gy', 'gz'), pairs)]
  transfers between devices with their start and end apart: 21 -> 21, of which waited for: 6 -> 7; matrix products, arithmetic and copies ran while one was open for 0% -> 0% of each run, Pallas kernels for 25% -> 18%
where the time goes in v5:
time: 120 us
  starting transfers between devices  44 us (37%)
  Pallas kernels  42.4 us (35%)
  blocking collectives  17 us (14%)
  waiting for transfers between devices  15.9 us (13%)
    ppermute x14, starting transfers between devices, turn(): lax.ppermute(value, axis, [(i, (i + step) % count) for i in range(count)])  25.2 us
    pallas_call x2, Pallas kernels, body(): pl.pallas_call(functools.partial(sweep, final), out_shape=outs, in_specs=...  19.2 us
    all_to_all x1, blocking collectives, body(): lax.all_to_all(outgoing, ('gx', 'gy'), split_axis=0, concat_axis=0, tiled...  17 us
    ppermute x6, starting transfers between devices, ring(): return lax.ppermute(value, ('gx', 'gy', 'gz'), pairs)  14.9 us
    ppermute x14, waiting for transfers between devices, turn(): lax.ppermute(value, axis, [(i, (i + step) % count) for i in range(count)])  8.01 us
    all_to_all x1, waiting for transfers between devices, body(): lax.all_to_all(factor, ('gx', 'gy'), split_axis=0, concat_axis=0, tiled=T...  7.92 us
    pallas_call x1, Pallas kernels, body(): pl.pallas_call(heat_step, out_shape=(shape(owners, slab_cap, LANES), shap...  5.56 us
    pallas_call x1, Pallas kernels, body(): pl.pallas_call(prepare_rest, out_shape=(shape(6, CZ, LANES), shape(1, CZ,...  4.06 us
  transfers between devices with their start and end apart: 21, of which 7 were waited for; matrix products, arithmetic and copies ran while one was open for 0% of the time, Pallas kernels for 18%

profile of v5, /device:TPU:1, one launch (start us, length us, event | category | flops | bytes accessed | tf_op | source)
XLA Modules:
  0.0 120.2 jit_solution(9483119200312791831)
XLA Ops:
  0.7 2.5 %prepare_field.1 = (f32[6,256,128]{2,1,0:T(8,128)S(1)}, f32[256,128]{1,0:T(8,128)S(1)}, f32[256,128]{1,0:T(8,128)S(1)}) custom-call(f32[6,128,256]{2,1,0:T(8,128)} %bitcast.27), custom_call_target="tpu_custom_call" | custom-call | flops 1048576 | bytes 1572864 | tf_op jit(solution)/shard_map/prepare_field/pallas_call | solution.py:556
  3.2 3.6 %collective-permute-start = (f32[256,128]{1,0:T(8,128)S(1)}, f32[256,128]{1,0:T(8,128)S(1)}, u32[]{:S(2)}, u32[]{:S(2)}) collective-permute-start(f32[256,128]{1,0:T(8,128)S(1)} %get-tuple-element.53), channel_id=1, source_target_pairs={{0,192},{64,0},{128,64},{192,128},{1,193},{65,1},{129,65},{193,129... | collective-permute-start | bytes 393224 | tf_op jit(solution)/shard_map/ppermute | solution.py:540
  6.8 4.1 %prepare_rest.1 = (f32[6,256,128]{2,1,0:T(8,128)S(1)}, f32[1,256,128]{2,1,0:T(8,128)S(1)}, f32[512,16]{1,0:T(8,128)S(1)}, f32[24,2,4,8,128]{4,3,2,1,0:T(8,128)S(1)}, bf16[16,512,512]{2,1,0:T(8,128)(2,1)S(1)}) custom-call(f32[6,128,256]{2,1,0:T(8,128)} %bitcast.26, f32[1,128,256]{2,1,0:T(8,128)} %bitcast.16, f32[16,512]{1,0:T(8,128)} %bitcast.33, ...), custom_call_target="tpu_custom_call" | custom-call | flops 1048576 | bytes 12582912 | tf_op jit(solution)/shard_map/prepare_rest/pallas_call | solution.py:568
  11.8 1.3 %pack_y.2 = (f32[128,128]{1,0:T(8,128)S(1)}, f32[128,128]{1,0:T(8,128)S(1)}) custom-call(s32[3]{0:T(128)S(1)} %pad_add_fusion.place, f32[6,256,128]{2,1,0:T(8,128)S(1)} %get-tuple-element.52.field.refs_0_.refs_5_, f32[256,128]{1,0:T(8,128)S(1)} %collective-permute-done.x_plus.refs_1_.refs_6_.xp, f32[256,128]{1,0:T(8,128)S(1)} %collective-permute-done.1.x_minus.refs_2_.refs_7_.xm), custom_call_target="tpu_custom_call" | custom-call | flops 1048576 | bytes 786432 | tf_op jit(solution)/shard_map/pack_y/pallas_call | solution.py:614
  13.2 2.1 %collective-permute-start.2 = (f32[128,128]{1,0:T(8,128)S(1)}, f32[128,128]{1,0:T(8,128)S(1)}, u32[]{:S(2)}, u32[]{:S(2)}) collective-permute-start(f32[128,128]{1,0:T(8,128)S(1)} %get-tuple-element.64), channel_id=1, source_target_pairs={{0,56},{8,0},{16,8},{24,16},{32,24},{40,32},{48,40},{56,48},{1,57}... | collective-permute-start | bytes 196616 | tf_op jit(solution)/shard_map/ppermute | solution.py:540
  18.9 5.6 %collective-permute-start.4 = (f32[16,128]{1,0:T(8,128)S(1)}, f32[16,128]{1,0:T(8,128)S(1)}, u32[]{:S(2)}, u32[]{:S(2)}) collective-permute-start(f32[16,128]{1,0:T(8,128)S(1)} %get-tuple-element.66), channel_id=1, source_target_pairs={{0,7},{1,0},{2,1},{3,2},{4,3},{5,4},{6,5},{7,6},{8,15},{9,8},{10,9... | collective-permute-start | bytes 24584 | tf_op jit(solution)/shard_map/ppermute | solution.py:540
  25.3 3.2 %collective-permute-done.5.zm = f32[16,128]{1,0:T(8,128)S(1)} collective-permute-done((f32[16,128]{1,0:T(8,128)S(1)}, f32[16,128]{1,0:T(8,128)S(1)}, u32[]{:S(2)}, u32[]{:S(2)}) %collective-permute-start.5) | collective-permute-done | bytes 8224 | tf_op jit(solution)/shard_map/ppermute | solution.py:540
  28.5 9.9 %sweep.2 = (f32[6,256,128]{2,1,0:T(8,128)S(1)}, f32[256,128]{1,0:T(8,128)S(1)}, f32[256,128]{1,0:T(8,128)S(1)}) custom-call(s32[3]{0:T(128)S(1)} %pad_add_fusion.place, s32[16]{0:T(128)S(1)} %bitcast.23, f32[6,256,128]{2,1,0:T(8,128)S(1)} %get-tuple-element.52.field.refs_0_.refs_5_, f32[6,256,128]{2,1,0:T(8,128)S(1)} %get-tuple-element.60.drive, ...), custom_call_target="tpu_custom_call" | custom-call | flops 268435456 | bytes 3145728 | tf_op jit(solution)/shard_map/sweep/pallas_call | solution.py:670
  40.6 3.6 %collective-permute-start.14 = (f32[200,128]{1,0:T(8,128)S(1)}, f32[200,128]{1,0:T(8,128)S(1)}, u32[]{:S(2)}, u32[]{:S(2)}) collective-permute-start(f32[200,128]{1,0:T(8,128)S(1)} %get-tuple-element.76), channel_id=1, source_target_pairs={{0,8},{8,16},{16,24},{24,32},{32,40},{40,48},{48,56},{56,64},{64,7... | collective-permute-start | bytes 307208 | tf_op jit(solution)/shard_map/ppermute | solution.py:548
  44.1 2.8 %collective-permute-start.15 = (f32[200,128]{1,0:T(8,128)S(1)}, f32[200,128]{1,0:T(8,128)S(1)}, u32[]{:S(2)}, u32[]{:S(2)}) collective-permute-start(f32[200,128]{1,0:T(8,128)S(1)} %get-tuple-element.77), channel_id=1, source_target_pairs={{0,255},{8,0},{16,8},{24,16},{32,24},{40,32},{48,40},{56,48},{64,5... | collective-permute-start | bytes 307208 | tf_op jit(solution)/shard_map/ppermute | solution.py:548
  46.9 1.3 %pack_y.3 = (f32[128,128]{1,0:T(8,128)S(1)}, f32[128,128]{1,0:T(8,128)S(1)}) custom-call(s32[3]{0:T(128)S(1)} %pad_add_fusion.place, f32[6,256,128]{2,1,0:T(8,128)S(1)} %get-tuple-element.70.field.refs_0_.refs_5_, f32[256,128]{1,0:T(8,128)S(1)} %collective-permute-done.6.x_plus.refs_1_.refs_6_.xp, ...), custom_call_target="tpu_custom_call" | custom-call | flops 1048576 | bytes 786432 | tf_op jit(solution)/shard_map/pack_y/pallas_call | solution.py:614
  48.3 6.9 %collective-permute-start.10 = (f32[128,128]{1,0:T(8,128)S(1)}, f32[128,128]{1,0:T(8,128)S(1)}, u32[]{:S(2)}, u32[]{:S(2)}) collective-permute-start(f32[128,128]{1,0:T(8,128)S(1)} %get-tuple-element.80), channel_id=1, source_target_pairs={{0,56},{8,0},{16,8},{24,16},{32,24},{40,32},{48,40},{56,48},{1,57}... | collective-permute-start | bytes 196616 | tf_op jit(solution)/shard_map/ppermute | solution.py:540
  55.9 7.8 %collective-permute-start.17 = (f32[128,128]{1,0:T(8,128)S(1)}, f32[128,128]{1,0:T(8,128)S(1)}, u32[]{:S(2)}, u32[]{:S(2)}) collective-permute-start(f32[128,128]{1,0:T(8,128)S(1)} %get-tuple-element.89), channel_id=1, source_target_pairs={{0,247},{8,255},{16,0},{24,8},{32,16},{40,24},{48,32},{56,40},{64,... | collective-permute-start | bytes 196616 | tf_op jit(solution)/shard_map/ppermute | solution.py:548
  64.4 1.4 %collective-permute-start.13 = (f32[16,128]{1,0:T(8,128)S(1)}, f32[16,128]{1,0:T(8,128)S(1)}, u32[]{:S(2)}, u32[]{:S(2)}) collective-permute-start(f32[16,128]{1,0:T(8,128)S(1)} %get-tuple-element.83), channel_id=1, source_target_pairs={{0,1},{1,2},{2,3},{3,4},{4,5},{5,6},{6,7},{7,0},{8,9},{9,10},{10,1... | collective-permute-start | bytes 24584 | tf_op jit(solution)/shard_map/ppermute | solution.py:540
  66.8 1.3 %collective-permute-done.13.zm = f32[16,128]{1,0:T(8,128)S(1)} collective-permute-done((f32[16,128]{1,0:T(8,128)S(1)}, f32[16,128]{1,0:T(8,128)S(1)}, u32[]{:S(2)}, u32[]{:S(2)}) %collective-permute-start.13) | collective-permute-done | bytes 8224 | tf_op jit(solution)/shard_map/ppermute | solution.py:540
  68.2 9.4 %sweep.3 = (f32[6,256,128]{2,1,0:T(8,128)S(1)}, f32[256,128]{1,0:T(8,128)S(1)}) custom-call(s32[3]{0:T(128)S(1)} %pad_add_fusion.place, s32[16]{0:T(128)S(1)} %bitcast.24, f32[6,256,128]{2,1,0:T(8,128)S(1)} %get-tuple-element.70.field.refs_0_.refs_5_, f32[6,256,128]{2,1,0:T(8,128)S(1)} %get-tuple-element.60.drive, ...), custom_call_target="tpu_custom_call" | custom-call | flops 268435456 | bytes 3145728 | tf_op jit(solution)/shard_map/sweep/pallas_call | solution.py:670
  77.8 2.5 %collective-permute-start.18 = (f32[8,128]{1,0:T(8,128)S(1)}, f32[8,128]{1,0:T(8,128)S(1)}, u32[]{:S(2)}, u32[]{:S(2)}) collective-permute-start(f32[8,128]{1,0:T(8,128)S(1)} %get-tuple-element.102), channel_id=1, source_target_pairs={{0,7},{1,0},{2,1},{3,2},{4,3},{5,4},{6,5},{7,6},{8,15},{9,8},{10,9... | collective-permute-start | bytes 12296 | tf_op jit(solution)/shard_map/ppermute | solution.py:540
  80.3 1.1 finish_field.1
  82.0 17.0 %all_to_all.10.arrived = f32[32,32,128]{2,1,0:T(8,128)S(1)} all-to-all(f32[32,32,128]{2,1,0:T(8,128)S(1)} %pack_heat.1), channel_id=1, replica_groups=mesh['gx'=4,'gy'=8,'gz'=8] {'gx','gy'}, dimensions={0} | all-to-all | bytes 1048576 | tf_op jit(solution)/shard_map/all_to_all | solution.py:709
  99.1 5.6 %heat_step.1 = (f32[32,24,128]{2,1,0:T(8,128)}, f32[24,4,8,128]{3,2,1,0:T(8,128)S(1)}) custom-call(s32[3]{0:T(128)S(1)} %pad_add_fusion.place, s32[32]{0:T(128)S(1)} %bitcast.20, f32[24,2,4,8,128]{4,3,2,1,0:T(8,128)S(1)} %get-tuple-element.73.slab, f32[264,128]{1,0:T(8,128)S(1)} %collective-permute-done.8.below.below1, ...), custom_call_target="tpu_custom_call" | custom-call | tf_op jit(solution)/shard_map/heat_step/pallas_call | solution.py:711
  104.6 4.0 %all-to-all-start.1 = ((f32[32,24,128]{2,1,0:T(8,128)}), f32[32,24,128]{2,1,0:T(8,128)S(1)}, u32[]{:S(2)}, u32[]{:S(2)}) async-start(f32[32,24,128]{2,1,0:T(8,128)} %get-tuple-element.100), calls=%async_computation.1 | async-start | bytes 786432 | tf_op jit(solution)/shard_map/all_to_all | solution.py:724
  108.6 2.4 %finish_slab.1 = f32[24,32,128]{2,1,0:T(8,128)} custom-call(s32[3]{0:T(128)S(1)} %pad_add_fusion.place, s32[32]{0:T(128)S(1)} %bitcast.21, f32[24,4,8,128]{3,2,1,0:T(8,128)S(1)} %get-tuple-element.99.warm), custom_call_target="tpu_custom_call" | custom-call | tf_op jit(solution)/shard_map/finish_slab/pallas_call | solution.py:725
  111.0 7.9 %all-to-all-done.1.returned = f32[32,24,128]{2,1,0:T(8,128)S(1)} async-done(((f32[32,24,128]{2,1,0:T(8,128)}), f32[32,24,128]{2,1,0:T(8,128)S(1)}, u32[]{:S(2)}, u32[]{:S(2)}) %all-to-all-start.1) | async-done | bytes 393248 | tf_op jit(solution)/shard_map/all_to_all | solution.py:724
  118.9 1.3 %finish_conduct.1 = f32[128,256]{1,0:T(8,128)} custom-call(s32[32]{0:T(128)S(1)} %bitcast.22, f32[32,24,128]{2,1,0:T(8,128)S(1)} %all-to-all-done.1.returned, f32[128,256]{1,0:T(8,128)S(1)} %bitcast.17), custom_call_target="tpu_custom_call" | custom-call | tf_op jit(solution)/shard_map/finish_conduct/pallas_call | solution.py:733
  (43 shorter events, 10.7 us)
Async XLA Ops:
  0.6 15.8 %copy-start.1 = (s32[1,32]{1,0:T(1,128)S(1)}, s32[1,32]{1,0:T(1,128)}, u32[]{:S(2)}) copy-start(s32[1,32]{1,0:T(1,128)} %param.15) | copy-start | bytes 388
  0.6 27.9 %copy-start.2 = (s32[1,1,1,16]{3,2,1,0:T(1,128)S(1)}, s32[1,1,1,16]{3,2,1,0:T(1,128)}, u32[]{:S(2)}) copy-start(s32[1,1,1,16]{3,2,1,0:T(1,128)} %param.14) | copy-start | bytes 196
  3.2 7.8 %collective-permute-start = (f32[256,128]{1,0:T(8,128)S(1)}, f32[256,128]{1,0:T(8,128)S(1)}, u32[]{:S(2)}, u32[]{:S(2)}) collective-permute-start(f32[256,128]{1,0:T(8,128)S(1)} %get-tuple-element.53), channel_id=1, source_target_pairs={{0,192},{64,0},{128,64},{192,128},{1,193},{65,1},{129,65},{193,129... | collective-permute-start | bytes 393224 | tf_op jit(solution)/shard_map/ppermute | solution.py:540
  6.8 5.0 %collective-permute-start.1 = (f32[256,128]{1,0:T(8,128)S(1)}, f32[256,128]{1,0:T(8,128)S(1)}, u32[]{:S(2)}, u32[]{:S(2)}) collective-permute-start(f32[256,128]{1,0:T(8,128)S(1)} %get-tuple-element.54), channel_id=1, source_target_pairs={{0,64},{64,128},{128,192},{192,0},{1,65},{65,129},{129,193},{193,1... | collective-permute-start | bytes 393224 | tf_op jit(solution)/shard_map/ppermute | solution.py:540
  13.2 5.2 %collective-permute-start.2 = (f32[128,128]{1,0:T(8,128)S(1)}, f32[128,128]{1,0:T(8,128)S(1)}, u32[]{:S(2)}, u32[]{:S(2)}) collective-permute-start(f32[128,128]{1,0:T(8,128)S(1)} %get-tuple-element.64), channel_id=1, source_target_pairs={{0,56},{8,0},{16,8},{24,16},{32,24},{40,32},{48,40},{56,48},{1,57}... | collective-permute-start | bytes 196616 | tf_op jit(solution)/shard_map/ppermute | solution.py:540
  15.3 3.0 %collective-permute-start.3 = (f32[128,128]{1,0:T(8,128)S(1)}, f32[128,128]{1,0:T(8,128)S(1)}, u32[]{:S(2)}, u32[]{:S(2)}) collective-permute-start(f32[128,128]{1,0:T(8,128)S(1)} %get-tuple-element.65), channel_id=1, source_target_pairs={{0,8},{8,16},{16,24},{24,32},{32,40},{40,48},{48,56},{56,0},{1,9},... | collective-permute-start | bytes 196616 | tf_op jit(solution)/shard_map/ppermute | solution.py:540
  17.0 23.0 %collective-permute-start.8 = (f32[264,128]{1,0:T(8,128)S(1)}, f32[264,128]{1,0:T(8,128)S(1)}, u32[]{:S(2)}, u32[]{:S(2)}) collective-permute-start(f32[264,128]{1,0:T(8,128)S(1)} %get-tuple-element.74), channel_id=1, source_target_pairs={{0,8},{8,16},{16,24},{24,32},{32,40},{40,48},{48,56},{56,64},{64,7... | collective-permute-start | bytes 405512 | tf_op jit(solution)/shard_map/ppermute | solution.py:548
  17.5 22.5 %collective-permute-start.9 = (f32[264,128]{1,0:T(8,128)S(1)}, f32[264,128]{1,0:T(8,128)S(1)}, u32[]{:S(2)}, u32[]{:S(2)}) collective-permute-start(f32[264,128]{1,0:T(8,128)S(1)} %get-tuple-element.75), channel_id=1, source_target_pairs={{0,255},{8,0},{16,8},{24,16},{32,24},{40,32},{48,40},{56,48},{64,5... | collective-permute-start | bytes 405512 | tf_op jit(solution)/shard_map/ppermute | solution.py:548
  18.9 6.4 %collective-permute-start.4 = (f32[16,128]{1,0:T(8,128)S(1)}, f32[16,128]{1,0:T(8,128)S(1)}, u32[]{:S(2)}, u32[]{:S(2)}) collective-permute-start(f32[16,128]{1,0:T(8,128)S(1)} %get-tuple-element.66), channel_id=1, source_target_pairs={{0,7},{1,0},{2,1},{3,2},{4,3},{5,4},{6,5},{7,6},{8,15},{9,8},{10,9... | collective-permute-start | bytes 24584 | tf_op jit(solution)/shard_map/ppermute | solution.py:540
  24.5 4.0 %collective-permute-start.5 = (f32[16,128]{1,0:T(8,128)S(1)}, f32[16,128]{1,0:T(8,128)S(1)}, u32[]{:S(2)}, u32[]{:S(2)}) collective-permute-start(f32[16,128]{1,0:T(8,128)S(1)} %get-tuple-element.67), channel_id=1, source_target_pairs={{0,1},{1,2},{2,3},{3,4},{4,5},{5,6},{6,7},{7,0},{8,9},{9,10},{10,1... | collective-permute-start | bytes 24584 | tf_op jit(solution)/shard_map/ppermute | solution.py:540
  38.4 8.5 %collective-permute-start.6 = (f32[256,128]{1,0:T(8,128)S(1)}, f32[256,128]{1,0:T(8,128)S(1)}, u32[]{:S(2)}, u32[]{:S(2)}) collective-permute-start(f32[256,128]{1,0:T(8,128)S(1)} %get-tuple-element.71), channel_id=1, source_target_pairs={{0,192},{64,0},{128,64},{192,128},{1,193},{65,1},{129,65},{193,129... | collective-permute-start | bytes 393224 | tf_op jit(solution)/shard_map/ppermute | solution.py:540
  39.2 7.8 %collective-permute-start.7 = (f32[256,128]{1,0:T(8,128)S(1)}, f32[256,128]{1,0:T(8,128)S(1)}, u32[]{:S(2)}, u32[]{:S(2)}) collective-permute-start(f32[256,128]{1,0:T(8,128)S(1)} %get-tuple-element.72), channel_id=1, source_target_pairs={{0,64},{64,128},{128,192},{192,0},{1,65},{65,129},{129,193},{193,1... | collective-permute-start | bytes 393224 | tf_op jit(solution)/shard_map/ppermute | solution.py:540
  40.6 14.6 %collective-permute-start.14 = (f32[200,128]{1,0:T(8,128)S(1)}, f32[200,128]{1,0:T(8,128)S(1)}, u32[]{:S(2)}, u32[]{:S(2)}) collective-permute-start(f32[200,128]{1,0:T(8,128)S(1)} %get-tuple-element.76), channel_id=1, source_target_pairs={{0,8},{8,16},{16,24},{24,32},{32,40},{40,48},{48,56},{56,64},{64,7... | collective-permute-start | bytes 307208 | tf_op jit(solution)/shard_map/ppermute | solution.py:548
  44.1 11.1 %collective-permute-start.15 = (f32[200,128]{1,0:T(8,128)S(1)}, f32[200,128]{1,0:T(8,128)S(1)}, u32[]{:S(2)}, u32[]{:S(2)}) collective-permute-start(f32[200,128]{1,0:T(8,128)S(1)} %get-tuple-element.77), channel_id=1, source_target_pairs={{0,255},{8,0},{16,8},{24,16},{32,24},{40,32},{48,40},{56,48},{64,5... | collective-permute-start | bytes 307208 | tf_op jit(solution)/shard_map/ppermute | solution.py:548
  48.3 15.4 %collective-permute-start.10 = (f32[128,128]{1,0:T(8,128)S(1)}, f32[128,128]{1,0:T(8,128)S(1)}, u32[]{:S(2)}, u32[]{:S(2)}) collective-permute-start(f32[128,128]{1,0:T(8,128)S(1)} %get-tuple-element.80), channel_id=1, source_target_pairs={{0,56},{8,0},{16,8},{24,16},{32,24},{40,32},{48,40},{56,48},{1,57}... | collective-permute-start | bytes 196616 | tf_op jit(solution)/shard_map/ppermute | solution.py:540
  55.2 8.5 %collective-permute-start.11 = (f32[128,128]{1,0:T(8,128)S(1)}, f32[128,128]{1,0:T(8,128)S(1)}, u32[]{:S(2)}, u32[]{:S(2)}) collective-permute-start(f32[128,128]{1,0:T(8,128)S(1)} %get-tuple-element.81), channel_id=1, source_target_pairs={{0,8},{8,16},{16,24},{24,32},{32,40},{40,48},{48,56},{56,0},{1,9},... | collective-permute-start | bytes 196616 | tf_op jit(solution)/shard_map/ppermute | solution.py:540
  55.8 12.4 %collective-permute-start.16 = (f32[128,128]{1,0:T(8,128)S(1)}, f32[128,128]{1,0:T(8,128)S(1)}, u32[]{:S(2)}, u32[]{:S(2)}) collective-permute-start(f32[128,128]{1,0:T(8,128)S(1)} %get-tuple-element.88), channel_id=1, source_target_pairs={{0,16},{8,24},{16,32},{24,40},{32,48},{40,56},{48,64},{56,72},{64,... | collective-permute-start | bytes 196616 | tf_op jit(solution)/shard_map/ppermute | solution.py:548
  55.9 12.3 %collective-permute-start.17 = (f32[128,128]{1,0:T(8,128)S(1)}, f32[128,128]{1,0:T(8,128)S(1)}, u32[]{:S(2)}, u32[]{:S(2)}) collective-permute-start(f32[128,128]{1,0:T(8,128)S(1)} %get-tuple-element.89), channel_id=1, source_target_pairs={{0,247},{8,255},{16,0},{24,8},{32,16},{40,24},{48,32},{56,40},{64,... | collective-permute-start | bytes 196616 | tf_op jit(solution)/shard_map/ppermute | solution.py:548
  64.3 2.5 %collective-permute-start.12 = (f32[16,128]{1,0:T(8,128)S(1)}, f32[16,128]{1,0:T(8,128)S(1)}, u32[]{:S(2)}, u32[]{:S(2)}) collective-permute-start(f32[16,128]{1,0:T(8,128)S(1)} %get-tuple-element.82), channel_id=1, source_target_pairs={{0,7},{1,0},{2,1},{3,2},{4,3},{5,4},{6,5},{7,6},{8,15},{9,8},{10,9... | collective-permute-start | bytes 24584 | tf_op jit(solution)/shard_map/ppermute | solution.py:540
  64.4 54.6 %copy-start = (f32[8,16,256]{2,1,0:T(8,128)S(1)}, f32[8,16,256]{2,1,0:T(8,128)}, u32[]{:S(2)}) copy-start(f32[8,16,256]{2,1,0:T(8,128)} %param.11) | copy-start | bytes 393220
  64.4 3.8 %collective-permute-start.13 = (f32[16,128]{1,0:T(8,128)S(1)}, f32[16,128]{1,0:T(8,128)S(1)}, u32[]{:S(2)}, u32[]{:S(2)}) collective-permute-start(f32[16,128]{1,0:T(8,128)S(1)} %get-tuple-element.83), channel_id=1, source_target_pairs={{0,1},{1,2},{2,3},{3,4},{4,5},{5,6},{6,7},{7,0},{8,9},{9,10},{10,1... | collective-permute-start | bytes 24584 | tf_op jit(solution)/shard_map/ppermute | solution.py:540
  77.5 3.9 %collective-permute-start.19 = (f32[8,128]{1,0:T(8,128)S(1)}, f32[8,128]{1,0:T(8,128)S(1)}, u32[]{:S(2)}, u32[]{:S(2)}) collective-permute-start(f32[8,128]{1,0:T(8,128)S(1)} %get-tuple-element.101), channel_id=1, source_target_pairs={{0,1},{1,2},{2,3},{3,4},{4,5},{5,6},{6,7},{7,0},{8,9},{9,10},{10,1... | collective-permute-start | bytes 12296 | tf_op jit(solution)/shard_map/ppermute | solution.py:540
  77.8 3.7 %collective-permute-start.18 = (f32[8,128]{1,0:T(8,128)S(1)}, f32[8,128]{1,0:T(8,128)S(1)}, u32[]{:S(2)}, u32[]{:S(2)}) collective-permute-start(f32[8,128]{1,0:T(8,128)S(1)} %get-tuple-element.102), channel_id=1, source_target_pairs={{0,7},{1,0},{2,1},{3,2},{4,3},{5,4},{6,5},{7,6},{8,15},{9,8},{10,9... | collective-permute-start | bytes 12296 | tf_op jit(solution)/shard_map/ppermute | solution.py:540
  104.6 14.3 %all-to-all-start.1 = ((f32[32,24,128]{2,1,0:T(8,128)}), f32[32,24,128]{2,1,0:T(8,128)S(1)}, u32[]{:S(2)}, u32[]{:S(2)}) async-start(f32[32,24,128]{2,1,0:T(8,128)} %get-tuple-element.100), calls=%async_computation.1 | async-start | bytes 786432 | tf_op jit(solution)/shard_map/all_to_all | solution.py:724

commit v6 on v5

--- a/solution.py
+++ b/solution.py
@@ -23,7 +23,7 @@
 MAXSEG = 19
 F32 = jnp.float32
 HALO = 8
-CHUNK = 32
+CHUNK = 128
 XP_PLUS, XP_MINUS = 6, 7
 X_BITS, Y_BITS = 112, 15
 RING = SECTIONS
@@ -355,7 +355,7 @@
                     columns[pl.ds(at, CHUNK, stride=PLANE), :] = ahead(rest_of, CORNER[q])
         return carry
 
-    lax.fori_loop(0, CZ // CHUNK, residual, 0)
+    lax.fori_loop(0, CZ // CHUNK, residual, 0, unroll=True)
 
     row_of = lax.broadcasted_iota(jnp.int32, (512, LANES), 0)
     start = jnp.int32(0)
@@ -394,7 +394,7 @@
             last[rows, :] = high
         return carry
 
-    lax.fori_loop(0, CZ // CHUNK, update, 0)
+    lax.fori_loop(0, CZ // CHUNK, update, 0, unroll=True)
 
 
 def finish_field(planes, out):
@@ -476,12 +476,8 @@
     for step in range(1, SECTIONS + 1):
         now, before = (step - 1) % 2, step % 2
 
-        def loop(g, carry):
-            one(step, now, before, step + g * group)
-            return carry
-
-        trips = (planes - 2 * step) // group
-        lax.fori_loop(0, trips, loop, 0, unroll={15: 5, 14: 7, 13: 13, 12: 6}[trips])
+        for base in range(step, planes - step, group):
+            one(step, now, before, base)
     final = SECTIONS % 2
     for plane in range(warm_out.shape[0]):
         result = temp[final, plane + RING]

time: 120 us -> 114 us (0.950)
  Pallas kernels: 42.4 us -> 36 us
    pallas_call x2, Pallas kernels: 19.2 us -> 14.7 us  [body(): pl.pallas_call(functools.partial(sweep, final), out_shape=outs, in_specs=...]
  transfers between devices with their start and end apart: 21 -> 21, of which waited for: 7 -> 7; matrix products, arithmetic and copies ran while one was open for 0% -> 0% of each run, Pallas kernels for 18% -> 17%
where the time goes in v6:
time: 114 us
  starting transfers between devices  44.4 us (39%)
  Pallas kernels  36 us (32%)
  blocking collectives  17 us (15%)
  waiting for transfers between devices  15.9 us (14%)
    ppermute x14, starting transfers between devices, turn(): lax.ppermute(value, axis, [(i, (i + step) % count) for i in range(count)])  25.6 us
    all_to_all x1, blocking collectives, body(): lax.all_to_all(outgoing, ('gx', 'gy'), split_axis=0, concat_axis=0, tiled...  17 us
    ppermute x6, starting transfers between devices, ring(): return lax.ppermute(value, ('gx', 'gy', 'gz'), pairs)  14.8 us
    pallas_call x2, Pallas kernels, body(): pl.pallas_call(functools.partial(sweep, final), out_shape=outs, in_specs=...  14.7 us
    ppermute x14, waiting for transfers between devices, turn(): lax.ppermute(value, axis, [(i, (i + step) % count) for i in range(count)])  8.01 us
    all_to_all x1, waiting for transfers between devices, body(): lax.all_to_all(factor, ('gx', 'gy'), split_axis=0, concat_axis=0, tiled=T...  7.92 us
    pallas_call x1, Pallas kernels, body(): pl.pallas_call(heat_step, out_shape=(shape(owners, slab_cap, LANES), shap...  4.53 us
    pallas_call x1, Pallas kernels, body(): pl.pallas_call(prepare_rest, out_shape=(shape(6, CZ, LANES), shape(1, CZ,...  4.06 us
  transfers between devices with their start and end apart: 21, of which 7 were waited for; matrix products, arithmetic and copies ran while one was open for 0% of the time, Pallas kernels for 17%

profile of v6, /device:TPU:1, one launch (start us, length us, event | category | flops | bytes accessed | tf_op | source)
XLA Modules:
  0.0 114.2 jit_solution(8316757313511737885)
XLA Ops:
  0.7 2.1 %prepare_field.1 = (f32[6,256,128]{2,1,0:T(8,128)S(1)}, f32[256,128]{1,0:T(8,128)S(1)}, f32[256,128]{1,0:T(8,128)S(1)}) custom-call(f32[6,128,256]{2,1,0:T(8,128)} %bitcast.27), custom_call_target="tpu_custom_call" | custom-call | flops 1048576 | bytes 1572864 | tf_op jit(solution)/shard_map/prepare_field/pallas_call | solution.py:552
  2.7 3.6 %collective-permute-start = (f32[256,128]{1,0:T(8,128)S(1)}, f32[256,128]{1,0:T(8,128)S(1)}, u32[]{:S(2)}, u32[]{:S(2)}) collective-permute-start(f32[256,128]{1,0:T(8,128)S(1)} %get-tuple-element.53), channel_id=1, source_target_pairs={{0,192},{64,0},{128,64},{192,128},{1,193},{65,1},{129,65},{193,129... | collective-permute-start | bytes 393224 | tf_op jit(solution)/shard_map/ppermute | solution.py:536
  6.4 4.1 %prepare_rest.1 = (f32[6,256,128]{2,1,0:T(8,128)S(1)}, f32[1,256,128]{2,1,0:T(8,128)S(1)}, f32[512,16]{1,0:T(8,128)S(1)}, f32[24,2,4,8,128]{4,3,2,1,0:T(8,128)S(1)}, bf16[16,512,512]{2,1,0:T(8,128)(2,1)S(1)}) custom-call(f32[6,128,256]{2,1,0:T(8,128)} %bitcast.26, f32[1,128,256]{2,1,0:T(8,128)} %bitcast.16, f32[16,512]{1,0:T(8,128)} %bitcast.33, ...), custom_call_target="tpu_custom_call" | custom-call | flops 1048576 | bytes 12582912 | tf_op jit(solution)/shard_map/prepare_rest/pallas_call | solution.py:564
  12.5 2.1 %collective-permute-start.2 = (f32[128,128]{1,0:T(8,128)S(1)}, f32[128,128]{1,0:T(8,128)S(1)}, u32[]{:S(2)}, u32[]{:S(2)}) collective-permute-start(f32[128,128]{1,0:T(8,128)S(1)} %get-tuple-element.64), channel_id=1, source_target_pairs={{0,56},{8,0},{16,8},{24,16},{32,24},{40,32},{48,40},{56,48},{1,57}... | collective-permute-start | bytes 196616 | tf_op jit(solution)/shard_map/ppermute | solution.py:536
  14.6 1.1 collective-permute-start.3
  18.3 5.6 %collective-permute-start.4 = (f32[16,128]{1,0:T(8,128)S(1)}, f32[16,128]{1,0:T(8,128)S(1)}, u32[]{:S(2)}, u32[]{:S(2)}) collective-permute-start(f32[16,128]{1,0:T(8,128)S(1)} %get-tuple-element.66), channel_id=1, source_target_pairs={{0,7},{1,0},{2,1},{3,2},{4,3},{5,4},{6,5},{7,6},{8,15},{9,8},{10,9... | collective-permute-start | bytes 24584 | tf_op jit(solution)/shard_map/ppermute | solution.py:536
  24.7 3.2 %collective-permute-done.5.zm = f32[16,128]{1,0:T(8,128)S(1)} collective-permute-done((f32[16,128]{1,0:T(8,128)S(1)}, f32[16,128]{1,0:T(8,128)S(1)}, u32[]{:S(2)}, u32[]{:S(2)}) %collective-permute-start.5) | collective-permute-done | bytes 8224 | tf_op jit(solution)/shard_map/ppermute | solution.py:536
  27.9 7.6 %sweep.2 = (f32[6,256,128]{2,1,0:T(8,128)S(1)}, f32[256,128]{1,0:T(8,128)S(1)}, f32[256,128]{1,0:T(8,128)S(1)}) custom-call(s32[3]{0:T(128)S(1)} %pad_add_fusion.place, s32[16]{0:T(128)S(1)} %bitcast.23, f32[6,256,128]{2,1,0:T(8,128)S(1)} %get-tuple-element.52.field.refs_0_.refs_5_, f32[6,256,128]{2,1,0:T(8,128)S(1)} %get-tuple-element.60.drive, ...), custom_call_target="tpu_custom_call" | custom-call | flops 268435456 | bytes 3145728 | tf_op jit(solution)/shard_map/sweep/pallas_call | solution.py:666
  37.6 3.5 %collective-permute-start.14 = (f32[200,128]{1,0:T(8,128)S(1)}, f32[200,128]{1,0:T(8,128)S(1)}, u32[]{:S(2)}, u32[]{:S(2)}) collective-permute-start(f32[200,128]{1,0:T(8,128)S(1)} %get-tuple-element.76), channel_id=1, source_target_pairs={{0,8},{8,16},{16,24},{24,32},{32,40},{40,48},{48,56},{56,64},{64,7... | collective-permute-start | bytes 307208 | tf_op jit(solution)/shard_map/ppermute | solution.py:544
  41.1 2.6 %collective-permute-start.15 = (f32[200,128]{1,0:T(8,128)S(1)}, f32[200,128]{1,0:T(8,128)S(1)}, u32[]{:S(2)}, u32[]{:S(2)}) collective-permute-start(f32[200,128]{1,0:T(8,128)S(1)} %get-tuple-element.77), channel_id=1, source_target_pairs={{0,255},{8,0},{16,8},{24,16},{32,24},{40,32},{48,40},{56,48},{64,5... | collective-permute-start | bytes 307208 | tf_op jit(solution)/shard_map/ppermute | solution.py:544
  43.7 1.1 pack_y.3
  44.9 7.1 %collective-permute-start.10 = (f32[128,128]{1,0:T(8,128)S(1)}, f32[128,128]{1,0:T(8,128)S(1)}, u32[]{:S(2)}, u32[]{:S(2)}) collective-permute-start(f32[128,128]{1,0:T(8,128)S(1)} %get-tuple-element.80), channel_id=1, source_target_pairs={{0,56},{8,0},{16,8},{24,16},{32,24},{40,32},{48,40},{56,48},{1,57}... | collective-permute-start | bytes 196616 | tf_op jit(solution)/shard_map/ppermute | solution.py:536
  52.6 8.0 %collective-permute-start.17 = (f32[128,128]{1,0:T(8,128)S(1)}, f32[128,128]{1,0:T(8,128)S(1)}, u32[]{:S(2)}, u32[]{:S(2)}) collective-permute-start(f32[128,128]{1,0:T(8,128)S(1)} %get-tuple-element.89), channel_id=1, source_target_pairs={{0,247},{8,255},{16,0},{24,8},{32,16},{40,24},{48,32},{56,40},{64,... | collective-permute-start | bytes 196616 | tf_op jit(solution)/shard_map/ppermute | solution.py:544
  61.6 1.4 %collective-permute-start.13 = (f32[16,128]{1,0:T(8,128)S(1)}, f32[16,128]{1,0:T(8,128)S(1)}, u32[]{:S(2)}, u32[]{:S(2)}) collective-permute-start(f32[16,128]{1,0:T(8,128)S(1)} %get-tuple-element.83), channel_id=1, source_target_pairs={{0,1},{1,2},{2,3},{3,4},{4,5},{5,6},{6,7},{7,0},{8,9},{9,10},{10,1... | collective-permute-start | bytes 24584 | tf_op jit(solution)/shard_map/ppermute | solution.py:536
  64.1 1.3 %collective-permute-done.13.zm = f32[16,128]{1,0:T(8,128)S(1)} collective-permute-done((f32[16,128]{1,0:T(8,128)S(1)}, f32[16,128]{1,0:T(8,128)S(1)}, u32[]{:S(2)}, u32[]{:S(2)}) %collective-permute-start.13) | collective-permute-done | bytes 8224 | tf_op jit(solution)/shard_map/ppermute | solution.py:536
  65.4 7.2 %sweep.3 = (f32[6,256,128]{2,1,0:T(8,128)S(1)}, f32[256,128]{1,0:T(8,128)S(1)}) custom-call(s32[3]{0:T(128)S(1)} %pad_add_fusion.place, s32[16]{0:T(128)S(1)} %bitcast.24, f32[6,256,128]{2,1,0:T(8,128)S(1)} %get-tuple-element.70.field.refs_0_.refs_5_, f32[6,256,128]{2,1,0:T(8,128)S(1)} %get-tuple-element.60.drive, ...), custom_call_target="tpu_custom_call" | custom-call | flops 268435456 | bytes 3145728 | tf_op jit(solution)/shard_map/sweep/pallas_call | solution.py:666
  72.8 2.5 %collective-permute-start.18 = (f32[8,128]{1,0:T(8,128)S(1)}, f32[8,128]{1,0:T(8,128)S(1)}, u32[]{:S(2)}, u32[]{:S(2)}) collective-permute-start(f32[8,128]{1,0:T(8,128)S(1)} %get-tuple-element.102), channel_id=1, source_target_pairs={{0,7},{1,0},{2,1},{3,2},{4,3},{5,4},{6,5},{7,6},{8,15},{9,8},{10,9... | collective-permute-start | bytes 12296 | tf_op jit(solution)/shard_map/ppermute | solution.py:536
  75.3 1.1 %finish_field.1 = f32[6,128,256]{2,1,0:T(8,128)} custom-call(f32[6,256,128]{2,1,0:T(8,128)S(1)} %get-tuple-element.93.planes), custom_call_target="tpu_custom_call" | custom-call | flops 1048576 | bytes 1572864 | tf_op jit(solution)/shard_map/finish_field/pallas_call | solution.py:682
  77.1 17.0 %all_to_all.10.arrived = f32[32,32,128]{2,1,0:T(8,128)S(1)} all-to-all(f32[32,32,128]{2,1,0:T(8,128)S(1)} %pack_heat.1), channel_id=1, replica_groups=mesh['gx'=4,'gy'=8,'gz'=8] {'gx','gy'}, dimensions={0} | all-to-all | bytes 1048576 | tf_op jit(solution)/shard_map/all_to_all | solution.py:705
  94.1 4.5 %heat_step.1 = (f32[32,24,128]{2,1,0:T(8,128)}, f32[24,4,8,128]{3,2,1,0:T(8,128)S(1)}) custom-call(s32[3]{0:T(128)S(1)} %pad_add_fusion.place, s32[32]{0:T(128)S(1)} %bitcast.20, f32[24,2,4,8,128]{4,3,2,1,0:T(8,128)S(1)} %get-tuple-element.73.slab, f32[264,128]{1,0:T(8,128)S(1)} %collective-permute-done.8.below.below1, ...), custom_call_target="tpu_custom_call" | custom-call | tf_op jit(solution)/shard_map/heat_step/pallas_call | solution.py:707
  98.6 4.0 %all-to-all-start.1 = ((f32[32,24,128]{2,1,0:T(8,128)}), f32[32,24,128]{2,1,0:T(8,128)S(1)}, u32[]{:S(2)}, u32[]{:S(2)}) async-start(f32[32,24,128]{2,1,0:T(8,128)} %get-tuple-element.100), calls=%async_computation.1 | async-start | bytes 786432 | tf_op jit(solution)/shard_map/all_to_all | solution.py:720
  102.6 2.4 %finish_slab.1 = f32[24,32,128]{2,1,0:T(8,128)} custom-call(s32[3]{0:T(128)S(1)} %pad_add_fusion.place, s32[32]{0:T(128)S(1)} %bitcast.21, f32[24,4,8,128]{3,2,1,0:T(8,128)S(1)} %get-tuple-element.99.warm), custom_call_target="tpu_custom_call" | custom-call | tf_op jit(solution)/shard_map/finish_slab/pallas_call | solution.py:721
  104.9 7.9 %all-to-all-done.1.returned = f32[32,24,128]{2,1,0:T(8,128)S(1)} async-done(((f32[32,24,128]{2,1,0:T(8,128)}), f32[32,24,128]{2,1,0:T(8,128)S(1)}, u32[]{:S(2)}, u32[]{:S(2)}) %all-to-all-start.1) | async-done | bytes 393248 | tf_op jit(solution)/shard_map/all_to_all | solution.py:720
  112.9 1.3 %finish_conduct.1 = f32[128,256]{1,0:T(8,128)} custom-call(s32[32]{0:T(128)S(1)} %bitcast.22, f32[32,24,128]{2,1,0:T(8,128)S(1)} %all-to-all-done.1.returned, f32[128,256]{1,0:T(8,128)S(1)} %bitcast.17), custom_call_target="tpu_custom_call" | custom-call | tf_op jit(solution)/shard_map/finish_conduct/pallas_call | solution.py:729
  (43 shorter events, 10.9 us)
Async XLA Ops:
  0.6 15.1 %copy-start.1 = (s32[1,32]{1,0:T(1,128)S(1)}, s32[1,32]{1,0:T(1,128)}, u32[]{:S(2)}) copy-start(s32[1,32]{1,0:T(1,128)} %param.15) | copy-start | bytes 388
  0.6 27.3 %copy-start.2 = (s32[1,1,1,16]{3,2,1,0:T(1,128)S(1)}, s32[1,1,1,16]{3,2,1,0:T(1,128)}, u32[]{:S(2)}) copy-start(s32[1,1,1,16]{3,2,1,0:T(1,128)} %param.14) | copy-start | bytes 196
  2.7 7.8 %collective-permute-start = (f32[256,128]{1,0:T(8,128)S(1)}, f32[256,128]{1,0:T(8,128)S(1)}, u32[]{:S(2)}, u32[]{:S(2)}) collective-permute-start(f32[256,128]{1,0:T(8,128)S(1)} %get-tuple-element.53), channel_id=1, source_target_pairs={{0,192},{64,0},{128,64},{192,128},{1,193},{65,1},{129,65},{193,129... | collective-permute-start | bytes 393224 | tf_op jit(solution)/shard_map/ppermute | solution.py:536
  6.4 5.0 %collective-permute-start.1 = (f32[256,128]{1,0:T(8,128)S(1)}, f32[256,128]{1,0:T(8,128)S(1)}, u32[]{:S(2)}, u32[]{:S(2)}) collective-permute-start(f32[256,128]{1,0:T(8,128)S(1)} %get-tuple-element.54), channel_id=1, source_target_pairs={{0,64},{64,128},{128,192},{192,0},{1,65},{65,129},{129,193},{193,1... | collective-permute-start | bytes 393224 | tf_op jit(solution)/shard_map/ppermute | solution.py:536
  12.5 5.2 %collective-permute-start.2 = (f32[128,128]{1,0:T(8,128)S(1)}, f32[128,128]{1,0:T(8,128)S(1)}, u32[]{:S(2)}, u32[]{:S(2)}) collective-permute-start(f32[128,128]{1,0:T(8,128)S(1)} %get-tuple-element.64), channel_id=1, source_target_pairs={{0,56},{8,0},{16,8},{24,16},{32,24},{40,32},{48,40},{56,48},{1,57}... | collective-permute-start | bytes 196616 | tf_op jit(solution)/shard_map/ppermute | solution.py:536
  14.6 3.0 %collective-permute-start.3 = (f32[128,128]{1,0:T(8,128)S(1)}, f32[128,128]{1,0:T(8,128)S(1)}, u32[]{:S(2)}, u32[]{:S(2)}) collective-permute-start(f32[128,128]{1,0:T(8,128)S(1)} %get-tuple-element.65), channel_id=1, source_target_pairs={{0,8},{8,16},{16,24},{24,32},{32,40},{40,48},{48,56},{56,0},{1,9},... | collective-permute-start | bytes 196616 | tf_op jit(solution)/shard_map/ppermute | solution.py:536
  16.3 20.7 %collective-permute-start.8 = (f32[264,128]{1,0:T(8,128)S(1)}, f32[264,128]{1,0:T(8,128)S(1)}, u32[]{:S(2)}, u32[]{:S(2)}) collective-permute-start(f32[264,128]{1,0:T(8,128)S(1)} %get-tuple-element.74), channel_id=1, source_target_pairs={{0,8},{8,16},{16,24},{24,32},{32,40},{40,48},{48,56},{56,64},{64,7... | collective-permute-start | bytes 405512 | tf_op jit(solution)/shard_map/ppermute | solution.py:544
  16.9 20.1 %collective-permute-start.9 = (f32[264,128]{1,0:T(8,128)S(1)}, f32[264,128]{1,0:T(8,128)S(1)}, u32[]{:S(2)}, u32[]{:S(2)}) collective-permute-start(f32[264,128]{1,0:T(8,128)S(1)} %get-tuple-element.75), channel_id=1, source_target_pairs={{0,255},{8,0},{16,8},{24,16},{32,24},{40,32},{48,40},{56,48},{64,5... | collective-permute-start | bytes 405512 | tf_op jit(solution)/shard_map/ppermute | solution.py:544
  18.3 6.4 %collective-permute-start.4 = (f32[16,128]{1,0:T(8,128)S(1)}, f32[16,128]{1,0:T(8,128)S(1)}, u32[]{:S(2)}, u32[]{:S(2)}) collective-permute-start(f32[16,128]{1,0:T(8,128)S(1)} %get-tuple-element.66), channel_id=1, source_target_pairs={{0,7},{1,0},{2,1},{3,2},{4,3},{5,4},{6,5},{7,6},{8,15},{9,8},{10,9... | collective-permute-start | bytes 24584 | tf_op jit(solution)/shard_map/ppermute | solution.py:536
  23.9 4.0 %collective-permute-start.5 = (f32[16,128]{1,0:T(8,128)S(1)}, f32[16,128]{1,0:T(8,128)S(1)}, u32[]{:S(2)}, u32[]{:S(2)}) collective-permute-start(f32[16,128]{1,0:T(8,128)S(1)} %get-tuple-element.67), channel_id=1, source_target_pairs={{0,1},{1,2},{2,3},{3,4},{4,5},{5,6},{6,7},{7,0},{8,9},{9,10},{10,1... | collective-permute-start | bytes 24584 | tf_op jit(solution)/shard_map/ppermute | solution.py:536
  35.5 8.3 %collective-permute-start.6 = (f32[256,128]{1,0:T(8,128)S(1)}, f32[256,128]{1,0:T(8,128)S(1)}, u32[]{:S(2)}, u32[]{:S(2)}) collective-permute-start(f32[256,128]{1,0:T(8,128)S(1)} %get-tuple-element.71), channel_id=1, source_target_pairs={{0,192},{64,0},{128,64},{192,128},{1,193},{65,1},{129,65},{193,129... | collective-permute-start | bytes 393224 | tf_op jit(solution)/shard_map/ppermute | solution.py:536
  36.2 7.6 %collective-permute-start.7 = (f32[256,128]{1,0:T(8,128)S(1)}, f32[256,128]{1,0:T(8,128)S(1)}, u32[]{:S(2)}, u32[]{:S(2)}) collective-permute-start(f32[256,128]{1,0:T(8,128)S(1)} %get-tuple-element.72), channel_id=1, source_target_pairs={{0,64},{64,128},{128,192},{192,0},{1,65},{65,129},{129,193},{193,1... | collective-permute-start | bytes 393224 | tf_op jit(solution)/shard_map/ppermute | solution.py:536
  37.6 14.4 %collective-permute-start.14 = (f32[200,128]{1,0:T(8,128)S(1)}, f32[200,128]{1,0:T(8,128)S(1)}, u32[]{:S(2)}, u32[]{:S(2)}) collective-permute-start(f32[200,128]{1,0:T(8,128)S(1)} %get-tuple-element.76), channel_id=1, source_target_pairs={{0,8},{8,16},{16,24},{24,32},{32,40},{40,48},{48,56},{56,64},{64,7... | collective-permute-start | bytes 307208 | tf_op jit(solution)/shard_map/ppermute | solution.py:544
  41.1 10.8 %collective-permute-start.15 = (f32[200,128]{1,0:T(8,128)S(1)}, f32[200,128]{1,0:T(8,128)S(1)}, u32[]{:S(2)}, u32[]{:S(2)}) collective-permute-start(f32[200,128]{1,0:T(8,128)S(1)} %get-tuple-element.77), channel_id=1, source_target_pairs={{0,255},{8,0},{16,8},{24,16},{32,24},{40,32},{48,40},{56,48},{64,5... | collective-permute-start | bytes 307208 | tf_op jit(solution)/shard_map/ppermute | solution.py:544
  44.9 15.8 %collective-permute-start.10 = (f32[128,128]{1,0:T(8,128)S(1)}, f32[128,128]{1,0:T(8,128)S(1)}, u32[]{:S(2)}, u32[]{:S(2)}) collective-permute-start(f32[128,128]{1,0:T(8,128)S(1)} %get-tuple-element.80), channel_id=1, source_target_pairs={{0,56},{8,0},{16,8},{24,16},{32,24},{40,32},{48,40},{56,48},{1,57}... | collective-permute-start | bytes 196616 | tf_op jit(solution)/shard_map/ppermute | solution.py:536
  52.0 8.7 %collective-permute-start.11 = (f32[128,128]{1,0:T(8,128)S(1)}, f32[128,128]{1,0:T(8,128)S(1)}, u32[]{:S(2)}, u32[]{:S(2)}) collective-permute-start(f32[128,128]{1,0:T(8,128)S(1)} %get-tuple-element.81), channel_id=1, source_target_pairs={{0,8},{8,16},{16,24},{24,32},{32,40},{40,48},{48,56},{56,0},{1,9},... | collective-permute-start | bytes 196616 | tf_op jit(solution)/shard_map/ppermute | solution.py:536
  52.6 12.8 %collective-permute-start.16 = (f32[128,128]{1,0:T(8,128)S(1)}, f32[128,128]{1,0:T(8,128)S(1)}, u32[]{:S(2)}, u32[]{:S(2)}) collective-permute-start(f32[128,128]{1,0:T(8,128)S(1)} %get-tuple-element.88), channel_id=1, source_target_pairs={{0,16},{8,24},{16,32},{24,40},{32,48},{40,56},{48,64},{56,72},{64,... | collective-permute-start | bytes 196616 | tf_op jit(solution)/shard_map/ppermute | solution.py:544
  52.6 12.7 %collective-permute-start.17 = (f32[128,128]{1,0:T(8,128)S(1)}, f32[128,128]{1,0:T(8,128)S(1)}, u32[]{:S(2)}, u32[]{:S(2)}) collective-permute-start(f32[128,128]{1,0:T(8,128)S(1)} %get-tuple-element.89), channel_id=1, source_target_pairs={{0,247},{8,255},{16,0},{24,8},{32,16},{40,24},{48,32},{56,40},{64,... | collective-permute-start | bytes 196616 | tf_op jit(solution)/shard_map/ppermute | solution.py:544
  61.3 2.7 %collective-permute-start.12 = (f32[16,128]{1,0:T(8,128)S(1)}, f32[16,128]{1,0:T(8,128)S(1)}, u32[]{:S(2)}, u32[]{:S(2)}) collective-permute-start(f32[16,128]{1,0:T(8,128)S(1)} %get-tuple-element.82), channel_id=1, source_target_pairs={{0,7},{1,0},{2,1},{3,2},{4,3},{5,4},{6,5},{7,6},{8,15},{9,8},{10,9... | collective-permute-start | bytes 24584 | tf_op jit(solution)/shard_map/ppermute | solution.py:536
  61.6 51.3 %copy-start = (f32[8,16,256]{2,1,0:T(8,128)S(1)}, f32[8,16,256]{2,1,0:T(8,128)}, u32[]{:S(2)}) copy-start(f32[8,16,256]{2,1,0:T(8,128)} %param.11) | copy-start | bytes 393220
  61.6 3.8 %collective-permute-start.13 = (f32[16,128]{1,0:T(8,128)S(1)}, f32[16,128]{1,0:T(8,128)S(1)}, u32[]{:S(2)}, u32[]{:S(2)}) collective-permute-start(f32[16,128]{1,0:T(8,128)S(1)} %get-tuple-element.83), channel_id=1, source_target_pairs={{0,1},{1,2},{2,3},{3,4},{4,5},{5,6},{6,7},{7,0},{8,9},{9,10},{10,1... | collective-permute-start | bytes 24584 | tf_op jit(solution)/shard_map/ppermute | solution.py:536
  72.6 3.9 %collective-permute-start.19 = (f32[8,128]{1,0:T(8,128)S(1)}, f32[8,128]{1,0:T(8,128)S(1)}, u32[]{:S(2)}, u32[]{:S(2)}) collective-permute-start(f32[8,128]{1,0:T(8,128)S(1)} %get-tuple-element.101), channel_id=1, source_target_pairs={{0,1},{1,2},{2,3},{3,4},{4,5},{5,6},{6,7},{7,0},{8,9},{9,10},{10,1... | collective-permute-start | bytes 12296 | tf_op jit(solution)/shard_map/ppermute | solution.py:536
  72.8 3.7 %collective-permute-start.18 = (f32[8,128]{1,0:T(8,128)S(1)}, f32[8,128]{1,0:T(8,128)S(1)}, u32[]{:S(2)}, u32[]{:S(2)}) collective-permute-start(f32[8,128]{1,0:T(8,128)S(1)} %get-tuple-element.102), channel_id=1, source_target_pairs={{0,7},{1,0},{2,1},{3,2},{4,3},{5,4},{6,5},{7,6},{8,15},{9,8},{10,9... | collective-permute-start | bytes 12296 | tf_op jit(solution)/shard_map/ppermute | solution.py:536
  98.6 14.3 %all-to-all-start.1 = ((f32[32,24,128]{2,1,0:T(8,128)}), f32[32,24,128]{2,1,0:T(8,128)S(1)}, u32[]{:S(2)}, u32[]{:S(2)}) async-start(f32[32,24,128]{2,1,0:T(8,128)} %get-tuple-element.100), calls=%async_computation.1 | async-start | bytes 786432 | tf_op jit(solution)/shard_map/all_to_all | solution.py:720

commit v7 on v6

--- a/solution.py
+++ b/solution.py
@@ -147,7 +147,7 @@
 
 def prepare_rest(
     drive, conduct, diagonal, warm, rates, solver,
-    drive_planes, conduct_planes, diagonal_turned, slab, solver_here,
+    drive_planes, conduct_planes, diagonal_spread, slab, solver_here,
     drive_in, conduct_in, diagonal_in, slab_in, sems,
 ):
     copies = [pltpu.make_async_copy(warm, slab_in.at[0], sems.at[0])]
@@ -173,7 +173,9 @@
     for comp in range(6):
         to_planes(drive_in, comp, drive_planes)
     to_planes(conduct_in, 0, conduct_planes)
-    diagonal_turned[...] = diagonal_in[...].T
+    turned = solver_scale * diagonal_in[...].T
+    for s in range(diagonal_spread.shape[0]):
+        diagonal_spread[s] = jnp.broadcast_to(turned[:, s : s + 1], diagonal_spread.shape[1:])
     for copy in copies[5:]:
         copy.wait()
 
@@ -364,7 +366,7 @@
         window = columns[pl.ds(pl.multiple_of(start * PLANE, 8), 512), :]
         window = jnp.where(row_of < (length + 2) * PLANE, window, 0.0).astype(jnp.bfloat16)
         product = jnp.dot(solver[s], window, preferred_element_type=F32)
-        scaled = solver_scale * diagonal[:, s : s + 1] * window.astype(F32)
+        scaled = diagonal[s] * window.astype(F32)
         result = coupling_scale * product + scaled
         to = pl.ds(pl.multiple_of(start * PLANE, 8), MAXSEG * PLANE)
         solved[to, :] = result[PLANE : (MAXSEG + 1) * PLANE, :]
@@ -566,7 +568,7 @@
         out_shape=(
             shape(6, CZ, LANES),
             shape(1, CZ, LANES),
-            shape(512, segs),
+            shape(segs, 512, LANES),
             shape(slab_cap, 2, 4, 8, LANES),
             jax.ShapeDtypeStruct(solver.shape, solver.dtype),
         ),

time: 114 us -> 114 us (level)
  no operation moved by 1% of the time
where the time goes in v7:
time: 114 us
  starting transfers between devices  44.3 us (39%)
  Pallas kernels  36.2 us (32%)
  blocking collectives  17.1 us (15%)
  waiting for transfers between devices  15.5 us (14%)
    ppermute x14, starting transfers between devices, turn(): lax.ppermute(value, axis, [(i, (i + step) % count) for i in range(count)])  25.3 us
    all_to_all x1, blocking collectives, body(): lax.all_to_all(outgoing, ('gx', 'gy'), split_axis=0, concat_axis=0, tiled...  17.1 us
    ppermute x6, starting transfers between devices, ring(): return lax.ppermute(value, ('gx', 'gy', 'gz'), pairs)  15 us
    pallas_call x2, Pallas kernels, body(): pl.pallas_call(functools.partial(sweep, final), out_shape=outs, in_specs=...  14.2 us
    all_to_all x1, waiting for transfers between devices, body(): lax.all_to_all(factor, ('gx', 'gy'), split_axis=0, concat_axis=0, tiled=T...  7.92 us
    ppermute x14, waiting for transfers between devices, turn(): lax.ppermute(value, axis, [(i, (i + step) % count) for i in range(count)])  7.55 us
    pallas_call x1, Pallas kernels, body(): pl.pallas_call(prepare_rest, out_shape=(shape(6, CZ, LANES), shape(1, CZ,...  4.74 us
    pallas_call x1, Pallas kernels, body(): pl.pallas_call(heat_step, out_shape=(shape(owners, slab_cap, LANES), shap...  4.53 us
  transfers between devices with their start and end apart: 21, of which 7 were waited for; matrix products, arithmetic and copies ran while one was open for 0% of the time, Pallas kernels for 17%

profile of v7, /device:TPU:1, one launch (start us, length us, event | category | flops | bytes accessed | tf_op | source)
XLA Modules:
  0.0 114.0 jit_solution(2538795645722649191)
XLA Ops:
  0.7 2.1 %prepare_field.1 = (f32[6,256,128]{2,1,0:T(8,128)S(1)}, f32[256,128]{1,0:T(8,128)S(1)}, f32[256,128]{1,0:T(8,128)S(1)}) custom-call(f32[6,128,256]{2,1,0:T(8,128)} %bitcast.27), custom_call_target="tpu_custom_call" | custom-call | flops 1048576 | bytes 1572864 | tf_op jit(solution)/shard_map/prepare_field/pallas_call | solution.py:554
  2.7 3.6 %collective-permute-start = (f32[256,128]{1,0:T(8,128)S(1)}, f32[256,128]{1,0:T(8,128)S(1)}, u32[]{:S(2)}, u32[]{:S(2)}) collective-permute-start(f32[256,128]{1,0:T(8,128)S(1)} %get-tuple-element.53), channel_id=1, source_target_pairs={{0,192},{64,0},{128,64},{192,128},{1,193},{65,1},{129,65},{193,129... | collective-permute-start | bytes 393224 | tf_op jit(solution)/shard_map/ppermute | solution.py:538
  6.4 4.7 %prepare_rest.1 = (f32[6,256,128]{2,1,0:T(8,128)S(1)}, f32[1,256,128]{2,1,0:T(8,128)S(1)}, f32[16,512,128]{2,1,0:T(8,128)S(1)}, f32[24,2,4,8,128]{4,3,2,1,0:T(8,128)S(1)}, bf16[16,512,512]{2,1,0:T(8,128)(2,1)S(1)}) custom-call(f32[6,128,256]{2,1,0:T(8,128)} %bitcast.26, f32[1,128,256]{2,1,0:T(8,128)} %bitcast.16, f32[16,512]{1,0:T(8,128)} %bitcast.33, ...), custom_call_target="tpu_custom_call" | custom-call | flops 1048576 | bytes 12582912 | tf_op jit(solution)/shard_map/prepare_rest/pallas_call | solution.py:566
  12.5 2.1 %collective-permute-start.2 = (f32[128,128]{1,0:T(8,128)S(1)}, f32[128,128]{1,0:T(8,128)S(1)}, u32[]{:S(2)}, u32[]{:S(2)}) collective-permute-start(f32[128,128]{1,0:T(8,128)S(1)} %get-tuple-element.64), channel_id=1, source_target_pairs={{0,56},{8,0},{16,8},{24,16},{32,24},{40,32},{48,40},{56,48},{1,57}... | collective-permute-start | bytes 196616 | tf_op jit(solution)/shard_map/ppermute | solution.py:538
  14.6 1.1 collective-permute-start.3
  18.3 5.6 %collective-permute-start.4 = (f32[16,128]{1,0:T(8,128)S(1)}, f32[16,128]{1,0:T(8,128)S(1)}, u32[]{:S(2)}, u32[]{:S(2)}) collective-permute-start(f32[16,128]{1,0:T(8,128)S(1)} %get-tuple-element.66), channel_id=1, source_target_pairs={{0,7},{1,0},{2,1},{3,2},{4,3},{5,4},{6,5},{7,6},{8,15},{9,8},{10,9... | collective-permute-start | bytes 24584 | tf_op jit(solution)/shard_map/ppermute | solution.py:538
  24.7 3.2 %collective-permute-done.5.zm = f32[16,128]{1,0:T(8,128)S(1)} collective-permute-done((f32[16,128]{1,0:T(8,128)S(1)}, f32[16,128]{1,0:T(8,128)S(1)}, u32[]{:S(2)}, u32[]{:S(2)}) %collective-permute-start.5) | collective-permute-done | bytes 8224 | tf_op jit(solution)/shard_map/ppermute | solution.py:538
  27.9 7.3 %sweep.2 = (f32[6,256,128]{2,1,0:T(8,128)S(1)}, f32[256,128]{1,0:T(8,128)S(1)}, f32[256,128]{1,0:T(8,128)S(1)}) custom-call(s32[3]{0:T(128)S(1)} %pad_add_fusion.place, s32[16]{0:T(128)S(1)} %bitcast.23, f32[6,256,128]{2,1,0:T(8,128)S(1)} %get-tuple-element.52.field.refs_0_.refs_5_, f32[6,256,128]{2,1,0:T(8,128)S(1)} %get-tuple-element.60.drive, ...), custom_call_target="tpu_custom_call" | custom-call | flops 268435456 | bytes 3145728 | tf_op jit(solution)/shard_map/sweep/pallas_call | solution.py:668
  35.2 1.5 %collective-permute-start.6 = (f32[256,128]{1,0:T(8,128)S(1)}, f32[256,128]{1,0:T(8,128)S(1)}, u32[]{:S(2)}, u32[]{:S(2)}) collective-permute-start(f32[256,128]{1,0:T(8,128)S(1)} %get-tuple-element.71), channel_id=1, source_target_pairs={{0,192},{64,0},{128,64},{192,128},{1,193},{65,1},{129,65},{193,129... | collective-permute-start | bytes 393224 | tf_op jit(solution)/shard_map/ppermute | solution.py:538
  37.3 3.6 %collective-permute-start.14 = (f32[200,128]{1,0:T(8,128)S(1)}, f32[200,128]{1,0:T(8,128)S(1)}, u32[]{:S(2)}, u32[]{:S(2)}) collective-permute-start(f32[200,128]{1,0:T(8,128)S(1)} %get-tuple-element.76), channel_id=1, source_target_pairs={{0,8},{8,16},{16,24},{24,32},{32,40},{40,48},{48,56},{56,64},{64,7... | collective-permute-start | bytes 307208 | tf_op jit(solution)/shard_map/ppermute | solution.py:546
  40.9 2.7 %collective-permute-start.15 = (f32[200,128]{1,0:T(8,128)S(1)}, f32[200,128]{1,0:T(8,128)S(1)}, u32[]{:S(2)}, u32[]{:S(2)}) collective-permute-start(f32[200,128]{1,0:T(8,128)S(1)} %get-tuple-element.77), channel_id=1, source_target_pairs={{0,255},{8,0},{16,8},{24,16},{32,24},{40,32},{48,40},{56,48},{64,5... | collective-permute-start | bytes 307208 | tf_op jit(solution)/shard_map/ppermute | solution.py:546
  44.7 7.1 %collective-permute-start.10 = (f32[128,128]{1,0:T(8,128)S(1)}, f32[128,128]{1,0:T(8,128)S(1)}, u32[]{:S(2)}, u32[]{:S(2)}) collective-permute-start(f32[128,128]{1,0:T(8,128)S(1)} %get-tuple-element.80), channel_id=1, source_target_pairs={{0,56},{8,0},{16,8},{24,16},{32,24},{40,32},{48,40},{56,48},{1,57}... | collective-permute-start | bytes 196616 | tf_op jit(solution)/shard_map/ppermute | solution.py:538
  52.5 8.0 %collective-permute-start.17 = (f32[128,128]{1,0:T(8,128)S(1)}, f32[128,128]{1,0:T(8,128)S(1)}, u32[]{:S(2)}, u32[]{:S(2)}) collective-permute-start(f32[128,128]{1,0:T(8,128)S(1)} %get-tuple-element.89), channel_id=1, source_target_pairs={{0,247},{8,255},{16,0},{24,8},{32,16},{40,24},{48,32},{56,40},{64,... | collective-permute-start | bytes 196616 | tf_op jit(solution)/shard_map/ppermute | solution.py:546
  61.2 1.4 %collective-permute-start.13 = (f32[16,128]{1,0:T(8,128)S(1)}, f32[16,128]{1,0:T(8,128)S(1)}, u32[]{:S(2)}, u32[]{:S(2)}) collective-permute-start(f32[16,128]{1,0:T(8,128)S(1)} %get-tuple-element.83), channel_id=1, source_target_pairs={{0,1},{1,2},{2,3},{3,4},{4,5},{5,6},{6,7},{7,0},{8,9},{9,10},{10,1... | collective-permute-start | bytes 24584 | tf_op jit(solution)/shard_map/ppermute | solution.py:538
  63.7 1.5 %collective-permute-done.13.zm = f32[16,128]{1,0:T(8,128)S(1)} collective-permute-done((f32[16,128]{1,0:T(8,128)S(1)}, f32[16,128]{1,0:T(8,128)S(1)}, u32[]{:S(2)}, u32[]{:S(2)}) %collective-permute-start.13) | collective-permute-done | bytes 8224 | tf_op jit(solution)/shard_map/ppermute | solution.py:538
  65.3 7.0 %sweep.3 = (f32[6,256,128]{2,1,0:T(8,128)S(1)}, f32[256,128]{1,0:T(8,128)S(1)}) custom-call(s32[3]{0:T(128)S(1)} %pad_add_fusion.place, s32[16]{0:T(128)S(1)} %bitcast.24, f32[6,256,128]{2,1,0:T(8,128)S(1)} %get-tuple-element.70.field.refs_0_.refs_5_, f32[6,256,128]{2,1,0:T(8,128)S(1)} %get-tuple-element.60.drive, ...), custom_call_target="tpu_custom_call" | custom-call | flops 268435456 | bytes 3145728 | tf_op jit(solution)/shard_map/sweep/pallas_call | solution.py:668
  72.3 2.7 %collective-permute-start.18 = (f32[8,128]{1,0:T(8,128)S(1)}, f32[8,128]{1,0:T(8,128)S(1)}, u32[]{:S(2)}, u32[]{:S(2)}) collective-permute-start(f32[8,128]{1,0:T(8,128)S(1)} %get-tuple-element.102), channel_id=1, source_target_pairs={{0,7},{1,0},{2,1},{3,2},{4,3},{5,4},{6,5},{7,6},{8,15},{9,8},{10,9... | collective-permute-start | bytes 12296 | tf_op jit(solution)/shard_map/ppermute | solution.py:538
  75.0 1.1 %finish_field.1 = f32[6,128,256]{2,1,0:T(8,128)} custom-call(f32[6,256,128]{2,1,0:T(8,128)S(1)} %get-tuple-element.93.planes), custom_call_target="tpu_custom_call" | custom-call | flops 1048576 | bytes 1572864 | tf_op jit(solution)/shard_map/finish_field/pallas_call | solution.py:684
  76.7 17.1 %all_to_all.10.arrived = f32[32,32,128]{2,1,0:T(8,128)S(1)} all-to-all(f32[32,32,128]{2,1,0:T(8,128)S(1)} %pack_heat.1), channel_id=1, replica_groups=mesh['gx'=4,'gy'=8,'gz'=8] {'gx','gy'}, dimensions={0} | all-to-all | bytes 1048576 | tf_op jit(solution)/shard_map/all_to_all | solution.py:707
  93.8 4.5 %heat_step.1 = (f32[32,24,128]{2,1,0:T(8,128)}, f32[24,4,8,128]{3,2,1,0:T(8,128)S(1)}) custom-call(s32[3]{0:T(128)S(1)} %pad_add_fusion.place, s32[32]{0:T(128)S(1)} %bitcast.20, f32[24,2,4,8,128]{4,3,2,1,0:T(8,128)S(1)} %get-tuple-element.73.slab, f32[264,128]{1,0:T(8,128)S(1)} %collective-permute-done.8.below.below1, ...), custom_call_target="tpu_custom_call" | custom-call | tf_op jit(solution)/shard_map/heat_step/pallas_call | solution.py:709
  98.4 4.0 %all-to-all-start.1 = ((f32[32,24,128]{2,1,0:T(8,128)}), f32[32,24,128]{2,1,0:T(8,128)S(1)}, u32[]{:S(2)}, u32[]{:S(2)}) async-start(f32[32,24,128]{2,1,0:T(8,128)} %get-tuple-element.100), calls=%async_computation.1 | async-start | bytes 786432 | tf_op jit(solution)/shard_map/all_to_all | solution.py:722
  102.3 2.4 %finish_slab.1 = f32[24,32,128]{2,1,0:T(8,128)} custom-call(s32[3]{0:T(128)S(1)} %pad_add_fusion.place, s32[32]{0:T(128)S(1)} %bitcast.21, f32[24,4,8,128]{3,2,1,0:T(8,128)S(1)} %get-tuple-element.99.warm), custom_call_target="tpu_custom_call" | custom-call | tf_op jit(solution)/shard_map/finish_slab/pallas_call | solution.py:723
  104.7 7.9 %all-to-all-done.1.returned = f32[32,24,128]{2,1,0:T(8,128)S(1)} async-done(((f32[32,24,128]{2,1,0:T(8,128)}), f32[32,24,128]{2,1,0:T(8,128)S(1)}, u32[]{:S(2)}, u32[]{:S(2)}) %all-to-all-start.1) | async-done | bytes 393248 | tf_op jit(solution)/shard_map/all_to_all | solution.py:722
  112.6 1.3 %finish_conduct.1 = f32[128,256]{1,0:T(8,128)} custom-call(s32[32]{0:T(128)S(1)} %bitcast.22, f32[32,24,128]{2,1,0:T(8,128)S(1)} %all-to-all-done.1.returned, f32[128,256]{1,0:T(8,128)S(1)} %bitcast.17), custom_call_target="tpu_custom_call" | custom-call | tf_op jit(solution)/shard_map/finish_conduct/pallas_call | solution.py:731
  (43 shorter events, 9.6 us)
Async XLA Ops:
  0.6 15.1 %copy-start.1 = (s32[1,32]{1,0:T(1,128)S(1)}, s32[1,32]{1,0:T(1,128)}, u32[]{:S(2)}) copy-start(s32[1,32]{1,0:T(1,128)} %param.15) | copy-start | bytes 388
  0.6 27.3 %copy-start.2 = (s32[1,1,1,16]{3,2,1,0:T(1,128)S(1)}, s32[1,1,1,16]{3,2,1,0:T(1,128)}, u32[]{:S(2)}) copy-start(s32[1,1,1,16]{3,2,1,0:T(1,128)} %param.14) | copy-start | bytes 196
  2.7 8.5 %collective-permute-start = (f32[256,128]{1,0:T(8,128)S(1)}, f32[256,128]{1,0:T(8,128)S(1)}, u32[]{:S(2)}, u32[]{:S(2)}) collective-permute-start(f32[256,128]{1,0:T(8,128)S(1)} %get-tuple-element.53), channel_id=1, source_target_pairs={{0,192},{64,0},{128,64},{192,128},{1,193},{65,1},{129,65},{193,129... | collective-permute-start | bytes 393224 | tf_op jit(solution)/shard_map/ppermute | solution.py:538
  6.4 5.0 %collective-permute-start.1 = (f32[256,128]{1,0:T(8,128)S(1)}, f32[256,128]{1,0:T(8,128)S(1)}, u32[]{:S(2)}, u32[]{:S(2)}) collective-permute-start(f32[256,128]{1,0:T(8,128)S(1)} %get-tuple-element.54), channel_id=1, source_target_pairs={{0,64},{64,128},{128,192},{192,0},{1,65},{65,129},{129,193},{193,1... | collective-permute-start | bytes 393224 | tf_op jit(solution)/shard_map/ppermute | solution.py:538
  12.5 5.2 %collective-permute-start.2 = (f32[128,128]{1,0:T(8,128)S(1)}, f32[128,128]{1,0:T(8,128)S(1)}, u32[]{:S(2)}, u32[]{:S(2)}) collective-permute-start(f32[128,128]{1,0:T(8,128)S(1)} %get-tuple-element.64), channel_id=1, source_target_pairs={{0,56},{8,0},{16,8},{24,16},{32,24},{40,32},{48,40},{56,48},{1,57}... | collective-permute-start | bytes 196616 | tf_op jit(solution)/shard_map/ppermute | solution.py:538
  14.6 3.0 %collective-permute-start.3 = (f32[128,128]{1,0:T(8,128)S(1)}, f32[128,128]{1,0:T(8,128)S(1)}, u32[]{:S(2)}, u32[]{:S(2)}) collective-permute-start(f32[128,128]{1,0:T(8,128)S(1)} %get-tuple-element.65), channel_id=1, source_target_pairs={{0,8},{8,16},{16,24},{24,32},{32,40},{40,48},{48,56},{56,0},{1,9},... | collective-permute-start | bytes 196616 | tf_op jit(solution)/shard_map/ppermute | solution.py:538
  16.3 20.4 %collective-permute-start.8 = (f32[264,128]{1,0:T(8,128)S(1)}, f32[264,128]{1,0:T(8,128)S(1)}, u32[]{:S(2)}, u32[]{:S(2)}) collective-permute-start(f32[264,128]{1,0:T(8,128)S(1)} %get-tuple-element.74), channel_id=1, source_target_pairs={{0,8},{8,16},{16,24},{24,32},{32,40},{40,48},{48,56},{56,64},{64,7... | collective-permute-start | bytes 405512 | tf_op jit(solution)/shard_map/ppermute | solution.py:546
  16.9 19.9 %collective-permute-start.9 = (f32[264,128]{1,0:T(8,128)S(1)}, f32[264,128]{1,0:T(8,128)S(1)}, u32[]{:S(2)}, u32[]{:S(2)}) collective-permute-start(f32[264,128]{1,0:T(8,128)S(1)} %get-tuple-element.75), channel_id=1, source_target_pairs={{0,255},{8,0},{16,8},{24,16},{32,24},{40,32},{48,40},{56,48},{64,5... | collective-permute-start | bytes 405512 | tf_op jit(solution)/shard_map/ppermute | solution.py:546
  18.3 6.4 %collective-permute-start.4 = (f32[16,128]{1,0:T(8,128)S(1)}, f32[16,128]{1,0:T(8,128)S(1)}, u32[]{:S(2)}, u32[]{:S(2)}) collective-permute-start(f32[16,128]{1,0:T(8,128)S(1)} %get-tuple-element.66), channel_id=1, source_target_pairs={{0,7},{1,0},{2,1},{3,2},{4,3},{5,4},{6,5},{7,6},{8,15},{9,8},{10,9... | collective-permute-start | bytes 24584 | tf_op jit(solution)/shard_map/ppermute | solution.py:538
  23.9 4.0 %collective-permute-start.5 = (f32[16,128]{1,0:T(8,128)S(1)}, f32[16,128]{1,0:T(8,128)S(1)}, u32[]{:S(2)}, u32[]{:S(2)}) collective-permute-start(f32[16,128]{1,0:T(8,128)S(1)} %get-tuple-element.67), channel_id=1, source_target_pairs={{0,1},{1,2},{2,3},{3,4},{4,5},{5,6},{6,7},{7,0},{8,9},{9,10},{10,1... | collective-permute-start | bytes 24584 | tf_op jit(solution)/shard_map/ppermute | solution.py:538
  35.2 8.4 %collective-permute-start.6 = (f32[256,128]{1,0:T(8,128)S(1)}, f32[256,128]{1,0:T(8,128)S(1)}, u32[]{:S(2)}, u32[]{:S(2)}) collective-permute-start(f32[256,128]{1,0:T(8,128)S(1)} %get-tuple-element.71), channel_id=1, source_target_pairs={{0,192},{64,0},{128,64},{192,128},{1,193},{65,1},{129,65},{193,129... | collective-permute-start | bytes 393224 | tf_op jit(solution)/shard_map/ppermute | solution.py:538
  36.7 7.0 %collective-permute-start.7 = (f32[256,128]{1,0:T(8,128)S(1)}, f32[256,128]{1,0:T(8,128)S(1)}, u32[]{:S(2)}, u32[]{:S(2)}) collective-permute-start(f32[256,128]{1,0:T(8,128)S(1)} %get-tuple-element.72), channel_id=1, source_target_pairs={{0,64},{64,128},{128,192},{192,0},{1,65},{65,129},{129,193},{193,1... | collective-permute-start | bytes 393224 | tf_op jit(solution)/shard_map/ppermute | solution.py:538
  37.3 14.5 %collective-permute-start.14 = (f32[200,128]{1,0:T(8,128)S(1)}, f32[200,128]{1,0:T(8,128)S(1)}, u32[]{:S(2)}, u32[]{:S(2)}) collective-permute-start(f32[200,128]{1,0:T(8,128)S(1)} %get-tuple-element.76), channel_id=1, source_target_pairs={{0,8},{8,16},{16,24},{24,32},{32,40},{40,48},{48,56},{56,64},{64,7... | collective-permute-start | bytes 307208 | tf_op jit(solution)/shard_map/ppermute | solution.py:546
  40.9 10.9 %collective-permute-start.15 = (f32[200,128]{1,0:T(8,128)S(1)}, f32[200,128]{1,0:T(8,128)S(1)}, u32[]{:S(2)}, u32[]{:S(2)}) collective-permute-start(f32[200,128]{1,0:T(8,128)S(1)} %get-tuple-element.77), channel_id=1, source_target_pairs={{0,255},{8,0},{16,8},{24,16},{32,24},{40,32},{48,40},{56,48},{64,5... | collective-permute-start | bytes 307208 | tf_op jit(solution)/shard_map/ppermute | solution.py:546
  44.7 15.8 %collective-permute-start.10 = (f32[128,128]{1,0:T(8,128)S(1)}, f32[128,128]{1,0:T(8,128)S(1)}, u32[]{:S(2)}, u32[]{:S(2)}) collective-permute-start(f32[128,128]{1,0:T(8,128)S(1)} %get-tuple-element.80), channel_id=1, source_target_pairs={{0,56},{8,0},{16,8},{24,16},{32,24},{40,32},{48,40},{56,48},{1,57}... | collective-permute-start | bytes 196616 | tf_op jit(solution)/shard_map/ppermute | solution.py:538
  51.8 8.7 %collective-permute-start.11 = (f32[128,128]{1,0:T(8,128)S(1)}, f32[128,128]{1,0:T(8,128)S(1)}, u32[]{:S(2)}, u32[]{:S(2)}) collective-permute-start(f32[128,128]{1,0:T(8,128)S(1)} %get-tuple-element.81), channel_id=1, source_target_pairs={{0,8},{8,16},{16,24},{24,32},{32,40},{40,48},{48,56},{56,0},{1,9},... | collective-permute-start | bytes 196616 | tf_op jit(solution)/shard_map/ppermute | solution.py:538
  52.4 12.8 %collective-permute-start.16 = (f32[128,128]{1,0:T(8,128)S(1)}, f32[128,128]{1,0:T(8,128)S(1)}, u32[]{:S(2)}, u32[]{:S(2)}) collective-permute-start(f32[128,128]{1,0:T(8,128)S(1)} %get-tuple-element.88), channel_id=1, source_target_pairs={{0,16},{8,24},{16,32},{24,40},{32,48},{40,56},{48,64},{56,72},{64,... | collective-permute-start | bytes 196616 | tf_op jit(solution)/shard_map/ppermute | solution.py:546
  52.5 12.7 %collective-permute-start.17 = (f32[128,128]{1,0:T(8,128)S(1)}, f32[128,128]{1,0:T(8,128)S(1)}, u32[]{:S(2)}, u32[]{:S(2)}) collective-permute-start(f32[128,128]{1,0:T(8,128)S(1)} %get-tuple-element.89), channel_id=1, source_target_pairs={{0,247},{8,255},{16,0},{24,8},{32,16},{40,24},{48,32},{56,40},{64,... | collective-permute-start | bytes 196616 | tf_op jit(solution)/shard_map/ppermute | solution.py:546
  61.2 2.5 %collective-permute-start.12 = (f32[16,128]{1,0:T(8,128)S(1)}, f32[16,128]{1,0:T(8,128)S(1)}, u32[]{:S(2)}, u32[]{:S(2)}) collective-permute-start(f32[16,128]{1,0:T(8,128)S(1)} %get-tuple-element.82), channel_id=1, source_target_pairs={{0,7},{1,0},{2,1},{3,2},{4,3},{5,4},{6,5},{7,6},{8,15},{9,8},{10,9... | collective-permute-start | bytes 24584 | tf_op jit(solution)/shard_map/ppermute | solution.py:538
  61.2 51.4 %copy-start = (f32[8,16,256]{2,1,0:T(8,128)S(1)}, f32[8,16,256]{2,1,0:T(8,128)}, u32[]{:S(2)}) copy-start(f32[8,16,256]{2,1,0:T(8,128)} %param.11) | copy-start | bytes 393220
  61.2 4.0 %collective-permute-start.13 = (f32[16,128]{1,0:T(8,128)S(1)}, f32[16,128]{1,0:T(8,128)S(1)}, u32[]{:S(2)}, u32[]{:S(2)}) collective-permute-start(f32[16,128]{1,0:T(8,128)S(1)} %get-tuple-element.83), channel_id=1, source_target_pairs={{0,1},{1,2},{2,3},{3,4},{4,5},{5,6},{6,7},{7,0},{8,9},{9,10},{10,1... | collective-permute-start | bytes 24584 | tf_op jit(solution)/shard_map/ppermute | solution.py:538
  72.2 3.9 %collective-permute-start.19 = (f32[8,128]{1,0:T(8,128)S(1)}, f32[8,128]{1,0:T(8,128)S(1)}, u32[]{:S(2)}, u32[]{:S(2)}) collective-permute-start(f32[8,128]{1,0:T(8,128)S(1)} %get-tuple-element.101), channel_id=1, source_target_pairs={{0,1},{1,2},{2,3},{3,4},{4,5},{5,6},{6,7},{7,0},{8,9},{9,10},{10,1... | collective-permute-start | bytes 12296 | tf_op jit(solution)/shard_map/ppermute | solution.py:538
  72.3 3.8 %collective-permute-start.18 = (f32[8,128]{1,0:T(8,128)S(1)}, f32[8,128]{1,0:T(8,128)S(1)}, u32[]{:S(2)}, u32[]{:S(2)}) collective-permute-start(f32[8,128]{1,0:T(8,128)S(1)} %get-tuple-element.102), channel_id=1, source_target_pairs={{0,7},{1,0},{2,1},{3,2},{4,3},{5,4},{6,5},{7,6},{8,15},{9,8},{10,9... | collective-permute-start | bytes 12296 | tf_op jit(solution)/shard_map/ppermute | solution.py:538
  98.4 14.3 %all-to-all-start.1 = ((f32[32,24,128]{2,1,0:T(8,128)}), f32[32,24,128]{2,1,0:T(8,128)S(1)}, u32[]{:S(2)}, u32[]{:S(2)}) async-start(f32[32,24,128]{2,1,0:T(8,128)} %get-tuple-element.100), calls=%async_computation.1 | async-start | bytes 786432 | tf_op jit(solution)/shard_map/all_to_all | solution.py:722
